TPU v7x, 32 devices: a whole 2x2x4 slice. The times are simulated.
32 devices in a mesh: areal: 8 (over z, y), layer: 4 (over x, core).
Axes of the slice: x: 2, y: 2, z: 4, core: 2. Of those that a mesh axis runs over, the one named last changes fastest.
Arguments:
- right_side: float32 [3, 16, 64, 256], P(None, 'layer', 'areal'), may hold values from -6 to 6
- diag_blocks: bfloat16 [3, 3, 16, 64, 256], P(None, None, 'layer', 'areal'), may hold values from -3 to 9
- couplings: bfloat16 [6, 3, 3, 16, 64, 256], P(None, None, None, 'layer', 'areal'), may hold values from -1 to 1
- pivot_inverse: bfloat16 [3, 3, 16, 64, 256], P(None, None, 'layer', 'areal'), may hold values from -0.2 to 0.2
- lower_blocks: bfloat16 [3, 3, 16, 64, 256], P(None, None, 'layer', 'areal'), may hold values from -0.1 to 1
- upper_blocks: bfloat16 [3, 3, 16, 64, 256], P(None, None, 'layer', 'areal'), may hold values from -0.1 to 1
- active_cells: int32 [16, 64, 256], P('layer', 'areal'), may hold values 0 or 1
- link_from: int32 [4, 32768], P('layer', 'areal'), may hold values from 0 to 8191
- link_owner: int32 [4, 32768, 1], P('layer', 'areal'), may hold values from 0 to 7; in each aligned block of 4096 rows (0 to 4095, 4096 to 8191, ..., all dimensions but the last counted through in order) at most 1024 rows name the same one
- link_target: int32 [4, 32768], P('layer', 'areal'), may hold values from 0 to 8191
- link_blocks: bfloat16 [3, 3, 4, 32768], P(None, None, 'layer', 'areal'), may hold values from -1.5 to 1.5
Outputs:
- update: float32 [3, 16, 64, 256], P(None, 'layer', 'areal')
- hessenberg: float32 [5, 4], replicated
Inputs may be any that keep to these rules, and one draw needn't show every extreme that they name: `link_owner`: among the 4096 connections listed on one device, at most 1024 name the same owner, and in every draw that number is reached.
All inputs are finite; a program needn't handle non-finite values. No bound on the sum of `active_cells` on one device may be relied on, other than what follows from the above.
Results may differ from a plain program's by a relative error of at most 0.0003.
Values sent between devices are 32-bit elements; how exact they have to be, the bound alone decides.
No kernel may reach another device: no remote copies, remote signals or barrier semaphores. Data moves between devices by JAX's collectives and lax.ppermute only.
A program may use at most 64 MiB of HBM per device.

v0:
```python
import jax
import jax.numpy as jnp
from jax import lax
from jax.sharding import PartitionSpec as P

ITERS = 4
SWEEP_BLOCKS = 2


tiny_square = 1e-06


def passed_along(array, axis, by):
    size = lax.axis_size(axis)
    pairs = [(i, i + by) for i in range(size) if 0 <= i + by < size]
    return lax.ppermute(array, axis, pairs)


def extended(block, sides, width):
    for axis, dim in sides:
        count = lax.axis_size(axis)
        forward = [(i, i + 1) for i in range(count - 1)]
        backward = [(target, source) for source, target in forward]
        low = lax.ppermute(
            lax.slice_in_dim(block, block.shape[dim] - width, None, axis=dim), axis, forward
        )
        high = lax.ppermute(lax.slice_in_dim(block, 0, width, axis=dim), axis, backward)
        block = jnp.concatenate([low, block, high], axis=dim)
    return block


def apply_block(matrix_blocks, vector):
    return jnp.sum(matrix_blocks.astype(jnp.float32) * vector[None], axis=1)


def sweep(values, blocks, downward, incoming):
    layers = values.shape[1]
    ordering = range(layers) if downward else range(layers - 1, -1, -1)
    previous = incoming
    results = [None] * layers
    for layer_at in ordering:
        previous = values[:, layer_at] - apply_block(blocks[:, :, layer_at], previous)
        results[layer_at] = previous
    return jnp.stack(results, axis=1)


def relay_sweep(values, blocks, downward):
    sections = lax.axis_size("layer")
    layer_index = lax.axis_index("layer")
    position = layer_index if downward else sections - 1 - layer_index
    block_rows = values.shape[2] // SWEEP_BLOCKS
    zero_edge = jnp.zeros((3, block_rows, values.shape[3]), jnp.float32)

    def moment(counter, state_pair):
        gathered, incoming = state_pair
        block_at = counter - position
        inside = jnp.logical_and(block_at >= 0, block_at < SWEEP_BLOCKS)
        first_row = jnp.clip(block_at, 0, SWEEP_BLOCKS - 1) * block_rows
        portion = lax.dynamic_slice_in_dim(values, first_row, block_rows, 2)
        coeffs = lax.dynamic_slice_in_dim(blocks, first_row, block_rows, 3)
        solved = sweep(portion, coeffs, downward, incoming)
        gathered = jnp.where(
            inside, lax.dynamic_update_slice_in_dim(gathered, solved, first_row, 2), gathered
        )
        if downward:
            passed = passed_along(solved[:, -1], "layer", 1)
        else:
            passed = passed_along(solved[:, 0], "layer", -1)
        return (gathered, passed)

    final_pair = lax.fori_loop(
        0, sections + SWEEP_BLOCKS - 1, moment, (jnp.zeros_like(values), zero_edge)
    )
    return final_pair[0]


def least_squares(hessenberg, initial):
    columns = hessenberg.shape[1]
    upper_form = hessenberg
    target_vector = jnp.zeros((columns + 1,), jnp.float32).at[0].set(initial)
    cosines = []
    sine_values = []
    for column in range(columns):
        entries = upper_form[:, column]
        for previous in range(column):
            upper_entry = entries[previous]
            lower_entry = entries[previous + 1]
            entries = entries.at[previous].set(
                cosines[previous] * upper_entry + sine_values[previous] * lower_entry
            )
            entries = entries.at[previous + 1].set(
                -sine_values[previous] * upper_entry + cosines[previous] * lower_entry
            )
        upper_entry = entries[column]
        lower_entry = entries[column + 1]
        radius = jnp.sqrt(upper_entry * upper_entry + lower_entry * lower_entry)
        cosines.append(upper_entry / radius)
        sine_values.append(lower_entry / radius)
        entries = entries.at[column].set(radius).at[column + 1].set(0.0)
        upper_form = upper_form.at[:, column].set(entries)
        leading = target_vector[column]
        target_vector = (
            target_vector.at[column]
            .set(cosines[column] * leading)
            .at[column + 1]
            .set(-sine_values[column] * leading)
        )
    solution = [None] * columns
    for row_at in range(columns - 1, -1, -1):
        partial_sum = target_vector[row_at]
        for later_row in range(row_at + 1, columns):
            partial_sum = partial_sum - upper_form[row_at, later_row] * solution[later_row]
        solution[row_at] = partial_sum / upper_form[row_at, row_at]
    return solution


def local(
    right_side,
    diag_blocks,
    couplings,
    pivot_inverse,
    lower_blocks,
    upper_blocks,
    active_cells,
    link_from,
    link_owner,
    link_target,
    link_blocks,
):
    active = active_cells.astype(jnp.float32)
    areal_count = lax.axis_size("areal")
    capacity = 2 * link_from.shape[1] // areal_count
    total_slots = capacity * areal_count
    owners = link_owner[0, :, 0]
    choose = (owners[:, None] == jnp.arange(areal_count, dtype=jnp.int32)[None, :]).astype(
        jnp.int32
    )
    before = jnp.sum((jnp.cumsum(choose, axis=0) - choose) * choose, axis=1)
    slot_of = owners * capacity + before
    outgoing_targets = jnp.zeros((1, total_slots), jnp.int32).at[0, slot_of].set(link_target[0])
    targets = lax.all_to_all(outgoing_targets, "areal", split_axis=1, concat_axis=1, tiled=True)[0]
    sources = link_from[0]
    link_matrix = link_blocks[:, :, 0]
    initial = jnp.sqrt(lax.psum(jnp.sum(right_side * right_side), ("areal", "layer")) + tiny_square)
    basis_list = [right_side / initial]
    directions = []
    hessenberg = jnp.zeros((ITERS + 1, ITERS), jnp.float32)
    for column in range(ITERS):
        scaled = apply_block(pivot_inverse, basis_list[column])
        forward = relay_sweep(scaled, lower_blocks, True)
        direction = relay_sweep(forward, upper_blocks, False)
        directions.append(direction)
        held_cells = direction * active[None]
        padded = extended(held_cells, (("areal", 2), ("layer", 1)), 1)
        padded = jnp.pad(padded, ((0, 0), (0, 0), (0, 0), (1, 1)))
        beside = [
            padded[:, :-2, 1:-1, 1:-1],
            padded[:, 2:, 1:-1, 1:-1],
            padded[:, 1:-1, :-2, 1:-1],
            padded[:, 1:-1, 2:, 1:-1],
            padded[:, 1:-1, 1:-1, :-2],
            padded[:, 1:-1, 1:-1, 2:],
        ]
        flattened = held_cells.reshape(3, -1)
        sending = apply_block(link_matrix, flattened[:, sources])
        outgoing = jnp.zeros((3, total_slots), jnp.float32).at[:, slot_of].set(sending)
        arriving = lax.all_to_all(outgoing, "areal", split_axis=1, concat_axis=1, tiled=True)
        result = apply_block(diag_blocks, held_cells)
        for operate_direction in range(6):
            result = result + apply_block(couplings[operate_direction], beside[operate_direction])
        result = result.reshape(3, -1).at[:, targets].add(arriving).reshape(direction.shape)
        result = active[None] * result + (1.0 - active[None]) * direction
        local_weights = jnp.stack([jnp.sum(earlier * result) for earlier in basis_list])
        weights, own_square = lax.psum(
            (local_weights, jnp.sum(result * result)), ("areal", "layer")
        )
        for position in range(column + 1):
            result = result - weights[position] * basis_list[position]
        length = jnp.sqrt(jnp.maximum(own_square - jnp.sum(weights * weights), 0.0) + tiny_square)
        hessenberg = (
            hessenberg.at[: column + 1, column].set(weights).at[column + 1, column].set(length)
        )
        basis_list.append(result / length)
    coefficients = least_squares(hessenberg, initial)
    update = coefficients[0] * directions[0]
    for position in range(1, ITERS):
        update = update + coefficients[position] * directions[position]
    return (update, hessenberg)


def solution(mesh):
    placed = (
        P(None, "layer", "areal", None),
        P(None, None, "layer", "areal", None),
        P(None, None, None, "layer", "areal", None),
        P(None, None, "layer", "areal", None),
        P(None, None, "layer", "areal", None),
        P(None, None, "layer", "areal", None),
        P("layer", "areal", None),
        P("layer", "areal"),
        P("layer", "areal", None),
        P("layer", "areal"),
        P(None, None, "layer", "areal"),
    )
    return jax.shard_map(
        local,
        mesh=mesh,
        in_specs=placed,
        out_specs=(P(None, "layer", "areal", None), P()),
        check_vma=False,
    )
```

profile of v0, /device:TPU:0, one launch (start us, length us, event | category | flops | bytes accessed | tf_op | source)
XLA Modules:
  0.0 1024.7 jit_solution(16016066879933783754)
XLA Ops:
  2.3 42.2 %psum.63 = f32[]{:T(128)} all-reduce(f32[]{:T(128)} %multiply_reduce_fusion.14), channel_id=1, replica_groups=mesh['areal'=8,'layer'=4] {'areal','layer'}, use_global_device_ids=true, to_apply=%region_1.2 | all-reduce | flops 1 | bytes 8 | tf_op jit(solution)/shard_map/psum | solution.py:144
  47.9 39.3 %while.161 = (s32[]{:T(128)}, f32[3,4,8,256]{3,2,1,0:T(8,128)S(1)}, f32[3,4,256]{2,1,0:T(4,128)S(1)}, s32[]{:T(128)}, f32[3,4,8,256]{3,2,1,0:T(8,128)S(1)}, /*in...) while((s32[]{:T(128)}, f32[3,4,8,256]{3,2,1,0:T(8,128)S(1)}, ...), condition=%wide.region_8.9_spmd, body=%wide.region_3.8_spmd.sunk | while | flops 172047 | bytes 665472 | solution.py:71
  56.6 4.9 collective-permute-start
  65.7 4.2 collective-permute-start
  74.0 4.2 collective-permute-start
  82.3 4.2 collective-permute-start
  87.3 26.6 %while.162 = (s32[]{:T(128)}, f32[3,4,8,256]{3,2,1,0:T(8,128)S(1)}, f32[3,4,256]{2,1,0:T(4,128)S(1)}, s32[]{:T(128)}, f32[3,4,8,256]{3,2,1,0:T(8,128)S(1)}, /*in...) while((s32[]{:T(128)}, f32[3,4,8,256]{3,2,1,0:T(8,128)S(1)}, ...), condition=%wide.region_14.15_spmd, body=%wide.region_9.14_spmd.sunk | while | flops 172047 | bytes 665472 | solution.py:71
  121.4 16.3 %scatter_custom_fusion.8 = s32[8192]{0:T(1024)} fusion(s32[4096]{0:T(1024)S(1)} %broadcast_select_fusion, s32[4096]{0:T(1024)} %bitcast.782, s32[]{:T(128)} %constant.1186.clone.1), kind=kCustom, calls=%fused_computation.380 | custom fusion | bytes 33280
  137.7 6.3 all-to-all-start
  146.7 16.3 %gather_fusion = f32[4096,3]{1,0:T(8,128)} fusion(f32[3,8192]{0,1:T(8,128)} %bitcast.749, s32[4096]{0:T(1024)S(1)} %broadcast_clamp_fusion), kind=kCustom, calls=%fused_computation | custom fusion | bytes 114688 | tf_op jit(solution)/shard_map/gather | solution.py:165
  176.1 13.1 %scatter_custom_fusion = f32[3,8192]{0,1:T(8,128)} fusion(s32[4096]{0:T(1024)S(1)} %bitcast.771, f32[4096,3]{1,0:T(8,128)} %copy.146, f32[]{:T(128)} %constant.1184.clone.1), kind=kCustom, calls=%fused_computation.195 | custom fusion | bytes 98816 | tf_op jit(solution)/shard_map/scatter | solution.py:166
  197.8 5.7 all-to-all-start.1
  203.6 7.7 all-to-all-done.1
  214.0 53.6 %scatter_fusion = f32[3,8192]{0,1:T(8,128)} fusion(f32[3,8192]{0,1:T(8,128)} %bitcast.737, s32[8192]{0:T(1024)S(1)} %bitcast.757, f32[8192,3]{1,0:T(8,128)} %copy.148), kind=kCustom, calls=%fused_computation.5 | custom fusion | flops 24576 | bytes 327680 | tf_op jit(solution)/shard_map/scatter-add | solution.py:171
  271.1 42.7 %all-reduce.9 = (f32[]{:T(128)}, f32[1]{0:T(128)}) all-reduce(f32[]{:T(128)} %get-tuple-element.1555, f32[1]{0:T(128)} %bitcast.155), channel_id=1, replica_groups=mesh['areal'=8,'layer'=4] {'areal','layer'}, use_global_device_ids=true, to_apply=%region_32.33 | all-reduce | flops 2 | bytes 16 | tf_op jit(solution)/shard_map/psum | solution.py:174
  316.6 24.0 %while.163 = (s32[]{:T(128)}, f32[3,4,8,256]{3,2,1,0:T(8,128)S(1)}, f32[3,4,256]{2,1,0:T(4,128)S(1)}, s32[]{:T(128)}, f32[3,4,8,256]{3,2,1,0:T(8,128)S(1)}, /*in...) while((s32[]{:T(128)}, f32[3,4,8,256]{3,2,1,0:T(8,128)S(1)}, ...), condition=%wide.region_40.41_spmd, body=%wide.region_35.40_spmd.sunk | while | flops 172047 | bytes 665472 | solution.py:71
  319.2 4.9 collective-permute-start.2
  325.1 4.2 collective-permute-start.2
  330.3 4.2 collective-permute-start.2
  335.6 4.2 collective-permute-start.2
  340.6 26.6 %while.164 = (s32[]{:T(128)}, f32[3,4,8,256]{3,2,1,0:T(8,128)S(1)}, f32[3,4,256]{2,1,0:T(4,128)S(1)}, s32[]{:T(128)}, f32[3,4,8,256]{3,2,1,0:T(8,128)S(1)}, /*in...) while((s32[]{:T(128)}, f32[3,4,8,256]{3,2,1,0:T(8,128)S(1)}, ...), condition=%wide.region_46.47_spmd, body=%wide.region_41.46_spmd.sunk | while | flops 172047 | bytes 665472 | solution.py:71
  375.3 16.3 %gather_fusion.1 = f32[4096,3]{1,0:T(8,128)} fusion(f32[3,8192]{0,1:T(8,128)} %bitcast.752, s32[4096]{0:T(1024)S(1)} %broadcast_clamp_fusion), kind=kCustom, calls=%fused_computation.1 | custom fusion | bytes 114688 | tf_op jit(solution)/shard_map/gather | solution.py:165
  401.4 13.1 %scatter_custom_fusion.2 = f32[3,8192]{0,1:T(8,128)} fusion(s32[4096]{0:T(1024)S(1)} %bitcast.772, f32[4096,3]{1,0:T(8,128)} %copy.155, f32[]{:T(128)} %constant.1184.clone.1), kind=kCustom, calls=%fused_computation.193 | custom fusion | bytes 98816 | tf_op jit(solution)/shard_map/scatter | solution.py:166
  417.9 4.6 all-to-all-start.2
  433.4 53.4 %scatter_fusion.1 = f32[3,8192]{0,1:T(8,128)} fusion(f32[3,8192]{0,1:T(8,128)} %bitcast.741, s32[8192]{0:T(1024)S(1)} %bitcast.758, f32[8192,3]{1,0:T(8,128)} %copy.157), kind=kCustom, calls=%fused_computation.7 | custom fusion | flops 24576 | bytes 327680 | tf_op jit(solution)/shard_map/scatter-add | solution.py:171
  491.6 41.9 %all-reduce.8 = (f32[]{:T(128)}, f32[2]{0:T(128)S(1)}) all-reduce(f32[]{:T(128)} %get-tuple-element.1552, f32[2]{0:T(128)S(1)} %pad_maximum_fusion.44), channel_id=1, replica_groups=mesh['areal'=8,'layer'=4] {'areal','layer'}, use_global_device_ids=true, to_apply=%region_61.62 | all-reduce | flops 3 | bytes 24 | tf_op jit(solution)/shard_map/psum | solution.py:174
  537.5 24.0 %while.165 = (s32[]{:T(128)}, f32[3,4,8,256]{3,2,1,0:T(8,128)S(1)}, f32[3,4,256]{2,1,0:T(4,128)S(1)}, s32[]{:T(128)}, f32[3,4,8,256]{3,2,1,0:T(8,128)S(1)}, /*in...) while((s32[]{:T(128)}, f32[3,4,8,256]{3,2,1,0:T(8,128)S(1)}, ...), condition=%wide.region_70.71_spmd, body=%wide.region_65.70_spmd.sunk | while | flops 172047 | bytes 665472 | solution.py:71
  540.1 4.9 collective-permute-start.4
  546.0 4.2 collective-permute-start.4
  551.2 4.2 collective-permute-start.4
  556.5 4.2 collective-permute-start.4
  561.5 26.6 %while.166 = (s32[]{:T(128)}, f32[3,4,8,256]{3,2,1,0:T(8,128)S(1)}, f32[3,4,256]{2,1,0:T(4,128)S(1)}, s32[]{:T(128)}, f32[3,4,8,256]{3,2,1,0:T(8,128)S(1)}, /*in...) while((s32[]{:T(128)}, f32[3,4,8,256]{3,2,1,0:T(8,128)S(1)}, ...), condition=%wide.region_76.77_spmd, body=%wide.region_71.0_spmd.sunk | while | flops 172047 | bytes 665472 | solution.py:71
  590.8 16.3 %gather_fusion.2 = f32[4096,3]{1,0:T(8,128)} fusion(f32[3,8192]{0,1:T(8,128)} %bitcast.751, s32[4096]{0:T(1024)S(1)} %broadcast_clamp_fusion), kind=kCustom, calls=%fused_computation.2 | custom fusion | bytes 114688 | tf_op jit(solution)/shard_map/gather | solution.py:165
  616.8 13.1 %scatter_custom_fusion.4 = f32[3,8192]{0,1:T(8,128)} fusion(s32[4096]{0:T(1024)S(1)} %bitcast.773, f32[4096,3]{1,0:T(8,128)} %copy.164, f32[]{:T(128)} %constant.1184.clone.1), kind=kCustom, calls=%fused_computation.191 | custom fusion | bytes 98816 | tf_op jit(solution)/shard_map/scatter | solution.py:166
  633.3 5.2 all-to-all-start.3
  652.9 53.4 %scatter_fusion.2 = f32[3,8192]{0,1:T(8,128)} fusion(f32[3,8192]{0,1:T(8,128)} %bitcast.743, s32[8192]{0:T(1024)S(1)} %bitcast.759, f32[8192,3]{1,0:T(8,128)} %copy.166), kind=kCustom, calls=%fused_computation.9 | custom fusion | flops 24576 | bytes 327680 | tf_op jit(solution)/shard_map/scatter-add | solution.py:171
  711.8 45.9 %all-reduce.7 = (f32[]{:T(128)}, f32[3]{0:T(128)S(1)}) all-reduce(f32[]{:T(128)} %get-tuple-element.1548, f32[3]{0:T(128)S(1)} %pad_maximum_fusion.45), channel_id=1, replica_groups=mesh['areal'=8,'layer'=4] {'areal','layer'}, use_global_device_ids=true, to_apply=%region_92.93 | all-reduce | flops 4 | bytes 32 | tf_op jit(solution)/shard_map/psum | solution.py:174
  762.4 24.0 %while.167 = (s32[]{:T(128)}, f32[3,4,8,256]{3,2,1,0:T(8,128)S(1)}, f32[3,4,256]{2,1,0:T(4,128)S(1)}, s32[]{:T(128)}, f32[3,4,8,256]{3,2,1,0:T(8,128)S(1)}, /*in...) while((s32[]{:T(128)}, f32[3,4,8,256]{3,2,1,0:T(8,128)S(1)}, ...), condition=%wide.region_101.102_spmd, body=%wide.region_96.101_spmd.sunk | while | flops 172047 | bytes 665472 | solution.py:71
  765.0 4.9 collective-permute-start.6
  770.9 4.2 collective-permute-start.6
  776.2 4.2 collective-permute-start.6
  781.4 4.2 collective-permute-start.6
  786.4 26.6 %while.168 = (s32[]{:T(128)}, f32[3,4,8,256]{3,2,1,0:T(8,128)S(1)}, f32[3,4,256]{2,1,0:T(4,128)S(1)}, s32[]{:T(128)}, f32[3,4,8,256]{3,2,1,0:T(8,128)S(1)}, /*in...) while((s32[]{:T(128)}, f32[3,4,8,256]{3,2,1,0:T(8,128)S(1)}, ...), condition=%wide.region_107.108_spmd, body=%wide.region_102.0_spmd.sunk | while | flops 172047 | bytes 665472 | solution.py:71
  815.7 16.3 %gather_fusion.3 = f32[4096,3]{1,0:T(8,128)} fusion(f32[3,8192]{0,1:T(8,128)} %bitcast.750, s32[4096]{0:T(1024)S(1)} %broadcast_clamp_fusion), kind=kCustom, calls=%fused_computation.3 | custom fusion | bytes 114688 | tf_op jit(solution)/shard_map/gather | solution.py:165
  841.0 13.1 %scatter_custom_fusion.6 = f32[3,8192]{0,1:T(8,128)} fusion(s32[4096]{0:T(1024)S(1)} %bitcast.774, f32[4096,3]{1,0:T(8,128)} %copy.173, f32[]{:T(128)} %constant.1184.clone.1), kind=kCustom, calls=%fused_computation.189 | custom fusion | bytes 98816 | tf_op jit(solution)/shard_map/scatter | solution.py:166
  857.5 6.4 all-to-all-start.4
  878.2 53.4 %scatter_fusion.3 = f32[3,8192]{0,1:T(8,128)} fusion(f32[3,8192]{0,1:T(8,128)} %bitcast.739, s32[8192]{0:T(1024)S(1)} %bitcast.760, f32[8192,3]{1,0:T(8,128)} %copy.175), kind=kCustom, calls=%fused_computation.11 | custom fusion | flops 24576 | bytes 327680 | tf_op jit(solution)/shard_map/scatter-add | solution.py:171
  937.8 45.7 %all-reduce.6 = (f32[4]{0:T(128)S(1)}, f32[]{:T(128)}) all-reduce(f32[4]{0:T(128)S(1)} %pad_maximum_fusion.46, f32[]{:T(128)} %get-tuple-element.1542), channel_id=1, replica_groups=mesh['areal'=8,'layer'=4] {'areal','layer'}, use_global_device_ids=true, to_apply=%region_122.123 | all-reduce | flops 5 | bytes 40 | tf_op jit(solution)/shard_map/psum | solution.py:174
  (707 shorter events, 315.2 us)
Async XLA Ops:
  56.6 5.7 collective-permute-start
  65.7 5.0 collective-permute-start
  74.0 5.0 collective-permute-start
  82.3 5.0 collective-permute-start
  92.7 5.6 collective-permute-start.1
  98.5 5.0 collective-permute-start.1
  103.7 5.0 collective-permute-start.1
  108.9 5.0 collective-permute-start.1
  114.0 54.0 %collective-permute-start.8 = (f32[3,4,1,256]{3,2,1,0:T(1,128)S(1)}, f32[3,4,1,256]{3,2,1,0:T(1,128)S(1)}, u32[]{:S(2)}, u32[]{:S(2)}) collective-permute-start(f32[3,4,1,256]{3,2,1,0:T(1,128)S(1)} %get-tuple-element.1733), channel_id=1, source_target_pairs={{0,4},{4,8},{8,12},{12,16},{16,20},{20,24},{24,28},{1,5},{5,9},{9,... | collective-permute-start | bytes 36872 | tf_op jit(solution)/shard_map/ppermute | solution.py:24
  116.7 51.2 %collective-permute-start.9 = (f32[3,4,1,256]{3,2,1,0:T(1,128)S(1)}, f32[3,4,1,256]{3,2,1,0:T(1,128)S(1)}, u32[]{:S(2)}, u32[]{:S(2)}) collective-permute-start(f32[3,4,1,256]{3,2,1,0:T(1,128)S(1)} %get-tuple-element.1734), channel_id=1, source_target_pairs={{4,0},{8,4},{12,8},{16,12},{20,16},{24,20},{28,24},{5,1},{9,5},{13... | collective-permute-start | bytes 36872 | tf_op jit(solution)/shard_map/ppermute | solution.py:27
  137.7 60.2 %all-to-all-start = ((s32[1,8,1024]{2,0,1:T(1,128)}), s32[1,8,1024]{2,0,1:T(1,128)S(1)}, u32[]{:S(2)}, u32[]{:S(2)}) async-start(s32[1,8,1024]{2,0,1:T(1,128)} %bitcast.141), calls=%async_computation | async-start | bytes 65536 | tf_op jit(solution)/shard_map/all_to_all | solution.py:141
  168.0 26.6 %collective-permute-start.10 = (f32[3,1,10,256]{3,2,1,0:T(8,128)S(1)}, f32[3,1,10,256]{3,2,1,0:T(8,128)S(1)}, u32[]{:S(2)}, u32[]{:S(2)}) collective-permute-start(f32[3,1,10,256]{3,2,1,0:T(8,128)S(1)} %get-tuple-element.1718), channel_id=1, source_target_pairs={{0,1},{1,2},{2,3},{4,5},{5,6},{6,7},{8,9},{9,10},{10,11},{12,13},{... | collective-permute-start | bytes 92168 | tf_op jit(solution)/shard_map/ppermute | solution.py:24
  171.5 23.1 %collective-permute-start.11 = (f32[3,1,10,256]{3,2,1,0:T(8,128)S(1)}, f32[3,1,10,256]{3,2,1,0:T(8,128)S(1)}, u32[]{:S(2)}, u32[]{:S(2)}) collective-permute-start(f32[3,1,10,256]{3,2,1,0:T(8,128)S(1)} %get-tuple-element.1717), channel_id=1, source_target_pairs={{1,0},{2,1},{3,2},{5,4},{6,5},{7,6},{9,8},{10,9},{11,10},{13,12},{... | collective-permute-start | bytes 92168 | tf_op jit(solution)/shard_map/ppermute | solution.py:27
  197.8 13.5 %all-to-all-start.1 = ((f32[3,8,1024]{2,0,1:T(4,128)}), f32[3,8,1024]{2,0,1:T(4,128)S(1)}, u32[]{:S(2)}, u32[]{:S(2)}) async-start(f32[3,8,1024]{2,0,1:T(4,128)} %copy.147), calls=%async_computation.1 | async-start | bytes 262144 | tf_op jit(solution)/shard_map/all_to_all | solution.py:167
  319.2 5.7 collective-permute-start.2
  325.1 5.0 collective-permute-start.2
  330.3 5.0 collective-permute-start.2
  335.6 5.0 collective-permute-start.2
  345.9 5.6 collective-permute-start.3
  351.7 5.0 collective-permute-start.3
  367.2 26.6 %collective-permute-start.12 = (f32[3,4,1,256]{3,2,1,0:T(1,128)S(1)}, f32[3,4,1,256]{3,2,1,0:T(1,128)S(1)}, u32[]{:S(2)}, u32[]{:S(2)}) collective-permute-start(f32[3,4,1,256]{3,2,1,0:T(1,128)S(1)} %get-tuple-element.1731), channel_id=1, source_target_pairs={{0,4},{4,8},{8,12},{12,16},{16,20},{20,24},{24,28},{1,5},{5,9},{9,... | collective-permute-start | bytes 36872 | tf_op jit(solution)/shard_map/ppermute | solution.py:24
  371.4 22.4 %collective-permute-start.13 = (f32[3,4,1,256]{3,2,1,0:T(1,128)S(1)}, f32[3,4,1,256]{3,2,1,0:T(1,128)S(1)}, u32[]{:S(2)}, u32[]{:S(2)}) collective-permute-start(f32[3,4,1,256]{3,2,1,0:T(1,128)S(1)} %get-tuple-element.1732), channel_id=1, source_target_pairs={{4,0},{8,4},{12,8},{16,12},{20,16},{24,20},{28,24},{5,1},{9,5},{13... | collective-permute-start | bytes 36872 | tf_op jit(solution)/shard_map/ppermute | solution.py:27
  393.9 29.4 %collective-permute-start.14 = (f32[3,1,10,256]{3,2,1,0:T(8,128)S(1)}, f32[3,1,10,256]{3,2,1,0:T(8,128)S(1)}, u32[]{:S(2)}, u32[]{:S(2)}) collective-permute-start(f32[3,1,10,256]{3,2,1,0:T(8,128)S(1)} %get-tuple-element.1714), channel_id=1, source_target_pairs={{0,1},{1,2},{2,3},{4,5},{5,6},{6,7},{8,9},{9,10},{10,11},{12,13},{... | collective-permute-start | bytes 92168 | tf_op jit(solution)/shard_map/ppermute | solution.py:24
  397.9 25.4 %collective-permute-start.15 = (f32[3,1,10,256]{3,2,1,0:T(8,128)S(1)}, f32[3,1,10,256]{3,2,1,0:T(8,128)S(1)}, u32[]{:S(2)}, u32[]{:S(2)}) collective-permute-start(f32[3,1,10,256]{3,2,1,0:T(8,128)S(1)} %get-tuple-element.1713), channel_id=1, source_target_pairs={{1,0},{2,1},{3,2},{5,4},{6,5},{7,6},{9,8},{10,9},{11,10},{13,12},{... | collective-permute-start | bytes 92168 | tf_op jit(solution)/shard_map/ppermute | solution.py:27
  417.9 12.8 %all-to-all-start.2 = ((f32[3,8,1024]{2,0,1:T(4,128)}), f32[3,8,1024]{2,0,1:T(4,128)S(1)}, u32[]{:S(2)}, u32[]{:S(2)}) async-start(f32[3,8,1024]{2,0,1:T(4,128)} %copy.156), calls=%async_computation.2 | async-start | bytes 262144 | tf_op jit(solution)/shard_map/all_to_all | solution.py:167
  540.1 5.7 collective-permute-start.4
  546.0 5.0 collective-permute-start.4
  551.2 5.0 collective-permute-start.4
  556.5 5.0 collective-permute-start.4
  566.8 5.6 collective-permute-start.5
  572.6 5.0 collective-permute-start.5
  583.1 5.0 collective-permute-start.5
  609.3 29.3 %collective-permute-start.16 = (f32[3,4,1,256]{3,2,1,0:T(1,128)S(1)}, f32[3,4,1,256]{3,2,1,0:T(1,128)S(1)}, u32[]{:S(2)}, u32[]{:S(2)}) collective-permute-start(f32[3,4,1,256]{3,2,1,0:T(1,128)S(1)} %get-tuple-element.1729), channel_id=1, source_target_pairs={{0,4},{4,8},{8,12},{12,16},{16,20},{20,24},{24,28},{1,5},{5,9},{9,... | collective-permute-start | bytes 36872 | tf_op jit(solution)/shard_map/ppermute | solution.py:24
  613.3 25.2 %collective-permute-start.17 = (f32[3,4,1,256]{3,2,1,0:T(1,128)S(1)}, f32[3,4,1,256]{3,2,1,0:T(1,128)S(1)}, u32[]{:S(2)}, u32[]{:S(2)}) collective-permute-start(f32[3,4,1,256]{3,2,1,0:T(1,128)S(1)} %get-tuple-element.1730), channel_id=1, source_target_pairs={{4,0},{8,4},{12,8},{16,12},{20,16},{24,20},{28,24},{5,1},{9,5},{13... | collective-permute-start | bytes 36872 | tf_op jit(solution)/shard_map/ppermute | solution.py:27
  633.3 16.9 %all-to-all-start.3 = ((f32[3,8,1024]{2,0,1:T(4,128)}), f32[3,8,1024]{2,0,1:T(4,128)S(1)}, u32[]{:S(2)}, u32[]{:S(2)}) async-start(f32[3,8,1024]{2,0,1:T(4,128)} %copy.165), calls=%async_computation.3 | async-start | bytes 262144 | tf_op jit(solution)/shard_map/all_to_all | solution.py:167
  638.6 8.3 collective-permute-start.18
  765.0 5.7 collective-permute-start.6
  770.9 5.0 collective-permute-start.6
  776.2 5.0 collective-permute-start.6
  781.4 5.0 collective-permute-start.6
  791.7 5.6 collective-permute-start.7
  797.5 5.0 collective-permute-start.7
  802.8 5.0 collective-permute-start.7
  808.0 5.0 collective-permute-start.7
  834.2 29.7 %collective-permute-start.20 = (f32[3,4,1,256]{3,2,1,0:T(1,128)S(1)}, f32[3,4,1,256]{3,2,1,0:T(1,128)S(1)}, u32[]{:S(2)}, u32[]{:S(2)}) collective-permute-start(f32[3,4,1,256]{3,2,1,0:T(1,128)S(1)} %get-tuple-element.1727), channel_id=1, source_target_pairs={{0,4},{4,8},{8,12},{12,16},{16,20},{20,24},{24,28},{1,5},{5,9},{9,... | collective-permute-start | bytes 36872 | tf_op jit(solution)/shard_map/ppermute | solution.py:24
  837.5 26.3 %collective-permute-start.21 = (f32[3,4,1,256]{3,2,1,0:T(1,128)S(1)}, f32[3,4,1,256]{3,2,1,0:T(1,128)S(1)}, u32[]{:S(2)}, u32[]{:S(2)}) collective-permute-start(f32[3,4,1,256]{3,2,1,0:T(1,128)S(1)} %get-tuple-element.1728), channel_id=1, source_target_pairs={{4,0},{8,4},{12,8},{16,12},{20,16},{24,20},{28,24},{5,1},{9,5},{13... | collective-permute-start | bytes 36872 | tf_op jit(solution)/shard_map/ppermute | solution.py:27
  857.5 18.1 %all-to-all-start.4 = ((f32[3,8,1024]{2,0,1:T(4,128)}), f32[3,8,1024]{2,0,1:T(4,128)S(1)}, u32[]{:S(2)}, u32[]{:S(2)}) async-start(f32[3,8,1024]{2,0,1:T(4,128)} %copy.174), calls=%async_computation.4 | async-start | bytes 262144 | tf_op jit(solution)/shard_map/all_to_all | solution.py:167
  863.9 8.3 collective-permute-start.22
  (28 other events, 1037.5 us)
where the time goes:
time: 1040 us; the launch traced here: 1020 us
  other arithmetic  276 us (27%)
  local copies, waits for them, and re-layouts  223 us (21%)
  blocking collectives  218 us (21%)
  starting transfers between devices  168 us (16%)
  waiting for transfers between devices  101 us (10%)
  between operations  34.7 us (3%)
    scatter-add x4, other arithmetic, local(): result.reshape(3, -1).at[:, targets].add(arriving).reshape(direction.shape)  214 us
    psum x4, blocking collectives, local(): lax.psum((local_weights, jnp.sum(result * result)), ('areal', 'layer'))  176 us
    ppermute x40, starting transfers between devices, passed_along(): return lax.ppermute(array, axis, pairs)  101 us
    ppermute x40, waiting for transfers between devices, passed_along(): return lax.ppermute(array, axis, pairs)  88.8 us
    gather x8, local copies, waits for them, and re-layouts, local(): sending = apply_block(link_matrix, flattened[:, sources])  73.9 us
    scatter x4, local copies, waits for them, and re-layouts, local(): jnp.zeros((3, total_slots), jnp.float32).at[:, slot_of].set(sending)  52.2 us
    psum x1, blocking collectives, local(): lax.psum(jnp.sum(right_side * right_side), ('areal', 'layer')) + tiny_square  42.2 us
    ppermute x8, starting transfers between devices, extended(): lax.ppermute(lax.slice_in_dim(block, block.shape[dim] - width, None, axis...  28.9 us
  transfers between devices with their start and end apart: 61, of which 42 were waited for; matrix products, arithmetic and copies ran while one was open for 16% of the time, Pallas kernels for 0%

commit v1 on v0

v1 whole, which is shorter than its diff:
```python
import functools

import jax
import jax.numpy as jnp
from jax import lax
from jax.experimental import pallas as pl
from jax.experimental.pallas import tpu as pltpu
from jax.sharding import PartitionSpec as P

ITERS = 4
PARTS = 3
TINY = 1e-06

F32 = jnp.float32
BF16 = jnp.bfloat16
VMEM = pl.BlockSpec(memory_space=pltpu.VMEM)


def call(kernel, outs, scratch=(), name=None, flops=1 << 22, moved=1 << 20):
    many = isinstance(outs, (list, tuple))
    return pl.pallas_call(
        kernel,
        out_shape=outs,
        out_specs=[VMEM] * len(outs) if many else VMEM,
        scratch_shapes=list(scratch),
        compiler_params=pltpu.CompilerParams(vmem_limit_bytes=40 << 20),
        cost_estimate=pl.CostEstimate(flops=flops, bytes_accessed=moved, transcendentals=0),
        name=name,
    )


def wide(value):
    return value.astype(F32)


def times(blocks, vector):
    result = []
    for row in blocks:
        total = row[0] * vector[0]
        for entry, element in zip(row[1:], vector[1:]):
            total = total + entry * element
        result.append(total)
    return result


def block_at(ref, layer):
    return [[wide(ref[c, d, layer]) for d in range(3)] for c in range(3)]


def minus(left, right):
    return [a - b for a, b in zip(left, right)]


def plus(left, right):
    return [a + b for a, b in zip(left, right)]


def local_sweeps(planes, pivot, lower, upper, layers):
    forward = []
    previous = None
    for k in range(layers):
        current = times(block_at(pivot, k), planes[k])
        if previous is not None:
            current = minus(current, times(block_at(lower, k), previous))
        forward.append(current)
        previous = current
    backward = [None] * layers
    previous = None
    for k in range(layers - 1, -1, -1):
        current = forward[k]
        if previous is not None:
            current = minus(current, times(block_at(upper, k), previous))
        backward[k] = current
        previous = current
    return forward[layers - 1], backward


def section_kernel(
    right_ref, pivot_ref, lower_ref, upper_ref, active_ref,
    edge_ref, alone_ref, from_above_ref, from_below_ref, matrix_ref,
):
    layers, rows = right_ref.shape[1], right_ref.shape[2]
    planes = [[right_ref[c, k] for c in range(3)] for k in range(layers)]
    lowest, solved = local_sweeps(planes, pivot_ref, lower_ref, upper_ref, layers)
    edge_ref[...] = jnp.zeros(edge_ref.shape, F32)
    for c in range(3):
        edge_ref[c * rows : (c + 1) * rows] = lowest[c]
        edge_ref[(3 + c) * rows : (4 + c) * rows] = solved[0][c]
        for k in range(layers):
            alone_ref[c, k] = solved[k][c]
    for d in range(3):
        carried = []
        previous = None
        for k in range(layers):
            blocks = block_at(lower_ref, k)
            if previous is None:
                previous = [-blocks[c][d] for c in range(3)]
            else:
                previous = [-value for value in times(blocks, previous)]
            carried.append(previous)
        for c in range(3):
            matrix_ref[(c * 3 + d) * rows : (c * 3 + d + 1) * rows] = carried[-1][c]
        response = carried[-1]
        for k in range(layers - 1, -1, -1):
            if k < layers - 1:
                response = minus(carried[k], times(block_at(upper_ref, k), response))
            for c in range(3):
                from_above_ref[c, d, k] = response[c]
        for c in range(3):
            matrix_ref[(9 + c * 3 + d) * rows : (10 + c * 3 + d) * rows] = response[c]
        response = None
        for k in range(layers - 1, -1, -1):
            blocks = block_at(upper_ref, k)
            if response is None:
                for c in range(3):
                    matrix_ref[(27 + c * 3 + d) * rows : (28 + c * 3 + d) * rows] = blocks[c][d]
                response = [-blocks[c][d] for c in range(3)]
            else:
                response = [-value for value in times(blocks, response)]
            for c in range(3):
                from_below_ref[c, d, k] = response[c]
        for c in range(3):
            matrix_ref[(18 + c * 3 + d) * rows : (19 + c * 3 + d) * rows] = response[c]
    matrix_ref[36 * rows : 37 * rows] = wide(active_ref[0])
    matrix_ref[37 * rows : 38 * rows] = wide(active_ref[layers - 1])


def routing_kernel(
    peers, from_ref, owner_ref, target_ref, block_ref,
    slot_block_ref, slot_source_ref, slot_target_ref, stacked, products,
):
    rows, width = from_ref.shape
    slots = slot_source_ref.shape[0]
    per_peer = slots // peers
    owner = owner_ref[...]
    for o in range(peers):
        stacked[o * rows : (o + 1) * rows] = jnp.where(owner == o, 1.0, 0.0).astype(BF16)
    chosen = stacked[...]
    ones_before = jnp.where(
        lax.broadcasted_iota(jnp.int32, (width, width), 0)
        < lax.broadcasted_iota(jnp.int32, (width, width), 1),
        1.0,
        0.0,
    ).astype(BF16)
    within = jnp.dot(chosen, ones_before, preferred_element_type=F32)
    totals = jnp.dot(chosen, jnp.ones((width, width), BF16), preferred_element_type=F32)
    row_before = jnp.where(
        lax.broadcasted_iota(jnp.int32, (rows, rows), 1)
        < lax.broadcasted_iota(jnp.int32, (rows, rows), 0),
        1.0,
        0.0,
    ).astype(BF16)
    rank = jnp.zeros((rows, width), F32)
    for o in range(peers):
        part = slice(o * rows, (o + 1) * rows)
        before = jnp.dot(row_before, totals[part].astype(BF16), preferred_element_type=F32)
        rank = rank + jnp.where(owner == o, within[part] + before, 0.0)
    rank = rank.astype(jnp.int32)
    slot_row = owner * per_peer + rank // width
    slot_column = rank % width
    source = from_ref[...]
    target = target_ref[...]
    payloads = [
        wide(source // width),
        wide(source % width),
        wide(target // width),
        wide(target % width),
    ] + [wide(block_ref[c, d]) for c in range(3) for d in range(3)]
    row_number = lax.broadcasted_iota(jnp.int32, (slots, width), 0)
    column_number = lax.broadcasted_iota(jnp.int32, (width, width), 0)
    total = jnp.zeros((len(payloads) * slots, width), F32)
    for r in range(rows):
        in_row = row_number == slot_row[r : r + 1]
        left = jnp.concatenate(
            [jnp.where(in_row, payload[r : r + 1], 0.0).astype(BF16) for payload in payloads], axis=0
        )
        right = jnp.where(column_number == slot_column[r : r + 1], 1.0, 0.0).astype(BF16)
        total = total + lax.dot_general(
            left, right, (((1,), (1,)), ((), ())), preferred_element_type=F32
        )
    products[...] = total
    slot_source_ref[...] = (products[0:slots] * width + products[slots : 2 * slots]).astype(jnp.int32)
    slot_target_ref[...] = products[2 * slots : 3 * slots] * width + products[3 * slots : 4 * slots]
    for c in range(3):
        for d in range(3):
            at = 4 + c * 3 + d
            slot_block_ref[c, d] = products[at * slots : (at + 1) * slots]


def couple_kernel(
    first, sections, edge_ref, matrix_ref, alone_ref, above_ref, below_ref, active_ref,
    slot_block_ref, slot_source_ref, slot_target_ref,
    solved_ref, layer_ref, sent_ref, arriving, tops, borders, table,
):
    layers, rows = alone_ref.shape[1], alone_ref.shape[2]
    width = alone_ref.shape[3]
    peers = sent_ref.shape[0]
    slots = slot_source_ref.shape[0]
    per_peer = slots // peers
    s = lax.axis_index("layer")
    a = lax.axis_index("areal")

    def matrix(section, which):
        return [
            [
                matrix_ref[section, (which * 9 + c * 3 + d) * rows : (which * 9 + c * 3 + d + 1) * rows]
                for d in range(3)
            ]
            for c in range(3)
        ]

    def edge(section, which):
        return [
            edge_ref[section, (which * 3 + c) * rows : (which * 3 + c + 1) * rows] for c in range(3)
        ]

    zero = jnp.zeros((rows, width), F32)
    coming = [[zero] * 3]
    for section in range(1, sections):
        value = edge(section - 1, 0)
        if section > 1:
            value = plus(value, times(matrix(section - 1, 0), coming[section - 1]))
        coming.append(value)
    rising = [None] * sections + [[zero] * 3]
    for section in range(sections - 1, 0, -1):
        value = plus(edge(section, 1), times(matrix(section, 1), coming[section]))
        if section < sections - 1:
            value = plus(value, times(matrix(section, 2), rising[section + 1]))
        rising[section] = value
    rising[0] = [zero] * 3
    for section in range(sections):
        for c in range(3):
            arriving[section, c] = coming[section][c]
            tops[section, c] = rising[section + 1][c]
    above = [arriving[s, c] for c in range(3)]
    below = [tops[s, c] for c in range(3)]
    active = [wide(active_ref[k]) for k in range(layers)]
    for k in range(layers):
        for c in range(3):
            value = alone_ref[c, k]
            for d in range(3):
                value = value + above_ref[c, d, k] * above[d] + below_ref[c, d, k] * below[d]
            solved_ref[c, k] = value
            held = value * active[k]
            table[c, k * rows : (k + 1) * rows] = held
            borders[0, c * layers + k : c * layers + k + 1] = held[0:1]
            borders[1, c * layers + k : c * layers + k + 1] = held[rows - 1 : rows]
    before = jnp.maximum(s - 1, 0)
    after = jnp.minimum(s + 1, sections - 1)
    bottom = [
        [
            matrix_ref[before, (27 + c * 3 + d) * rows : (28 + c * 3 + d) * rows]
            for d in range(3)
        ]
        for c in range(3)
    ]
    own_top = [solved_ref[c, 0] for c in range(3)]
    upstairs = minus(above, times(bottom, own_top))
    upper_active = jnp.where(s > 0, matrix_ref[before, 37 * rows : 38 * rows], 0.0)
    lower_active = jnp.where(s < sections - 1, matrix_ref[after, 36 * rows : 37 * rows], 0.0)
    for c in range(3):
        layer_ref[0, c] = upstairs[c] * upper_active
        layer_ref[1, c] = below[c] * lower_active
    half = 128
    groups = [(g, h) for g in range(slots // 8) for h in range(width // half)]
    for g in range(slots // 8):
        for h in range(width // half):
            source = slot_source_ref[g * 8 : (g + 1) * 8, h * half : (h + 1) * half]
            line = source // half
            lane = source % half
            found = [jnp.zeros((8, half), F32)] * 3
            for r in range(layers * rows):
                for q in range(width // half):
                    here = line == r * (width // half) + q
                    for c in range(3):
                        row = jnp.broadcast_to(
                            table[c, r : r + 1, q * half : (q + 1) * half], (8, half)
                        )
                        picked = jnp.take_along_axis(row, lane, axis=1)
                        found[c] = jnp.where(here, picked, found[c])
            for c in range(3):
                value = slot_block_ref[c, 0, g * 8 : (g + 1) * 8, h * half : (h + 1) * half] * found[0]
                for d in range(1, 3):
                    value = value + (
                        slot_block_ref[c, d, g * 8 : (g + 1) * 8, h * half : (h + 1) * half] * found[d]
                    )
                for i in range(8):
                    slot = g * 8 + i
                    peer, at = slot // per_peer, slot % per_peer
                    sent_ref[
                        peer, c * per_peer + at : c * per_peer + at + 1, h * half : (h + 1) * half
                    ] = value[i : i + 1]
    base = 3 * per_peer
    many = 3 * layers
    sums = edge_ref[0, 6 * rows : 6 * rows + 1]
    for section in range(1, sections):
        sums = sums + edge_ref[section, 6 * rows : 6 * rows + 1]
    for peer in range(peers):
        side = jnp.where(peer > a, 1, 0)
        sent_ref[peer, base : base + many] = borders[side, 0:many]
        sent_ref[peer, base + many : base + many + 1] = sums
        if first:
            sent_ref[peer, base + many + 1 : base + many + 1 + per_peer] = slot_target_ref[
                peer * per_peer : (peer + 1) * per_peer
            ]


def weights_of(sums, upto):
    value = lambda step, at: sums[step : step + 1, at : at + 1]
    squared = value(0, 0)
    beta = jnp.sqrt(squared + TINY)
    unscale = 1.0 / beta
    gram = [[squared * unscale * unscale]]
    columns = []
    lengths = []
    for step in range(upto):
        if step == 0:
            weights = [value(0, 1) * unscale * unscale]
            own = value(0, 2) * unscale * unscale
        else:
            weights = [value(step, i) for i in range(step + 1)]
            own = value(step, step + 1)
        size = step + 1
        shadow = []
        for i in range(size):
            total = weights[0] * gram[i][0]
            for k in range(1, size):
                total = total + weights[k] * gram[i][k]
            shadow.append(total)
        left = own
        for i in range(size):
            left = left - weights[i] * (2.0 * weights[i] - shadow[i])
        left = jnp.maximum(left, 0.0)
        length = jnp.sqrt(left + TINY)
        inverse = 1.0 / length
        column = [(weights[i] - shadow[i]) * inverse for i in range(size)]
        for i in range(size):
            gram[i].append(column[i])
        gram.append(column + [left * inverse * inverse])
        columns.append(weights)
        lengths.append(length)
    return beta, unscale, columns, lengths


def operate_kernel(step, *refs):
    last = step == ITERS - 1
    (got_ref, target_ref, solved_ref, layer_ref, diag_ref, coupling_ref, active_ref) = refs[:7]
    at = 7
    if not last:
        pivot_ref, lower_ref, upper_ref = refs[at : at + 3]
        at += 3
    right_ref = refs[at]
    at += 1
    if step > 0:
        sums_ref = refs[at]
        at += 1
        earlier = []
        for i in range(step):
            earlier.append(refs[at : at + (2 if i == 0 else 3)])
            at += len(earlier[-1])
    outs = refs[at:]
    layers, rows, width = solved_ref.shape[1:]
    peers = got_ref.shape[0]
    per_peer = layers * rows // peers
    base = 3 * per_peer
    many = 3 * layers
    cells = layers * rows
    a = lax.axis_index("areal")
    total_ref = outs[-1]
    products_ref = outs[-2]
    outs = outs[:-2]

    row_number = lax.broadcasted_iota(jnp.int32, (cells, width), 0)
    column_number = lax.broadcasted_iota(jnp.int32, (width, width), 0)
    total_ref[...] = jnp.zeros(total_ref.shape, F32)

    def from_peer(peer, carry):
        lefts, rights = [], []
        for i in range(per_peer):
            where = target_ref[peer, base + many + 1 + i : base + many + 2 + i].astype(jnp.int32)
            in_row = row_number == where // width
            rights.append(jnp.where(column_number == where % width, 1.0, 0.0).astype(BF16))
            pieces = []
            for c in range(3):
                rest = got_ref[peer, c * per_peer + i : c * per_peer + i + 1]
                for part in range(PARTS):
                    piece = rest.astype(BF16).astype(F32)
                    rest = rest - piece
                    pieces.append(jnp.where(in_row, piece, 0.0).astype(BF16))
            lefts.append(jnp.concatenate(pieces, axis=0))
        left = jnp.concatenate(lefts, axis=1)
        right = jnp.concatenate(rights, axis=1)
        total_ref[...] += lax.dot_general(
            left, right, (((1,), (1,)), ((), ())), preferred_element_type=F32
        )
        return carry

    lax.fori_loop(0, peers, from_peer, 0)

    active = [wide(active_ref[k]) for k in range(layers)]
    held = [[solved_ref[c, k] * active[k] for c in range(3)] for k in range(layers)]
    row_at = lax.broadcasted_iota(jnp.int32, (rows, width), 0)
    column_at = lax.broadcasted_iota(jnp.int32, (rows, width), 1)
    before, after = jnp.maximum(a - 1, 0), jnp.minimum(a + 1, peers - 1)
    has_before = jnp.where(a > 0, 1.0, 0.0)
    has_after = jnp.where(a < peers - 1, 1.0, 0.0)
    applied = []
    for k in range(layers):
        beside = []
        beside.append(held[k - 1] if k > 0 else [layer_ref[0, c] for c in range(3)])
        beside.append(held[k + 1] if k < layers - 1 else [layer_ref[1, c] for c in range(3)])
        sides = [[], [], [], []]
        for c in range(3):
            border = base + c * layers + k
            low = got_ref[before, border : border + 1] * has_before
            high = got_ref[after, border : border + 1] * has_after
            value = held[k][c]
            sides[0].append(jnp.where(row_at == 0, low, pltpu.roll(value, 1, 0)))
            sides[1].append(jnp.where(row_at == rows - 1, high, pltpu.roll(value, rows - 1, 0)))
            sides[2].append(jnp.where(column_at == 0, 0.0, pltpu.roll(value, 1, 1)))
            sides[3].append(jnp.where(column_at == width - 1, 0.0, pltpu.roll(value, width - 1, 1)))
        result = times(block_at(diag_ref, k), held[k])
        for d, neighbour in enumerate(beside + sides):
            blocks = [[wide(coupling_ref[d, i, j, k]) for j in range(3)] for i in range(3)]
            result = plus(result, times(blocks, neighbour))
        for c in range(3):
            for part in range(PARTS):
                start = (c * PARTS + part) * cells + k * rows
                result[c] = result[c] + total_ref[start : start + rows]
        applied.append(
            [
                active[k] * result[c] + (1.0 - active[k]) * solved_ref[c, k]
                for c in range(3)
            ]
        )

    pairs = []
    if step == 0:
        (applied_ref, edge_ref, alone_ref) = outs
        for k in range(layers):
            for c in range(3):
                applied_ref[c, k] = applied[k][c]
        new = applied
        r = [[right_ref[c, k] for c in range(3)] for k in range(layers)]
        pairs = [(r, r), (r, applied), (applied, applied)]
    else:
        if last:
            (v_ref, z_ref, edge_ref, history_ref) = outs
        else:
            (v_ref, z_ref, w_ref, edge_ref, alone_ref, history_ref) = outs
        fresh = got_ref[0, base + many : base + many + 1]
        for peer in range(1, peers):
            fresh = fresh + got_ref[peer, base + many : base + many + 1]
        history_row = lax.broadcasted_iota(jnp.int32, history_ref.shape, 0)
        sums = jnp.where(history_row == step - 1, fresh, sums_ref[...])
        history_ref[...] = sums
        beta, unscale, columns, lengths = weights_of(sums, step)
        weights = columns[-1]
        inverse = 1.0 / lengths[-1]
        spread = lambda value: jnp.broadcast_to(value, (rows, width))
        lead = spread(inverse * unscale if step == 1 else inverse)
        factors = [spread(weights[i] * inverse * (unscale if i == 0 else 1.0)) for i in range(step)]
        new = []
        members = []
        v_all = [[] for _ in range(step)]
        for k in range(layers):
            new.append([])
            members.append([])
            for c in range(3):
                old_v = [right_ref[c, k]] + [earlier[i][0][c, k] for i in range(1, step)]
                old_z = [earlier[0][0][c, k]] + [earlier[i][1][c, k] for i in range(1, step)]
                old_w = [earlier[0][1][c, k]] + [earlier[i][2][c, k] for i in range(1, step)]
                v = old_w[-1] * lead
                z = solved_ref[c, k] * lead
                w = applied[k][c] * lead
                for i in range(step):
                    v = v - factors[i] * old_v[i]
                    z = z - factors[i] * old_z[i]
                    w = w - factors[i] * old_w[i]
                v_ref[c, k] = v
                z_ref[c, k] = z
                if not last:
                    w_ref[c, k] = w
                new[k].append(w)
                members[k].append(v)
        first = spread(unscale)
        basis = [[[right_ref[c, k] * first for c in range(3)] for k in range(layers)]]
        for i in range(1, step):
            basis.append([[earlier[i][0][c, k] for c in range(3)] for k in range(layers)])
        basis.append(members)
        pairs = [(member, new) for member in basis] + [(new, new)]

    edge_ref[...] = jnp.zeros(edge_ref.shape, F32)
    lane = lax.broadcasted_iota(jnp.int32, (1, width), 1)
    line = jnp.zeros((1, width), F32)
    for number, (left, right) in enumerate(pairs):
        total = jnp.zeros((rows, width), F32)
        for k in range(layers):
            for c in range(3):
                total = total + left[k][c] * right[k][c]
        total = jnp.sum(jnp.sum(total, axis=0, keepdims=True), axis=1, keepdims=True)
        line = jnp.where(lane == number, total, line)
    if last:
        for peer in range(edge_ref.shape[0]):
            edge_ref[peer] = line
    else:
        edge_ref[6 * rows : 6 * rows + 1] = line
        lowest, alone = local_sweeps(new, pivot_ref, lower_ref, upper_ref, layers)
        for c in range(3):
            edge_ref[c * rows : (c + 1) * rows] = lowest[c]
            edge_ref[(3 + c) * rows : (4 + c) * rows] = alone[0][c]
            for k in range(layers):
                alone_ref[c, k] = alone[k][c]


def finish_kernel(dots_ref, sums_ref, z0_ref, z1_ref, z2_ref, z3_ref, update_ref, hessenberg_ref):
    z_refs = (z0_ref, z1_ref, z2_ref, z3_ref)
    rows, width = z0_ref.shape[2:]
    fresh = dots_ref[0]
    for peer in range(1, dots_ref.shape[0]):
        fresh = fresh + dots_ref[peer]
    history_row = lax.broadcasted_iota(jnp.int32, sums_ref.shape, 0)
    sums = jnp.where(history_row == ITERS - 1, fresh, sums_ref[...])
    beta, unscale, columns, lengths = weights_of(sums, ITERS)
    shape = hessenberg_ref.shape
    row_at = lax.broadcasted_iota(jnp.int32, shape, 0)
    column_at = lax.broadcasted_iota(jnp.int32, shape, 1)
    table = jnp.zeros(shape, F32)
    for j in range(ITERS):
        for i, weight in enumerate(columns[j] + [lengths[j]]):
            table = jnp.where((row_at == i) & (column_at == j), weight, table)
    hessenberg_ref[...] = table
    goal = [beta]
    triangle = []
    rotations = []
    for j in range(ITERS):
        entries = list(columns[j])
        for i, (cosine, sine) in enumerate(rotations):
            upper, lower = entries[i], entries[i + 1]
            entries[i] = cosine * upper + sine * lower
            entries[i + 1] = cosine * lower - sine * upper
        radius = jnp.sqrt(entries[j] * entries[j] + lengths[j] * lengths[j])
        cosine, sine = entries[j] / radius, lengths[j] / radius
        rotations.append((cosine, sine))
        entries[j] = radius
        triangle.append(entries)
        leading = goal[j]
        goal[j] = cosine * leading
        goal.append(-sine * leading)
    answer = [None] * ITERS
    for i in range(ITERS - 1, -1, -1):
        partial = goal[i]
        for j in range(i + 1, ITERS):
            partial = partial - triangle[j][i] * answer[j]
        answer[i] = partial / triangle[i][i]
    factors = [
        jnp.broadcast_to(answer[j] * unscale if j == 0 else answer[j], (rows, width))
        for j in range(ITERS)
    ]
    for c in range(3):
        for k in range(z0_ref.shape[1]):
            value = factors[0] * z_refs[0][c, k]
            for j in range(1, ITERS):
                value = value + factors[j] * z_refs[j][c, k]
            update_ref[c, k] = value


def shape_of(*dims, kind=F32):
    return jax.ShapeDtypeStruct(dims, kind)


def local(
    right_side,
    diag_blocks,
    couplings,
    pivot_inverse,
    lower_blocks,
    upper_blocks,
    active_cells,
    link_from,
    link_owner,
    link_target,
    link_blocks,
):
    _, layers, rows, width = right_side.shape
    peers = lax.axis_size("areal")
    sections = lax.axis_size("layer")
    links = link_from.shape[1]
    capacity = 2 * links // peers
    slots = capacity * peers // width
    per_peer = slots // peers
    link_rows = links // width
    field = shape_of(3, layers, rows, width)
    edge_rows = 7 * rows
    sent_rows = -(-(4 * per_peer + 3 * layers + 1) // 8) * 8
    edge_shape = shape_of(edge_rows, width)

    edge, alone, from_above, from_below, matrices = call(
        section_kernel,
        [
            edge_shape,
            field,
            shape_of(3, 3, layers, rows, width),
            shape_of(3, 3, layers, rows, width),
            shape_of(38 * rows, width),
        ],
        name="sections",
    )(right_side, pivot_inverse, lower_blocks, upper_blocks, active_cells)
    all_matrices = lax.all_gather(matrices, "layer", axis=0, tiled=False)
    slot_block, slot_source, slot_target = call(
        functools.partial(routing_kernel, peers),
        [
            shape_of(3, 3, slots, width),
            shape_of(slots, width, kind=jnp.int32),
            shape_of(slots, width),
        ],
        [
            pltpu.VMEM((peers * link_rows, width), BF16),
            pltpu.VMEM((13 * slots, width), F32),
        ],
        name="routing",
    )(
        link_from.reshape(link_rows, width),
        link_owner.reshape(link_rows, width),
        link_target.reshape(link_rows, width),
        link_blocks.reshape(3, 3, link_rows, width),
    )

    target = None
    sums = jnp.zeros((8, width), F32)
    earlier = []
    zs = []
    for step in range(ITERS):
        last = step == ITERS - 1
        edges = lax.all_gather(edge, "layer", axis=0, tiled=False)
        solved, layer_sides, sent = call(
            functools.partial(couple_kernel, step == 0, sections),
            [field, shape_of(2, 3, rows, width), shape_of(peers, sent_rows, width)],
            [
                pltpu.VMEM((sections, 3, rows, width), F32),
                pltpu.VMEM((sections, 3, rows, width), F32),
                pltpu.VMEM((2, 16, width), F32),
                pltpu.VMEM((3, layers * rows, width), F32),
            ],
            name="couple",
        )(
            edges, all_matrices, alone, from_above, from_below, active_cells,
            slot_block, slot_source, slot_target,
        )
        got = lax.all_to_all(sent, "areal", split_axis=0, concat_axis=0, tiled=True)
        if step == 0:
            target = got
        operands = [got, target, solved, layer_sides, diag_blocks, couplings, active_cells]
        if not last:
            operands += [pivot_inverse, lower_blocks, upper_blocks]
        operands.append(right_side)
        if step > 0:
            operands.append(sums)
            for group in earlier:
                operands += list(group)
        history = shape_of(8, width)
        if step == 0:
            outs = [field, edge_shape, field]
        elif last:
            outs = [field, field, shape_of(peers * sections, 1, width), history]
        else:
            outs = [field, field, field, edge_shape, field, history]
        results = call(
            functools.partial(operate_kernel, step),
            outs,
            [
                pltpu.VMEM((8, 128), F32),
                pltpu.VMEM((3 * PARTS * layers * rows, width), F32),
            ],
            name="operate",
        )(*operands)
        if step == 0:
            applied, edge, alone = results
            earlier.append((solved, applied))
            zs.append(solved)
        elif last:
            _, z, dots, sums = results
            zs.append(z)
        else:
            v, z, w, edge, alone, sums = results
            earlier.append((v, z, w))
            zs.append(z)
    dots = lax.all_to_all(dots, ("areal", "layer"), split_axis=0, concat_axis=0, tiled=True)
    update, hessenberg = call(
        finish_kernel, [field, shape_of(ITERS + 1, ITERS)], name="finish"
    )(dots, sums, *zs)
    return update, hessenberg


def solution(mesh):
    placed = (
        P(None, "layer", "areal", None),
        P(None, None, "layer", "areal", None),
        P(None, None, None, "layer", "areal", None),
        P(None, None, "layer", "areal", None),
        P(None, None, "layer", "areal", None),
        P(None, None, "layer", "areal", None),
        P("layer", "areal", None),
        P("layer", "areal"),
        P("layer", "areal", None),
        P("layer", "areal"),
        P(None, None, "layer", "areal"),
    )
    return jax.shard_map(
        local,
        mesh=mesh,
        in_specs=placed,
        out_specs=(P(None, "layer", "areal", None), P()),
        check_vma=False,
    )
```

time: 1040 us -> 150 us (0.14); the launches traced: 1020 us -> 149 us
  other arithmetic: 276 us -> 4.21 us
  local copies, waits for them, and re-layouts: 223 us -> 7.9 us
  starting transfers between devices: 168 us -> 0.04 us
  blocking collectives: 218 us -> 88.5 us
  waiting for transfers between devices: 101 us -> 6.23 us
  Pallas kernels: 0 us -> 27.8 us
  between operations: 34.7 us -> 14.2 us
    psum x5 -> x0, blocking collectives: 218 us -> none  [the longest x4 176 us: local(): lax.psum((local_weights, jnp.sum(result * result)), ('areal', 'layer'))]
    scatter-add x4 -> x0, other arithmetic: 214 us -> none  [local(): result.reshape(3, -1).at[:, targets].add(arriving).reshape(direction.shape)]
    ppermute x56 -> x0, starting transfers between devices: 140 us -> none  [the longest x40 101 us: passed_along(): return lax.ppermute(array, axis, pairs)]
    ppermute x56 -> x0, waiting for transfers between devices: 88.9 us -> none  [the longest x40 88.8 us: passed_along(): return lax.ppermute(array, axis, pairs)]
    gather x8 -> x0, local copies, waits for them, and re-layouts: 73.9 us -> none  [local(): sending = apply_block(link_matrix, flattened[:, sources])]
    all_to_all x0 -> x5, blocking collectives: none -> 63.1 us  [the longest x4 53.4 us: local(): got = lax.all_to_all(sent, 'areal', split_axis=0, concat_axis=0, tiled=True)]
    scatter x31 -> x0, local copies, waits for them, and re-layouts: 58.3 us -> none  [the longest x4 52.2 us: local(): jnp.zeros((3, total_slots), jnp.float32).at[:, slot_of].set(sending)]
    reduce_sum x185 -> x0, other arithmetic: 29.6 us -> none  [the longest x176 23 us: apply_block(): return jnp.sum(matrix_blocks.astype(jnp.float32) * vector[None], axis=1)]
  transfers between devices with their start and end apart: 61 -> 1, of which waited for: 42 -> 1; matrix products, arithmetic and copies ran while one was open for 16% -> 4% of each run, Pallas kernels for 0% -> 1%
where the time goes in v1:
time: 150 us; the launch traced here: 149 us
  blocking collectives  88.5 us (59%)
  Pallas kernels  27.8 us (19%)
  between operations  14.2 us (9%)
  local copies, waits for them, and re-layouts  7.9 us (5%)
  waiting for transfers between devices  6.23 us (4%)
  other arithmetic  4.21 us (3%)
    all_to_all x4, blocking collectives, local(): got = lax.all_to_all(sent, 'areal', split_axis=0, concat_axis=0, tiled=True)  53.4 us
    all_gather x4, blocking collectives, local(): edges = lax.all_gather(edge, 'layer', axis=0, tiled=False)  25.4 us
    pallas_call x4, Pallas kernels, local(): call(functools.partial(operate_kernel, step), outs, [pltpu.VMEM((8, 128),...  16.1 us
    all_to_all x1, blocking collectives, local(): lax.all_to_all(dots, ('areal', 'layer'), split_axis=0, concat_axis=0, til...  9.73 us
    pallas_call x4, Pallas kernels, local(): call(functools.partial(couple_kernel, step == 0, sections), [field, shape...  7.23 us
    all_gather x1, waiting for transfers between devices, local(): all_matrices = lax.all_gather(matrices, 'layer', axis=0, tiled=False)  6.22 us
    unnamed x29, local copies, waits for them, and re-layouts  6.21 us
    unnamed x3, other arithmetic  4.21 us
  transfers between devices with their start and end apart: 1, of which 1 were waited for; matrix products, arithmetic and copies ran while one was open for 4% of the time, Pallas kernels for 1%

profile of v1, /device:TPU:0, one launch (start us, length us, event | category | flops | bytes accessed | tf_op | source)
XLA Modules:
  0.0 148.8 jit_solution(5175260548290911293)
XLA Ops:
  7.2 0.0 all-gather.7.cloned.1.call-start
  7.2 0.0 copy-start.3
  7.2 0.7 copy-done.3
  8.0 0.0 copy-start.5
  8.0 0.9 copy-done.5
  8.9 0.9 copy-done.8
  9.8 0.9 copy-done.10
  10.7 0.9 copy-done.12
  11.6 0.9 sections.1
  12.5 0.0 all-gather.7.cloned.1.call-update
  12.5 0.5 broadcast.9
  13.1 1.4 reduce.9
  14.5 1.4 reduce.10
  15.9 1.4 reduce.11
  17.3 1.0 reshape.19.block_ref
  18.3 1.4 routing.1
  19.8 8.1 %all-gather = f32[224,256]{1,0:T(8,128)S(1)} all-gather(f32[56,256]{1,0:T(8,128)S(1)} %get-tuple-element.40), channel_id=2, replica_groups=mesh['areal'=8,'layer'=4] {'layer'}, dimensions={0}, use_global_device_ids=true | all-gather | bytes 286720 | tf_op jit(solution)/shard_map/all_gather | solution.py:635
  27.9 6.2 %all-gather.7.cloned.1.call-done = f32[1216,256]{1,0:T(8,128)} async-done(((f32[304,256]{1,0:T(8,128)}), f32[1216,256]{1,0:T(8,128)}) %all-gather.7.cloned.1.call-update) | async-done | bytes 1245200 | tf_op jit(solution)/shard_map/all_gather | solution.py:609
  34.1 0.0 copy-done.4
  34.1 1.3 copy-done
  35.4 0.0 copy-start.11
  35.4 0.0 copy-start.13
  35.4 1.8 %couple.4 = (f32[3,4,8,256]{3,2,1,0:T(8,128)S(1)}, f32[2,3,8,256]{3,2,1,0:T(8,128)S(1)}, f32[8,32,256]{2,1,0:T(8,128)S(1)}) custom-call(f32[4,56,256]{2,1,0:T(8,128)S(1)} %bitcast.12, f32[4,304,256]{2,1,0:T(8,128)S(1)} %bitcast.8, f32[3,4,8,256]{3,2,1,0:T(8,128)S(1)} %get-tuple-element.42.alone_ref, f32[3,3,4,8,256]{4,3,2,1,0:T(8,128)S(1)} %get-tuple-element.43.above_ref, ...), custom_call_target="tpu_custom_call" | custom-call | flops 4194304 | bytes 1048576 | tf_op jit(solution)/shard_map/couple/pallas_call | solution.py:636
  37.3 14.9 %all_to_all.25.refs_0_.refs_1_ = f32[8,32,256]{2,1,0:T(8,128)S(1)} all-to-all(f32[8,32,256]{2,1,0:T(8,128)S(1)} %get-tuple-element.48), channel_id=1, replica_groups=mesh['areal'=8,'layer'=4] {'areal'}, dimensions={0} | all-to-all | bytes 524288 | tf_op jit(solution)/shard_map/all_to_all | solution.py:650
  52.2 0.0 copy-done.2
  52.2 0.0 copy-done.6
  52.2 0.0 copy-done.7
  52.2 0.0 copy-done.9
  52.2 0.0 copy-done.11
  52.2 0.0 copy-done.13
  52.2 0.0 copy-start.1
  52.3 3.5 %operate.4 = (f32[3,4,8,256]{3,2,1,0:T(8,128)S(1)}, f32[56,256]{1,0:T(8,128)S(1)}, f32[3,4,8,256]{3,2,1,0:T(8,128)S(1)}) custom-call(f32[8,32,256]{2,1,0:T(8,128)S(1)} %all_to_all.25.refs_0_.refs_1_, f32[8,32,256]{2,1,0:T(8,128)S(1)} %all_to_all.25.refs_0_.refs_1_, f32[3,4,8,256]{3,2,1,0:T(8,128)S(1)} %get-tuple-element.49.refs_2_.refs_12_.refs_9_.z0_ref, ...), custom_call_target="tpu_custom_call" | custom-call | flops 4194304 | bytes 1048576 | tf_op jit(solution)/shard_map/operate/pallas_call | solution.py:668
  55.7 5.7 %all-gather.2 = f32[224,256]{1,0:T(8,128)S(1)} all-gather(f32[56,256]{1,0:T(8,128)S(1)} %get-tuple-element.51), channel_id=4, replica_groups=mesh['areal'=8,'layer'=4] {'layer'}, dimensions={0}, use_global_device_ids=true | all-gather | bytes 286720 | tf_op jit(solution)/shard_map/all_gather | solution.py:635
  61.4 0.0 copy-done.1
  61.4 1.8 %couple.5 = (f32[3,4,8,256]{3,2,1,0:T(8,128)S(1)}, f32[2,3,8,256]{3,2,1,0:T(8,128)S(1)}, f32[8,32,256]{2,1,0:T(8,128)S(1)}) custom-call(f32[4,56,256]{2,1,0:T(8,128)S(1)} %bitcast.14, f32[4,304,256]{2,1,0:T(8,128)S(1)} %bitcast.9, f32[3,4,8,256]{3,2,1,0:T(8,128)S(1)} %get-tuple-element.52.alone_ref, f32[3,3,4,8,256]{4,3,2,1,0:T(8,128)S(1)} %get-tuple-element.43.above_ref, ...), custom_call_target="tpu_custom_call" | custom-call | flops 4194304 | bytes 1048576 | tf_op jit(solution)/shard_map/couple/pallas_call | solution.py:636
  63.2 12.8 %all_to_all.26.refs_0_ = f32[8,32,256]{2,1,0:T(8,128)S(1)} all-to-all(f32[8,32,256]{2,1,0:T(8,128)S(1)} %get-tuple-element.53), channel_id=1, replica_groups=mesh['areal'=8,'layer'=4] {'areal'}, dimensions={0} | all-to-all | bytes 524288 | tf_op jit(solution)/shard_map/all_to_all | solution.py:650
  76.0 3.7 %operate.5 = (f32[3,4,8,256]{3,2,1,0:T(8,128)S(1)}, f32[3,4,8,256]{3,2,1,0:T(8,128)S(1)}, f32[3,4,8,256]{3,2,1,0:T(8,128)S(1)}, f32[56,256]{1,0:T(8,128)S(1)}, f...) custom-call(f32[8,32,256]{2,1,0:T(8,128)S(1)} %all_to_all.26.refs_0_, f32[8,32,256]{2,1,0:T(8,128)S(1)} %all_to_all.25.refs_0_.refs_1_, ...), custom_call_target="tpu_custom_call" | custom-call | flops 4194304 | bytes 1048576 | tf_op jit(solution)/shard_map/operate/pallas_call | solution.py:668
  79.7 5.7 %all-gather.3 = f32[224,256]{1,0:T(8,128)S(1)} all-gather(f32[56,256]{1,0:T(8,128)S(1)} %get-tuple-element.57), channel_id=5, replica_groups=mesh['areal'=8,'layer'=4] {'layer'}, dimensions={0}, use_global_device_ids=true | all-gather | bytes 286720 | tf_op jit(solution)/shard_map/all_gather | solution.py:635
  85.4 1.8 %couple.6 = (f32[3,4,8,256]{3,2,1,0:T(8,128)S(1)}, f32[2,3,8,256]{3,2,1,0:T(8,128)S(1)}, f32[8,32,256]{2,1,0:T(8,128)S(1)}) custom-call(f32[4,56,256]{2,1,0:T(8,128)S(1)} %bitcast.15, f32[4,304,256]{2,1,0:T(8,128)S(1)} %bitcast.10, f32[3,4,8,256]{3,2,1,0:T(8,128)S(1)} %get-tuple-element.58.alone_ref, f32[3,3,4,8,256]{4,3,2,1,0:T(8,128)S(1)} %get-tuple-element.43.above_ref, ...), custom_call_target="tpu_custom_call" | custom-call | flops 4194304 | bytes 1048576 | tf_op jit(solution)/shard_map/couple/pallas_call | solution.py:636
  87.3 12.8 %all_to_all.27.refs_0_ = f32[8,32,256]{2,1,0:T(8,128)S(1)} all-to-all(f32[8,32,256]{2,1,0:T(8,128)S(1)} %get-tuple-element.59), channel_id=1, replica_groups=mesh['areal'=8,'layer'=4] {'areal'}, dimensions={0} | all-to-all | bytes 524288 | tf_op jit(solution)/shard_map/all_to_all | solution.py:650
  100.1 4.0 %operate.6 = (f32[3,4,8,256]{3,2,1,0:T(8,128)S(1)}, f32[3,4,8,256]{3,2,1,0:T(8,128)S(1)}, f32[3,4,8,256]{3,2,1,0:T(8,128)S(1)}, f32[56,256]{1,0:T(8,128)S(1)}, f...) custom-call(f32[8,32,256]{2,1,0:T(8,128)S(1)} %all_to_all.27.refs_0_, f32[8,32,256]{2,1,0:T(8,128)S(1)} %all_to_all.25.refs_0_.refs_1_, ...), custom_call_target="tpu_custom_call" | custom-call | flops 4194304 | bytes 1048576 | tf_op jit(solution)/shard_map/operate/pallas_call | solution.py:668
  104.1 5.9 %all-gather.4 = f32[224,256]{1,0:T(8,128)S(1)} all-gather(f32[56,256]{1,0:T(8,128)S(1)} %get-tuple-element.66), channel_id=6, replica_groups=mesh['areal'=8,'layer'=4] {'layer'}, dimensions={0}, use_global_device_ids=true | all-gather | bytes 286720 | tf_op jit(solution)/shard_map/all_gather | solution.py:635
  110.0 1.8 %couple.7 = (f32[3,4,8,256]{3,2,1,0:T(8,128)S(1)}, f32[2,3,8,256]{3,2,1,0:T(8,128)S(1)}, f32[8,32,256]{2,1,0:T(8,128)S(1)}) custom-call(f32[4,56,256]{2,1,0:T(8,128)S(1)} %bitcast.13, f32[4,304,256]{2,1,0:T(8,128)S(1)} %bitcast.11, f32[3,4,8,256]{3,2,1,0:T(8,128)S(1)} %get-tuple-element.67.alone_ref, f32[3,3,4,8,256]{4,3,2,1,0:T(8,128)S(1)} %get-tuple-element.43.above_ref, ...), custom_call_target="tpu_custom_call" | custom-call | flops 4194304 | bytes 1048576 | tf_op jit(solution)/shard_map/couple/pallas_call | solution.py:636
  111.8 12.8 %all_to_all.28.refs_0_ = f32[8,32,256]{2,1,0:T(8,128)S(1)} all-to-all(f32[8,32,256]{2,1,0:T(8,128)S(1)} %get-tuple-element.68), channel_id=1, replica_groups=mesh['areal'=8,'layer'=4] {'areal'}, dimensions={0} | all-to-all | bytes 524288 | tf_op jit(solution)/shard_map/all_to_all | solution.py:650
  124.6 4.9 %operate.7 = (f32[3,4,8,256]{3,2,1,0:T(8,128)}, f32[3,4,8,256]{3,2,1,0:T(8,128)S(1)}, f32[32,1,256]{2,1,0:T(1,128)S(1)}, f32[8,256]{1,0:T(8,128)S(1)}) custom-call(f32[8,32,256]{2,1,0:T(8,128)S(1)} %all_to_all.28.refs_0_, f32[8,32,256]{2,1,0:T(8,128)S(1)} %all_to_all.25.refs_0_.refs_1_, f32[3,4,8,256]{3,2,1,0:T(8,128)S(1)} %get-tuple-element.69.refs_2_, ...), custom_call_target="tpu_custom_call" | custom-call | flops 4194304 | bytes 1048576 | tf_op jit(solution)/shard_map/operate/pallas_call | solution.py:668
  129.5 9.7 %all_to_all.29.dots_ref = f32[32,1,256]{2,1,0:T(1,128)S(1)} all-to-all(f32[32,1,256]{2,1,0:T(1,128)S(1)} %get-tuple-element.75), channel_id=1, replica_groups=mesh['areal'=8,'layer'=4] {'areal','layer'}, dimensions={0} | all-to-all | bytes 65536 | tf_op jit(solution)/shard_map/all_to_all | solution.py:688
  139.2 2.1 %finish.1 = (f32[3,4,8,256]{3,2,1,0:T(8,128)}, f32[5,4]{1,0:T(8,128)S(1)}) custom-call(f32[32,1,256]{2,1,0:T(1,128)S(1)} %all_to_all.29.dots_ref, f32[8,256]{1,0:T(8,128)S(1)} %get-tuple-element.76.sums_ref, f32[3,4,8,256]{3,2,1,0:T(8,128)S(1)} %get-tuple-element.49.refs_2_.refs_12_.refs_9_.z0_ref, ...), custom_call_target="tpu_custom_call" | custom-call | flops 4194304 | bytes 1048576 | tf_op jit(solution)/shard_map/finish/pallas_call | solution.py:689
  141.3 0.7 copy.13
  (13 shorter events, 0.0 us)
Async XLA Ops:
  7.2 27.0 %all-gather.7.cloned.1.call-start = ((), (), s32[]{:S(2)}) async-start(), calls=%async_computation.5 | async-start | bytes 1556480 | tf_op jit(solution)/shard_map/all_gather | solution.py:609
  7.2 0.8 copy-start.3
  8.0 0.9 copy-start.5
  8.9 0.9 copy-start.8
  9.8 0.9 copy-start.10
  10.7 0.9 copy-start.12
  11.6 22.5 %copy-start.4 = (s32[4,8,256]{2,1,0:T(8,128)S(1)}, s32[4,8,256]{2,1,0:T(8,128)}, u32[]{:S(2)}) copy-start(s32[4,8,256]{2,1,0:T(8,128)} %refs_6_.7) | copy-start | bytes 98308
  34.1 1.3 copy-start
  35.4 16.8 %copy-start.2 = (bf16[6,3,3,4,8,256]{5,4,3,2,1,0:T(8,128)(2,1)S(1)}, bf16[6,3,3,4,8,256]{5,4,3,2,1,0:T(8,128)(2,1)}, u32[]{:S(2)}) copy-start(bf16[6,3,3,4,8,256]{5,4,3,2,1,0:T(8,128)(2,1)} %refs_5_.7) | copy-start | bytes 2654212
  35.4 16.8 %copy-start.6 = (f32[3,4,8,256]{3,2,1,0:T(8,128)S(1)}, f32[3,4,8,256]{3,2,1,0:T(8,128)}, u32[]{:S(2)}) copy-start(f32[3,4,8,256]{3,2,1,0:T(8,128)} %refs_7_.7) | copy-start | bytes 294916
  35.4 16.8 %copy-start.7 = (bf16[3,3,4,8,256]{4,3,2,1,0:T(8,128)(2,1)S(1)}, bf16[3,3,4,8,256]{4,3,2,1,0:T(8,128)(2,1)}, u32[]{:S(2)}) copy-start(bf16[3,3,4,8,256]{4,3,2,1,0:T(8,128)(2,1)} %refs_4_.7) | copy-start | bytes 442372
  35.4 16.8 %copy-start.9 = (bf16[3,3,4,8,256]{4,3,2,1,0:T(8,128)(2,1)S(1)}, bf16[3,3,4,8,256]{4,3,2,1,0:T(8,128)(2,1)}, u32[]{:S(2)}) copy-start(bf16[3,3,4,8,256]{4,3,2,1,0:T(8,128)(2,1)} %refs_7_.6) | copy-start | bytes 442372
  35.4 16.8 %copy-start.11 = (bf16[3,3,4,8,256]{4,3,2,1,0:T(8,128)(2,1)S(1)}, bf16[3,3,4,8,256]{4,3,2,1,0:T(8,128)(2,1)}, u32[]{:S(2)}) copy-start(bf16[3,3,4,8,256]{4,3,2,1,0:T(8,128)(2,1)} %refs_8_.5) | copy-start | bytes 442372
  35.4 16.8 %copy-start.13 = (bf16[3,3,4,8,256]{4,3,2,1,0:T(8,128)(2,1)S(1)}, bf16[3,3,4,8,256]{4,3,2,1,0:T(8,128)(2,1)}, u32[]{:S(2)}) copy-start(bf16[3,3,4,8,256]{4,3,2,1,0:T(8,128)(2,1)} %refs_9_.5) | copy-start | bytes 442372
  52.2 9.2 %copy-start.1 = (f32[1216,256]{1,0:T(8,128)S(1)}, f32[1216,256]{1,0:T(8,128)}, u32[]{:S(2)}) copy-start(f32[1216,256]{1,0:T(8,128)} %all-gather.7.cloned.1.call-done) | copy-start | bytes 3735556
Sparse Core Ops, SparseCore 0:
  12.7 21.4 all-gather.6

commit v2 on v1

--- a/solution.py
+++ b/solution.py
@@ -16,11 +16,13 @@
 VMEM = pl.BlockSpec(memory_space=pltpu.VMEM)
 
 
-def call(kernel, outs, scratch=(), name=None, flops=1 << 22, moved=1 << 20):
+def call(kernel, outs, scratch=(), name=None, inputs=None, flops=1 << 22, moved=1 << 20):
     many = isinstance(outs, (list, tuple))
+    where = {} if inputs is None else {"in_specs": inputs}
     return pl.pallas_call(
         kernel,
         out_shape=outs,
+        **where,
         out_specs=[VMEM] * len(outs) if many else VMEM,
         scratch_shapes=list(scratch),
         compiler_params=pltpu.CompilerParams(vmem_limit_bytes=40 << 20),
@@ -75,17 +77,17 @@
     return forward[layers - 1], backward
 
 
-def section_kernel(
+def section_part(
     right_ref, pivot_ref, lower_ref, upper_ref, active_ref,
-    edge_ref, alone_ref, from_above_ref, from_below_ref, matrix_ref,
+    edge_ref, next_ref, alone_ref, from_above_ref, from_below_ref, matrix_ref,
 ):
     layers, rows = right_ref.shape[1], right_ref.shape[2]
     planes = [[right_ref[c, k] for c in range(3)] for k in range(layers)]
     lowest, solved = local_sweeps(planes, pivot_ref, lower_ref, upper_ref, layers)
-    edge_ref[...] = jnp.zeros(edge_ref.shape, F32)
     for c in range(3):
-        edge_ref[c * rows : (c + 1) * rows] = lowest[c]
-        edge_ref[(3 + c) * rows : (4 + c) * rows] = solved[0][c]
+        for ref in (edge_ref, next_ref):
+            ref[c * rows : (c + 1) * rows] = lowest[c]
+            ref[(3 + c) * rows : (4 + c) * rows] = solved[0][c]
         for k in range(layers):
             alone_ref[c, k] = solved[k][c]
     for d in range(3):
@@ -113,7 +115,7 @@
             blocks = block_at(upper_ref, k)
             if response is None:
                 for c in range(3):
-                    matrix_ref[(27 + c * 3 + d) * rows : (28 + c * 3 + d) * rows] = blocks[c][d]
+                    next_ref[(6 + c * 3 + d) * rows : (7 + c * 3 + d) * rows] = blocks[c][d]
                 response = [-blocks[c][d] for c in range(3)]
             else:
                 response = [-value for value in times(blocks, response)]
@@ -121,18 +123,17 @@
                 from_below_ref[c, d, k] = response[c]
         for c in range(3):
             matrix_ref[(18 + c * 3 + d) * rows : (19 + c * 3 + d) * rows] = response[c]
-    matrix_ref[36 * rows : 37 * rows] = wide(active_ref[0])
-    matrix_ref[37 * rows : 38 * rows] = wide(active_ref[layers - 1])
-
-
-def routing_kernel(
-    peers, from_ref, owner_ref, target_ref, block_ref,
-    slot_block_ref, slot_source_ref, slot_target_ref, stacked, products,
+    edge_ref[6 * rows : 7 * rows] = wide(active_ref[0])
+    next_ref[15 * rows : 16 * rows] = wide(active_ref[layers - 1])
+
+
+def routing_part(
+    peers, folded, block_ref, slot_block_ref, slot_source_ref, slot_target_ref, stacked, products
 ):
-    rows, width = from_ref.shape
+    rows, width = folded.shape[1:]
     slots = slot_source_ref.shape[0]
     per_peer = slots // peers
-    owner = owner_ref[...]
+    owner = folded[1]
     for o in range(peers):
         stacked[o * rows : (o + 1) * rows] = jnp.where(owner == o, 1.0, 0.0).astype(BF16)
     chosen = stacked[...]
@@ -158,21 +159,30 @@
     rank = rank.astype(jnp.int32)
     slot_row = owner * per_peer + rank // width
     slot_column = rank % width
-    source = from_ref[...]
-    target = target_ref[...]
+    source = folded[0]
+    target = folded[2]
     payloads = [
         wide(source // width),
         wide(source % width),
         wide(target // width),
         wide(target % width),
-    ] + [wide(block_ref[c, d]) for c in range(3) for d in range(3)]
+    ]
     row_number = lax.broadcasted_iota(jnp.int32, (slots, width), 0)
     column_number = lax.broadcasted_iota(jnp.int32, (width, width), 0)
-    total = jnp.zeros((len(payloads) * slots, width), F32)
+    total = jnp.zeros(products.shape, F32)
     for r in range(rows):
         in_row = row_number == slot_row[r : r + 1]
         left = jnp.concatenate(
-            [jnp.where(in_row, payload[r : r + 1], 0.0).astype(BF16) for payload in payloads], axis=0
+            [
+                jnp.where(in_row, payload, 0.0).astype(BF16)
+                for payload in [payload[r : r + 1] for payload in payloads]
+                + [
+                    wide(block_ref[c, d : d + 1, r * width : (r + 1) * width])
+                    for c in range(3)
+                    for d in range(3)
+                ]
+            ],
+            axis=0,
         )
         right = jnp.where(column_number == slot_column[r : r + 1], 1.0, 0.0).astype(BF16)
         total = total + lax.dot_general(
@@ -187,11 +197,64 @@
             slot_block_ref[c, d] = products[at * slots : (at + 1) * slots]
 
 
+def setup_kernel(
+    peers,
+    right_hbm, pivot_hbm, lower_hbm, upper_hbm, active_hbm,
+    from_hbm, owner_hbm, target_hbm, block_hbm,
+    edge_ref, next_ref, alone_ref, from_above_ref, from_below_ref, matrix_ref,
+    slot_block_ref, slot_source_ref, slot_target_ref,
+    right_ref, pivot_ref, lower_ref, upper_ref, active_ref,
+    from_ref, owner_ref, target_ref, block_ref,
+    stacked, products, folded, semaphores,
+):
+    copies = [
+        pltpu.make_async_copy(source, landing, semaphores.at[number])
+        for number, (source, landing) in enumerate(
+            [
+                (lower_hbm, lower_ref),
+                (upper_hbm, upper_ref),
+                (active_hbm, active_ref),
+                (pivot_hbm, pivot_ref),
+                (right_hbm, right_ref),
+                (owner_hbm, owner_ref),
+                (from_hbm, from_ref),
+                (target_hbm, target_ref),
+                (block_hbm, block_ref),
+            ]
+        )
+    ]
+    for copy in copies:
+        copy.start()
+    for copy in copies:
+        copy.wait()
+    section_part(
+        right_ref, pivot_ref, lower_ref, upper_ref, active_ref,
+        edge_ref, next_ref, alone_ref, from_above_ref, from_below_ref, matrix_ref,
+    )
+    rows, width = folded.shape[1:]
+    for r in range(rows):
+        for number, ref in enumerate((from_ref, owner_ref, target_ref)):
+            folded[number, r : r + 1] = ref[0:1, r * width : (r + 1) * width]
+    routing_part(
+        peers, folded, block_ref, slot_block_ref, slot_source_ref, slot_target_ref, stacked, products
+    )
+
+
 def couple_kernel(
-    first, sections, edge_ref, matrix_ref, alone_ref, above_ref, below_ref, active_ref,
-    slot_block_ref, slot_source_ref, slot_target_ref,
-    solved_ref, layer_ref, sent_ref, arriving, tops, borders, table,
+    first, sections, *refs,
 ):
+    turned, refs = refs[: sections - 1], refs[sections - 1 :]
+    if first:
+        own_ref, refs = refs[0], refs[1:]
+        edge_ref = refs[-1]
+        refs = refs[:-1]
+    else:
+        edge_ref, refs = refs[0], refs[1:]
+    (
+        matrix_ref, alone_ref, above_ref, below_ref, active_ref,
+        slot_block_ref, slot_source_ref, slot_target_ref,
+        solved_ref, layer_ref, sent_ref, arriving, tops, borders, table,
+    ) = refs
     layers, rows = alone_ref.shape[1], alone_ref.shape[2]
     width = alone_ref.shape[3]
     peers = sent_ref.shape[0]
@@ -199,6 +262,10 @@
     per_peer = slots // peers
     s = lax.axis_index("layer")
     a = lax.axis_index("areal")
+    if first:
+        edge_ref[s] = own_ref[0 : 6 * rows]
+        for turn in range(1, sections):
+            edge_ref[lax.rem(s - turn + sections, sections)] = turned[turn - 1][0 : 6 * rows]
 
     def matrix(section, which):
         return [
@@ -245,19 +312,15 @@
             table[c, k * rows : (k + 1) * rows] = held
             borders[0, c * layers + k : c * layers + k + 1] = held[0:1]
             borders[1, c * layers + k : c * layers + k + 1] = held[rows - 1 : rows]
-    before = jnp.maximum(s - 1, 0)
-    after = jnp.minimum(s + 1, sections - 1)
+    previous, following = turned[0], turned[-1]
     bottom = [
-        [
-            matrix_ref[before, (27 + c * 3 + d) * rows : (28 + c * 3 + d) * rows]
-            for d in range(3)
-        ]
+        [previous[(6 + c * 3 + d) * rows : (7 + c * 3 + d) * rows] for d in range(3)]
         for c in range(3)
     ]
     own_top = [solved_ref[c, 0] for c in range(3)]
     upstairs = minus(above, times(bottom, own_top))
-    upper_active = jnp.where(s > 0, matrix_ref[before, 37 * rows : 38 * rows], 0.0)
-    lower_active = jnp.where(s < sections - 1, matrix_ref[after, 36 * rows : 37 * rows], 0.0)
+    upper_active = jnp.where(s > 0, previous[15 * rows : 16 * rows], 0.0)
+    lower_active = jnp.where(s < sections - 1, following[6 * rows : 7 * rows], 0.0)
     for c in range(3):
         layer_ref[0, c] = upstairs[c] * upper_active
         layer_ref[1, c] = below[c] * lower_active
@@ -287,22 +350,28 @@
                 for i in range(8):
                     slot = g * 8 + i
                     peer, at = slot // per_peer, slot % per_peer
-                    sent_ref[
-                        peer, c * per_peer + at : c * per_peer + at + 1, h * half : (h + 1) * half
-                    ] = value[i : i + 1]
-    base = 3 * per_peer
+                    start = (c * per_peer + at) * width + h * half
+                    sent_ref[peer, 0:1, start : start + half] = value[i : i + 1]
+    base = 3 * per_peer * width
     many = 3 * layers
-    sums = edge_ref[0, 6 * rows : 6 * rows + 1]
-    for section in range(1, sections):
-        sums = sums + edge_ref[section, 6 * rows : 6 * rows + 1]
+    if not first:
+        sums = edge_ref[0, 6 * rows : 6 * rows + 1, 0:half]
+        for section in range(1, sections):
+            sums = sums + edge_ref[section, 6 * rows : 6 * rows + 1, 0:half]
     for peer in range(peers):
         side = jnp.where(peer > a, 1, 0)
-        sent_ref[peer, base : base + many] = borders[side, 0:many]
-        sent_ref[peer, base + many : base + many + 1] = sums
-        if first:
-            sent_ref[peer, base + many + 1 : base + many + 1 + per_peer] = slot_target_ref[
-                peer * per_peer : (peer + 1) * per_peer
-            ]
+        for i in range(many):
+            start = base + i * width
+            sent_ref[peer, 0:1, start : start + width] = borders[side, i : i + 1]
+        start = base + many * width
+        if not first:
+            sent_ref[peer, 0:1, start : start + half] = sums
+        else:
+            for i in range(per_peer):
+                at = peer * per_peer + i
+                sent_ref[peer, 0:1, start + i * width : start + (i + 1) * width] = slot_target_ref[
+                    at : at + 1
+                ]
 
 
 def weights_of(sums, upto):
@@ -362,13 +431,13 @@
     layers, rows, width = solved_ref.shape[1:]
     peers = got_ref.shape[0]
     per_peer = layers * rows // peers
-    base = 3 * per_peer
+    base = 3 * per_peer * width
     many = 3 * layers
+    ending = base + many * width
     cells = layers * rows
     a = lax.axis_index("areal")
     total_ref = outs[-1]
-    products_ref = outs[-2]
-    outs = outs[:-2]
+    outs = outs[:-1]
 
     row_number = lax.broadcasted_iota(jnp.int32, (cells, width), 0)
     column_number = lax.broadcasted_iota(jnp.int32, (width, width), 0)
@@ -377,12 +446,15 @@
     def from_peer(peer, carry):
         lefts, rights = [], []
         for i in range(per_peer):
-            where = target_ref[peer, base + many + 1 + i : base + many + 2 + i].astype(jnp.int32)
+            where = target_ref[
+                peer, 0:1, ending + i * width : ending + (i + 1) * width
+            ].astype(jnp.int32)
             in_row = row_number == where // width
             rights.append(jnp.where(column_number == where % width, 1.0, 0.0).astype(BF16))
             pieces = []
             for c in range(3):
-                rest = got_ref[peer, c * per_peer + i : c * per_peer + i + 1]
+                start = (c * per_peer + i) * width
+                rest = got_ref[peer, 0:1, start : start + width]
                 for part in range(PARTS):
                     piece = rest.astype(BF16).astype(F32)
                     rest = rest - piece
@@ -411,9 +483,9 @@
         beside.append(held[k + 1] if k < layers - 1 else [layer_ref[1, c] for c in range(3)])
         sides = [[], [], [], []]
         for c in range(3):
-            border = base + c * layers + k
-            low = got_ref[before, border : border + 1] * has_before
-            high = got_ref[after, border : border + 1] * has_after
+            border = base + (c * layers + k) * width
+            low = got_ref[before, 0:1, border : border + width] * has_before
+            high = got_ref[after, 0:1, border : border + width] * has_after
             value = held[k][c]
             sides[0].append(jnp.where(row_at == 0, low, pltpu.roll(value, 1, 0)))
             sides[1].append(jnp.where(row_at == rows - 1, high, pltpu.roll(value, rows - 1, 0)))
@@ -448,9 +520,9 @@
             (v_ref, z_ref, edge_ref, history_ref) = outs
         else:
             (v_ref, z_ref, w_ref, edge_ref, alone_ref, history_ref) = outs
-        fresh = got_ref[0, base + many : base + many + 1]
+        fresh = got_ref[0, 0:1, ending : ending + 128]
         for peer in range(1, peers):
-            fresh = fresh + got_ref[peer, base + many : base + many + 1]
+            fresh = fresh + got_ref[peer, 0:1, ending : ending + 128]
         history_row = lax.broadcasted_iota(jnp.int32, history_ref.shape, 0)
         sums = jnp.where(history_row == step - 1, fresh, sums_ref[...])
         history_ref[...] = sums
@@ -491,8 +563,8 @@
         pairs = [(member, new) for member in basis] + [(new, new)]
 
     edge_ref[...] = jnp.zeros(edge_ref.shape, F32)
-    lane = lax.broadcasted_iota(jnp.int32, (1, width), 1)
-    line = jnp.zeros((1, width), F32)
+    lane = lax.broadcasted_iota(jnp.int32, (1, 128), 1)
+    line = jnp.zeros((1, 128), F32)
     for number, (left, right) in enumerate(pairs):
         total = jnp.zeros((rows, width), F32)
         for k in range(layers):
@@ -504,7 +576,7 @@
         for peer in range(edge_ref.shape[0]):
             edge_ref[peer] = line
     else:
-        edge_ref[6 * rows : 6 * rows + 1] = line
+        edge_ref[6 * rows : 6 * rows + 1, 0:128] = line
         lowest, alone = local_sweeps(new, pivot_ref, lower_ref, upper_ref, layers)
         for c in range(3):
             edge_ref[c * rows : (c + 1) * rows] = lowest[c]
@@ -565,6 +637,11 @@
             update_ref[c, k] = value
 
 
+def turn(array, by):
+    count = lax.axis_size("layer")
+    return lax.ppermute(array, "layer", [(i, (i + by) % count) for i in range(count)])
+
+
 def shape_of(*dims, kind=F32):
     return jax.ShapeDtypeStruct(dims, kind)
 
@@ -592,59 +669,78 @@
     link_rows = links // width
     field = shape_of(3, layers, rows, width)
     edge_rows = 7 * rows
-    sent_rows = -(-(4 * per_peer + 3 * layers + 1) // 8) * 8
+    sent_width = (3 * per_peer + 3 * layers) * width + 128
+    first_width = (4 * per_peer + 3 * layers) * width
     edge_shape = shape_of(edge_rows, width)
-
-    edge, alone, from_above, from_below, matrices = call(
-        section_kernel,
+    hbm = pl.BlockSpec(memory_space=pltpu.HBM)
+    operands = [
+        right_side,
+        pivot_inverse,
+        lower_blocks,
+        upper_blocks,
+        active_cells,
+        link_from,
+        link_owner.reshape(1, links),
+        link_target,
+        link_blocks.reshape(3, 3, links),
+    ]
+    (
+        edge, following, alone, from_above, from_below, matrices,
+        slot_block, slot_source, slot_target,
+    ) = call(
+        functools.partial(setup_kernel, peers),
         [
             edge_shape,
+            shape_of(16 * rows, width),
             field,
             shape_of(3, 3, layers, rows, width),
             shape_of(3, 3, layers, rows, width),
-            shape_of(38 * rows, width),
-        ],
-        name="sections",
-    )(right_side, pivot_inverse, lower_blocks, upper_blocks, active_cells)
-    all_matrices = lax.all_gather(matrices, "layer", axis=0, tiled=False)
-    slot_block, slot_source, slot_target = call(
-        functools.partial(routing_kernel, peers),
-        [
+            shape_of(27 * rows, width),
             shape_of(3, 3, slots, width),
             shape_of(slots, width, kind=jnp.int32),
             shape_of(slots, width),
         ],
-        [
+        [pltpu.VMEM(operand.shape, operand.dtype) for operand in operands]
+        + [
             pltpu.VMEM((peers * link_rows, width), BF16),
             pltpu.VMEM((13 * slots, width), F32),
+            pltpu.VMEM((3, link_rows, width), jnp.int32),
+            pltpu.SemaphoreType.DMA((len(operands),)),
         ],
-        name="routing",
-    )(
-        link_from.reshape(link_rows, width),
-        link_owner.reshape(link_rows, width),
-        link_target.reshape(link_rows, width),
-        link_blocks.reshape(3, 3, link_rows, width),
-    )
+        name="setup",
+        inputs=[hbm] * len(operands),
+    )(*operands)
+    turned = [turn(following, 1)] + [turn(edge, by) for by in range(2, sections)]
+    all_matrices = lax.all_gather(matrices, "layer", axis=0, tiled=False)
 
     target = None
-    sums = jnp.zeros((8, width), F32)
+    sums = jnp.zeros((8, 128), F32)
     earlier = []
     zs = []
     for step in range(ITERS):
         last = step == ITERS - 1
-        edges = lax.all_gather(edge, "layer", axis=0, tiled=False)
+        scratch = [
+            pltpu.VMEM((sections, 3, rows, width), F32),
+            pltpu.VMEM((sections, 3, rows, width), F32),
+            pltpu.VMEM((2, 16, width), F32),
+            pltpu.VMEM((3, layers * rows, width), F32),
+        ]
+        if step == 0:
+            edges = edge
+            scratch.append(pltpu.VMEM((sections, 6 * rows, width), F32))
+        else:
+            edges = lax.all_gather(edge, "layer", axis=0, tiled=False)
         solved, layer_sides, sent = call(
             functools.partial(couple_kernel, step == 0, sections),
-            [field, shape_of(2, 3, rows, width), shape_of(peers, sent_rows, width)],
             [
-                pltpu.VMEM((sections, 3, rows, width), F32),
-                pltpu.VMEM((sections, 3, rows, width), F32),
-                pltpu.VMEM((2, 16, width), F32),
-                pltpu.VMEM((3, layers * rows, width), F32),
+                field,
+                shape_of(2, 3, rows, width),
+                shape_of(peers, 1, first_width if step == 0 else sent_width),
             ],
+            scratch,
             name="couple",
         )(
-            edges, all_matrices, alone, from_above, from_below, active_cells,
+            *turned, edges, all_matrices, alone, from_above, from_below, active_cells,
             slot_block, slot_source, slot_target,
         )
         got = lax.all_to_all(sent, "areal", split_axis=0, concat_axis=0, tiled=True)
@@ -658,18 +754,17 @@
             operands.append(sums)
             for group in earlier:
                 operands += list(group)
-        history = shape_of(8, width)
+        history = shape_of(8, 128)
         if step == 0:
             outs = [field, edge_shape, field]
         elif last:
-            outs = [field, field, shape_of(peers * sections, 1, width), history]
+            outs = [field, field, shape_of(peers * sections, 1, 128), history]
         else:
             outs = [field, field, field, edge_shape, field, history]
         results = call(
             functools.partial(operate_kernel, step),
             outs,
             [
-                pltpu.VMEM((8, 128), F32),
                 pltpu.VMEM((3 * PARTS * layers * rows, width), F32),
             ],
             name="operate",

time: 150 us -> 128 us (0.85)
  between operations: 14.2 us -> 0.75 us
  waiting for transfers between devices: 6.23 us -> 0.01 us
  other arithmetic: 4.21 us -> 0 us
  starting transfers between devices: 0.04 us -> 3.25 us
  blocking collectives: 88.5 us -> 86.5 us
    all_gather x0 -> x1, blocking collectives: none -> 10.1 us  [local(): all_matrices = lax.all_gather(matrices, 'layer', axis=0, tiled=False)]
    all_gather x4 -> x3, blocking collectives: 25.4 us -> 17.2 us  [local(): edges = lax.all_gather(edge, 'layer', axis=0, tiled=False)]
    all_gather x1 -> x0, waiting for transfers between devices: 6.22 us -> none  [local(): all_matrices = lax.all_gather(matrices, 'layer', axis=0, tiled=False)]
    unnamed x3 -> x0, other arithmetic: 4.21 us -> none
    all_to_all x4, blocking collectives: 53.4 us -> 49.2 us  [local(): got = lax.all_to_all(sent, 'areal', split_axis=0, concat_axis=0, tiled=True)]
    ppermute x0 -> x3, starting transfers between devices: none -> 3.25 us  [turn(): lax.ppermute(array, 'layer', [(i, (i + by) % count) for i in range(count)])]
    unnamed x29 -> x28, local copies, waits for them, and re-layouts: 6.21 us -> 7.45 us
    pallas_call x6 -> x5, Pallas kernels: 18.5 us -> 18.8 us  [the longest x4 16.1 us: local(): call(functools.partial(operate_kernel, step), outs, [pltpu.VMEM((3 * PART...]
  transfers between devices with their start and end apart: 1 -> 3, of which waited for: 1 -> 0; matrix products, arithmetic and copies ran while one was open for 4% -> 0% of each run, Pallas kernels for 1% -> 0%
where the time goes in v2:
time: 128 us; the launch traced here: 127 us
  blocking collectives  86.5 us (68%)
  Pallas kernels  28.3 us (22%)
  local copies, waits for them, and re-layouts  8.11 us (6%)
  starting transfers between devices  3.25 us (3%)
    all_to_all x4, blocking collectives, local(): got = lax.all_to_all(sent, 'areal', split_axis=0, concat_axis=0, tiled=True)  49.2 us
    all_gather x3, blocking collectives, local(): edges = lax.all_gather(edge, 'layer', axis=0, tiled=False)  17.2 us
    pallas_call x4, Pallas kernels, local(): call(functools.partial(operate_kernel, step), outs, [pltpu.VMEM((3 * PART...  16.1 us
    all_gather x1, blocking collectives, local(): all_matrices = lax.all_gather(matrices, 'layer', axis=0, tiled=False)  10.1 us
    all_to_all x1, blocking collectives, local(): lax.all_to_all(dots, ('areal', 'layer'), split_axis=0, concat_axis=0, til...  9.95 us
    unnamed x28, local copies, waits for them, and re-layouts  7.45 us
    pallas_call x4, Pallas kernels, local(): call(functools.partial(couple_kernel, step == 0, sections), [field, shape...  7.41 us
    ppermute x3, starting transfers between devices, turn(): lax.ppermute(array, 'layer', [(i, (i + by) % count) for i in range(count)])  3.25 us
  transfers between devices with their start and end apart: 3, of which 0 were waited for; matrix products, arithmetic and copies ran while one was open for 0% of the time, Pallas kernels for 0%

profile of v2, /device:TPU:0, one launch (start us, length us, event | category | flops | bytes accessed | tf_op | source)
XLA Modules:
  0.0 126.9 jit_solution(14694443362857078081)
XLA Ops:
  0.6 0.0 copy-start.1
  0.6 0.7 copy-done.1
  1.4 0.0 copy-start.3
  1.4 0.9 copy-done.3
  2.3 0.0 copy-start.6
  2.3 0.9 copy-done.6
  3.2 0.9 copy-done.8
  4.1 0.9 copy-done.9
  5.0 0.9 copy-done.10
  5.9 0.7 copy-done.11
  6.6 0.7 copy-done.12
  7.3 0.7 copy-done.13
  8.1 2.7 %setup.1 = (f32[56,256]{1,0:T(8,128)S(1)}, f32[128,256]{1,0:T(8,128)S(1)}, f32[3,4,8,256]{3,2,1,0:T(8,128)S(1)}, f32[3,3,4,8,256]{4,3,2,1,0:T(8,128)S(1)}, f32[3...) custom-call(f32[3,4,8,256]{3,2,1,0:T(8,128)S(1)} %copy-done.3, ...), custom_call_target="tpu_custom_call" | custom-call | flops 4194304 | bytes 1048576 | tf_op jit(solution)/shard_map/setup/pallas_call | solution.py:690
  10.8 2.4 %collective-permute-start.2 = (f32[56,256]{1,0:T(8,128)S(1)}, f32[56,256]{1,0:T(8,128)S(1)}, u32[]{:S(2)}, u32[]{:S(2)}) collective-permute-start(f32[56,256]{1,0:T(8,128)S(1)} %get-tuple-element.42.refs_3_), channel_id=1, source_target_pairs={{0,3},{1,0},{2,1},{3,2},{4,7},{5,4},{6,5},{7,6},{8,11},{9,8},{10,9... | collective-permute-start | bytes 172040 | tf_op jit(solution)/shard_map/ppermute | solution.py:642
  13.2 0.7 collective-permute-start.1
  13.9 0.2 collective-permute-start
  14.0 10.1 %all-gather = f32[864,256]{1,0:T(8,128)S(1)} all-gather(f32[216,256]{1,0:T(8,128)S(1)} %get-tuple-element.43), channel_id=2, replica_groups=mesh['areal'=8,'layer'=4] {'layer'}, dimensions={0}, use_global_device_ids=true | all-gather | bytes 1105920 | tf_op jit(solution)/shard_map/all_gather | solution.py:714
  24.1 0.0 collective-permute-done.2.refs_2_
  24.1 0.0 collective-permute-done.1.refs_1_
  24.1 0.0 collective-permute-done.refs_0_
  24.1 0.0 copy-start
  24.1 1.9 %couple.4 = (f32[3,4,8,256]{3,2,1,0:T(8,128)S(1)}, f32[2,3,8,256]{3,2,1,0:T(8,128)S(1)}, f32[8,1,7168]{2,1,0:T(1,128)S(1)}) custom-call(f32[128,256]{1,0:T(8,128)S(1)} %collective-permute-done.refs_0_, f32[56,256]{1,0:T(8,128)S(1)} %collective-permute-done.1.refs_1_, f32[56,256]{1,0:T(8,128)S(1)} %collective-permute-done.2.refs_2_, ...), custom_call_target="tpu_custom_call" | custom-call | flops 4194304 | bytes 1048576 | tf_op jit(solution)/shard_map/couple/pallas_call | solution.py:733
  26.0 0.0 copy-start.4
  26.0 0.0 copy-start.5
  26.0 0.0 copy-start.7
  26.0 14.6 %all_to_all.25.refs_0_.refs_1_ = f32[8,1,7168]{2,1,0:T(1,128)S(1)} all-to-all(f32[8,1,7168]{2,1,0:T(1,128)S(1)} %get-tuple-element.50), channel_id=1, replica_groups=mesh['areal'=8,'layer'=4] {'areal'}, dimensions={0} | all-to-all | bytes 458752 | tf_op jit(solution)/shard_map/all_to_all | solution.py:746
  40.6 0.0 copy-done
  40.6 0.0 copy-done.4
  40.6 0.0 copy-done.5
  40.6 0.0 copy-done.7
  40.6 3.5 %operate.4 = (f32[3,4,8,256]{3,2,1,0:T(8,128)S(1)}, f32[56,256]{1,0:T(8,128)S(1)}, f32[3,4,8,256]{3,2,1,0:T(8,128)S(1)}) custom-call(f32[8,1,7168]{2,1,0:T(1,128)S(1)} %all_to_all.25.refs_0_.refs_1_, f32[8,1,7168]{2,1,0:T(1,128)S(1)} %all_to_all.25.refs_0_.refs_1_, f32[3,4,8,256]{3,2,1,0:T(8,128)S(1)} %get-tuple-element.51.refs_2_.refs_12_.refs_9_.z0_ref, ...), custom_call_target="tpu_custom_call" | custom-call | flops 4194304 | bytes 1048576 | tf_op jit(solution)/shard_map/operate/pallas_call | solution.py:764
  44.1 5.7 %all-gather.1 = f32[224,256]{1,0:T(8,128)S(1)} all-gather(f32[56,256]{1,0:T(8,128)S(1)} %get-tuple-element.53), channel_id=3, replica_groups=mesh['areal'=8,'layer'=4] {'layer'}, dimensions={0}, use_global_device_ids=true | all-gather | bytes 286720 | tf_op jit(solution)/shard_map/all_gather | solution.py:732
  49.8 1.8 %couple.5 = (f32[3,4,8,256]{3,2,1,0:T(8,128)S(1)}, f32[2,3,8,256]{3,2,1,0:T(8,128)S(1)}, f32[8,1,6272]{2,1,0:T(1,128)S(1)}) custom-call(f32[128,256]{1,0:T(8,128)S(1)} %collective-permute-done.refs_0_, f32[56,256]{1,0:T(8,128)S(1)} %collective-permute-done.1.refs_1_, f32[56,256]{1,0:T(8,128)S(1)} %collective-permute-done.2.refs_2_, ...), custom_call_target="tpu_custom_call" | custom-call | flops 4194304 | bytes 1048576 | tf_op jit(solution)/shard_map/couple/pallas_call | solution.py:733
  51.6 11.7 %all_to_all.26.refs_0_ = f32[8,1,6272]{2,1,0:T(1,128)S(1)} all-to-all(f32[8,1,6272]{2,1,0:T(1,128)S(1)} %get-tuple-element.55), channel_id=1, replica_groups=mesh['areal'=8,'layer'=4] {'areal'}, dimensions={0} | all-to-all | bytes 401408 | tf_op jit(solution)/shard_map/all_to_all | solution.py:746
  63.3 3.7 %operate.5 = (f32[3,4,8,256]{3,2,1,0:T(8,128)S(1)}, f32[3,4,8,256]{3,2,1,0:T(8,128)S(1)}, f32[3,4,8,256]{3,2,1,0:T(8,128)S(1)}, f32[56,256]{1,0:T(8,128)S(1)}, f...) custom-call(f32[8,1,6272]{2,1,0:T(1,128)S(1)} %all_to_all.26.refs_0_, f32[8,1,7168]{2,1,0:T(1,128)S(1)} %all_to_all.25.refs_0_.refs_1_, ...), custom_call_target="tpu_custom_call" | custom-call | flops 4194304 | bytes 1048576 | tf_op jit(solution)/shard_map/operate/pallas_call | solution.py:764
  67.0 5.7 %all-gather.2 = f32[224,256]{1,0:T(8,128)S(1)} all-gather(f32[56,256]{1,0:T(8,128)S(1)} %get-tuple-element.59), channel_id=4, replica_groups=mesh['areal'=8,'layer'=4] {'layer'}, dimensions={0}, use_global_device_ids=true | all-gather | bytes 286720 | tf_op jit(solution)/shard_map/all_gather | solution.py:732
  72.7 1.8 %couple.6 = (f32[3,4,8,256]{3,2,1,0:T(8,128)S(1)}, f32[2,3,8,256]{3,2,1,0:T(8,128)S(1)}, f32[8,1,6272]{2,1,0:T(1,128)S(1)}) custom-call(f32[128,256]{1,0:T(8,128)S(1)} %collective-permute-done.refs_0_, f32[56,256]{1,0:T(8,128)S(1)} %collective-permute-done.1.refs_1_, f32[56,256]{1,0:T(8,128)S(1)} %collective-permute-done.2.refs_2_, ...), custom_call_target="tpu_custom_call" | custom-call | flops 4194304 | bytes 1048576 | tf_op jit(solution)/shard_map/couple/pallas_call | solution.py:733
  74.6 11.5 %all_to_all.27.refs_0_ = f32[8,1,6272]{2,1,0:T(1,128)S(1)} all-to-all(f32[8,1,6272]{2,1,0:T(1,128)S(1)} %get-tuple-element.61), channel_id=1, replica_groups=mesh['areal'=8,'layer'=4] {'areal'}, dimensions={0} | all-to-all | bytes 401408 | tf_op jit(solution)/shard_map/all_to_all | solution.py:746
  86.1 4.0 %operate.6 = (f32[3,4,8,256]{3,2,1,0:T(8,128)S(1)}, f32[3,4,8,256]{3,2,1,0:T(8,128)S(1)}, f32[3,4,8,256]{3,2,1,0:T(8,128)S(1)}, f32[56,256]{1,0:T(8,128)S(1)}, f...) custom-call(f32[8,1,6272]{2,1,0:T(1,128)S(1)} %all_to_all.27.refs_0_, f32[8,1,7168]{2,1,0:T(1,128)S(1)} %all_to_all.25.refs_0_.refs_1_, ...), custom_call_target="tpu_custom_call" | custom-call | flops 4194304 | bytes 1048576 | tf_op jit(solution)/shard_map/operate/pallas_call | solution.py:764
  90.1 5.9 %all-gather.3 = f32[224,256]{1,0:T(8,128)S(1)} all-gather(f32[56,256]{1,0:T(8,128)S(1)} %get-tuple-element.68), channel_id=5, replica_groups=mesh['areal'=8,'layer'=4] {'layer'}, dimensions={0}, use_global_device_ids=true | all-gather | bytes 286720 | tf_op jit(solution)/shard_map/all_gather | solution.py:732
  96.0 1.8 %couple.7 = (f32[3,4,8,256]{3,2,1,0:T(8,128)S(1)}, f32[2,3,8,256]{3,2,1,0:T(8,128)S(1)}, f32[8,1,6272]{2,1,0:T(1,128)S(1)}) custom-call(f32[128,256]{1,0:T(8,128)S(1)} %collective-permute-done.refs_0_, f32[56,256]{1,0:T(8,128)S(1)} %collective-permute-done.1.refs_1_, f32[56,256]{1,0:T(8,128)S(1)} %collective-permute-done.2.refs_2_, ...), custom_call_target="tpu_custom_call" | custom-call | flops 4194304 | bytes 1048576 | tf_op jit(solution)/shard_map/couple/pallas_call | solution.py:733
  97.8 0.0 copy-start.2
  97.8 11.5 %all_to_all.28.refs_0_ = f32[8,1,6272]{2,1,0:T(1,128)S(1)} all-to-all(f32[8,1,6272]{2,1,0:T(1,128)S(1)} %get-tuple-element.70), channel_id=1, replica_groups=mesh['areal'=8,'layer'=4] {'areal'}, dimensions={0} | all-to-all | bytes 401408 | tf_op jit(solution)/shard_map/all_to_all | solution.py:746
  109.3 0.0 copy-done.2
  109.3 4.9 %operate.7 = (f32[3,4,8,256]{3,2,1,0:T(8,128)}, f32[3,4,8,256]{3,2,1,0:T(8,128)S(1)}, f32[32,1,128]{2,1,0:T(1,128)S(1)}, f32[8,128]{1,0:T(8,128)S(1)}) custom-call(f32[8,1,6272]{2,1,0:T(1,128)S(1)} %all_to_all.28.refs_0_, f32[8,1,7168]{2,1,0:T(1,128)S(1)} %all_to_all.25.refs_0_.refs_1_, f32[3,4,8,256]{3,2,1,0:T(8,128)S(1)} %get-tuple-element.71.refs_2_, ...), custom_call_target="tpu_custom_call" | custom-call | flops 4194304 | bytes 1048576 | tf_op jit(solution)/shard_map/operate/pallas_call | solution.py:764
  114.2 9.9 %all_to_all.29.dots_ref = f32[32,1,128]{2,1,0:T(1,128)S(1)} all-to-all(f32[32,1,128]{2,1,0:T(1,128)S(1)} %get-tuple-element.77), channel_id=1, replica_groups=mesh['areal'=8,'layer'=4] {'areal','layer'}, dimensions={0} | all-to-all | bytes 32768 | tf_op jit(solution)/shard_map/all_to_all | solution.py:783
  124.2 2.1 %finish.1 = (f32[3,4,8,256]{3,2,1,0:T(8,128)}, f32[5,4]{1,0:T(8,128)S(1)}) custom-call(f32[32,1,128]{2,1,0:T(1,128)S(1)} %all_to_all.29.dots_ref, f32[8,128]{1,0:T(8,128)S(1)} %get-tuple-element.78.sums_ref, f32[3,4,8,256]{3,2,1,0:T(8,128)S(1)} %get-tuple-element.51.refs_2_.refs_12_.refs_9_.z0_ref, ...), custom_call_target="tpu_custom_call" | custom-call | flops 4194304 | bytes 1048576 | tf_op jit(solution)/shard_map/finish/pallas_call | solution.py:784
  126.3 0.7 copy.13
  (7 shorter events, 0.0 us)
Async XLA Ops:
  0.6 0.8 copy-start.1
  1.4 0.9 copy-start.3
  2.3 0.9 copy-start.6
  3.2 0.9 copy-start.8
  4.1 0.9 copy-start.9
  5.0 0.9 copy-start.10
  5.9 0.7 copy-start.11
  6.6 0.7 copy-start.12
  7.3 0.7 copy-start.13
  10.8 13.3 %collective-permute-start.2 = (f32[56,256]{1,0:T(8,128)S(1)}, f32[56,256]{1,0:T(8,128)S(1)}, u32[]{:S(2)}, u32[]{:S(2)}) collective-permute-start(f32[56,256]{1,0:T(8,128)S(1)} %get-tuple-element.42.refs_3_), channel_id=1, source_target_pairs={{0,3},{1,0},{2,1},{3,2},{4,7},{5,4},{6,5},{7,6},{8,11},{9,8},{10,9... | collective-permute-start | bytes 172040 | tf_op jit(solution)/shard_map/ppermute | solution.py:642
  13.2 10.9 %collective-permute-start.1 = (f32[56,256]{1,0:T(8,128)S(1)}, f32[56,256]{1,0:T(8,128)S(1)}, u32[]{:S(2)}, u32[]{:S(2)}) collective-permute-start(f32[56,256]{1,0:T(8,128)S(1)} %get-tuple-element.42.refs_3_), channel_id=1, source_target_pairs={{0,2},{1,3},{2,0},{3,1},{4,6},{5,7},{6,4},{7,5},{8,10},{9,11},{10,... | collective-permute-start | bytes 172040 | tf_op jit(solution)/shard_map/ppermute | solution.py:642
  13.9 10.2 %collective-permute-start = (f32[128,256]{1,0:T(8,128)S(1)}, f32[128,256]{1,0:T(8,128)S(1)}, u32[]{:S(2)}, u32[]{:S(2)}) collective-permute-start(f32[128,256]{1,0:T(8,128)S(1)} %get-tuple-element.41), channel_id=1, source_target_pairs={{0,1},{1,2},{2,3},{3,0},{4,5},{5,6},{6,7},{7,4},{8,9},{9,10},{10,1... | collective-permute-start | bytes 393224 | tf_op jit(solution)/shard_map/ppermute | solution.py:642
  24.1 16.5 %copy-start = (bf16[6,3,3,4,8,256]{5,4,3,2,1,0:T(8,128)(2,1)S(1)}, bf16[6,3,3,4,8,256]{5,4,3,2,1,0:T(8,128)(2,1)}, u32[]{:S(2)}) copy-start(bf16[6,3,3,4,8,256]{5,4,3,2,1,0:T(8,128)(2,1)} %refs_5_.7) | copy-start | bytes 2654212
  26.0 14.6 %copy-start.4 = (f32[3,4,8,256]{3,2,1,0:T(8,128)S(1)}, f32[3,4,8,256]{3,2,1,0:T(8,128)}, u32[]{:S(2)}) copy-start(f32[3,4,8,256]{3,2,1,0:T(8,128)} %refs_7_.7) | copy-start | bytes 294916
  26.0 14.6 %copy-start.5 = (bf16[3,3,4,8,256]{4,3,2,1,0:T(8,128)(2,1)S(1)}, bf16[3,3,4,8,256]{4,3,2,1,0:T(8,128)(2,1)}, u32[]{:S(2)}) copy-start(bf16[3,3,4,8,256]{4,3,2,1,0:T(8,128)(2,1)} %refs_4_.7) | copy-start | bytes 442372
  26.0 14.6 %copy-start.7 = (bf16[3,3,4,8,256]{4,3,2,1,0:T(8,128)(2,1)S(1)}, bf16[3,3,4,8,256]{4,3,2,1,0:T(8,128)(2,1)}, u32[]{:S(2)}) copy-start(bf16[3,3,4,8,256]{4,3,2,1,0:T(8,128)(2,1)} %refs_7_.6) | copy-start | bytes 442372
  97.8 11.5 %copy-start.2 = (s32[4,8,256]{2,1,0:T(8,128)S(1)}, s32[4,8,256]{2,1,0:T(8,128)}, u32[]{:S(2)}) copy-start(s32[4,8,256]{2,1,0:T(8,128)} %refs_6_.7) | copy-start | bytes 98308

commit v3 on v2

--- a/solution.py
+++ b/solution.py
@@ -16,7 +16,7 @@
 VMEM = pl.BlockSpec(memory_space=pltpu.VMEM)
 
 
-def call(kernel, outs, scratch=(), name=None, inputs=None, flops=1 << 22, moved=1 << 20):
+def call(kernel, outs, scratch=(), name=None, inputs=None, limit=20, flops=1 << 22, moved=1 << 20):
     many = isinstance(outs, (list, tuple))
     where = {} if inputs is None else {"in_specs": inputs}
     return pl.pallas_call(
@@ -25,7 +25,7 @@
         **where,
         out_specs=[VMEM] * len(outs) if many else VMEM,
         scratch_shapes=list(scratch),
-        compiler_params=pltpu.CompilerParams(vmem_limit_bytes=40 << 20),
+        compiler_params=pltpu.CompilerParams(vmem_limit_bytes=limit << 20),
         cost_estimate=pl.CostEstimate(flops=flops, bytes_accessed=moved, transcendentals=0),
         name=name,
     )
@@ -375,7 +375,10 @@
 
 
 def weights_of(sums, upto):
-    value = lambda step, at: sums[step : step + 1, at : at + 1]
+    def value(step, at):
+        row = jnp.broadcast_to(sums[step : step + 1], (8, 128))
+        return jnp.take_along_axis(row, jnp.full((8, 128), at, jnp.int32), axis=1)
+
     squared = value(0, 0)
     beta = jnp.sqrt(squared + TINY)
     unscale = 1.0 / beta
@@ -413,8 +416,11 @@
 
 def operate_kernel(step, *refs):
     last = step == ITERS - 1
-    (got_ref, target_ref, solved_ref, layer_ref, diag_ref, coupling_ref, active_ref) = refs[:7]
-    at = 7
+    got_ref, solved_ref, layer_ref, diag_ref, coupling_ref, active_ref = refs[:6]
+    at = 6
+    if step > 0:
+        hot_row_ref, hot_column_ref = refs[6:8]
+        at = 8
     if not last:
         pivot_ref, lower_ref, upper_ref = refs[at : at + 3]
         at += 3
@@ -438,32 +444,46 @@
     a = lax.axis_index("areal")
     total_ref = outs[-1]
     outs = outs[:-1]
-
-    row_number = lax.broadcasted_iota(jnp.int32, (cells, width), 0)
-    column_number = lax.broadcasted_iota(jnp.int32, (width, width), 0)
+    if step == 0:
+        lines_ref = outs[-1]
+        hot_row_ref, hot_column_ref = outs[-3:-1]
+        outs = outs[:-3]
+
+    capacity = per_peer * width
+    if step == 0:
+        for peer in range(peers):
+            for i in range(per_peer):
+                at = peer * per_peer + i
+                lines_ref[at : at + 1] = got_ref[
+                    peer, 0:1, ending + i * width : ending + (i + 1) * width
+                ]
+        where = lines_ref[...].astype(jnp.int32)
+        upright = jnp.transpose(wide(where % width))
+        upper = where // width
+        row_number = lax.broadcasted_iota(jnp.int32, (cells, width), 0)
+        column_number = wide(lax.broadcasted_iota(jnp.int32, (width, width), 1))
+        for peer in range(peers):
+            for i in range(per_peer):
+                at = peer * per_peer + i
+                hot_column_ref[peer, i * width : (i + 1) * width] = jnp.where(
+                    column_number == upright[:, at : at + 1], 1.0, 0.0
+                ).astype(BF16)
+                hot_row_ref[peer, :, i * width : (i + 1) * width] = jnp.where(
+                    row_number == upper[at : at + 1], 1.0, 0.0
+                ).astype(BF16)
     total_ref[...] = jnp.zeros(total_ref.shape, F32)
 
     def from_peer(peer, carry):
-        lefts, rights = [], []
-        for i in range(per_peer):
-            where = target_ref[
-                peer, 0:1, ending + i * width : ending + (i + 1) * width
-            ].astype(jnp.int32)
-            in_row = row_number == where // width
-            rights.append(jnp.where(column_number == where % width, 1.0, 0.0).astype(BF16))
-            pieces = []
-            for c in range(3):
-                start = (c * per_peer + i) * width
-                rest = got_ref[peer, 0:1, start : start + width]
-                for part in range(PARTS):
-                    piece = rest.astype(BF16).astype(F32)
-                    rest = rest - piece
-                    pieces.append(jnp.where(in_row, piece, 0.0).astype(BF16))
-            lefts.append(jnp.concatenate(pieces, axis=0))
-        left = jnp.concatenate(lefts, axis=1)
-        right = jnp.concatenate(rights, axis=1)
-        total_ref[...] += lax.dot_general(
-            left, right, (((1,), (1,)), ((), ())), preferred_element_type=F32
+        hot = hot_row_ref[peer]
+        pieces = []
+        for c in range(3):
+            rest = got_ref[peer, 0:1, c * capacity : (c + 1) * capacity]
+            for part in range(PARTS):
+                piece = rest.astype(BF16)
+                rest = rest - wide(piece)
+                pieces.append(hot * jnp.broadcast_to(piece, hot.shape))
+        total_ref[...] += jnp.dot(
+            jnp.concatenate(pieces, axis=0), hot_column_ref[peer], preferred_element_type=F32
         )
         return carry
 
@@ -529,7 +549,7 @@
         beta, unscale, columns, lengths = weights_of(sums, step)
         weights = columns[-1]
         inverse = 1.0 / lengths[-1]
-        spread = lambda value: jnp.broadcast_to(value, (rows, width))
+        spread = lambda value: jnp.concatenate([value] * (width // 128), axis=1)
         lead = spread(inverse * unscale if step == 1 else inverse)
         factors = [spread(weights[i] * inverse * (unscale if i == 0 else 1.0)) for i in range(step)]
         new = []
@@ -594,14 +614,13 @@
     history_row = lax.broadcasted_iota(jnp.int32, sums_ref.shape, 0)
     sums = jnp.where(history_row == ITERS - 1, fresh, sums_ref[...])
     beta, unscale, columns, lengths = weights_of(sums, ITERS)
-    shape = hessenberg_ref.shape
-    row_at = lax.broadcasted_iota(jnp.int32, shape, 0)
-    column_at = lax.broadcasted_iota(jnp.int32, shape, 1)
-    table = jnp.zeros(shape, F32)
+    row_at = lax.broadcasted_iota(jnp.int32, (8, 128), 0)
+    column_at = lax.broadcasted_iota(jnp.int32, (8, 128), 1)
+    table = jnp.zeros((8, 128), F32)
     for j in range(ITERS):
         for i, weight in enumerate(columns[j] + [lengths[j]]):
             table = jnp.where((row_at == i) & (column_at == j), weight, table)
-    hessenberg_ref[...] = table
+    hessenberg_ref[...] = table[0 : hessenberg_ref.shape[0], 0 : hessenberg_ref.shape[1]]
     goal = [beta]
     triangle = []
     rotations = []
@@ -626,7 +645,7 @@
             partial = partial - triangle[j][i] * answer[j]
         answer[i] = partial / triangle[i][i]
     factors = [
-        jnp.broadcast_to(answer[j] * unscale if j == 0 else answer[j], (rows, width))
+        jnp.concatenate([answer[j] * unscale if j == 0 else answer[j]] * (width // 128), axis=1)
         for j in range(ITERS)
     ]
     for c in range(3):
@@ -709,11 +728,11 @@
         ],
         name="setup",
         inputs=[hbm] * len(operands),
-    )(*operands)
+        limit=16,
+    )(*[pltpu.with_memory_space_constraint(operand, pltpu.HBM) for operand in operands])
     turned = [turn(following, 1)] + [turn(edge, by) for by in range(2, sections)]
     all_matrices = lax.all_gather(matrices, "layer", axis=0, tiled=False)
 
-    target = None
     sums = jnp.zeros((8, 128), F32)
     earlier = []
     zs = []
@@ -744,9 +763,9 @@
             slot_block, slot_source, slot_target,
         )
         got = lax.all_to_all(sent, "areal", split_axis=0, concat_axis=0, tiled=True)
-        if step == 0:
-            target = got
-        operands = [got, target, solved, layer_sides, diag_blocks, couplings, active_cells]
+        operands = [got, solved, layer_sides, diag_blocks, couplings, active_cells]
+        if step > 0:
+            operands += [hot_row, hot_column]
         if not last:
             operands += [pivot_inverse, lower_blocks, upper_blocks]
         operands.append(right_side)
@@ -756,7 +775,13 @@
                 operands += list(group)
         history = shape_of(8, 128)
         if step == 0:
-            outs = [field, edge_shape, field]
+            outs = [
+                field,
+                edge_shape,
+                field,
+                shape_of(peers, layers * rows, capacity, kind=BF16),
+                shape_of(peers, capacity, width, kind=BF16),
+            ]
         elif last:
             outs = [field, field, shape_of(peers * sections, 1, 128), history]
         else:
@@ -764,13 +789,12 @@
         results = call(
             functools.partial(operate_kernel, step),
             outs,
-            [
-                pltpu.VMEM((3 * PARTS * layers * rows, width), F32),
-            ],
+            ([pltpu.VMEM((slots, width), F32)] if step == 0 else [])
+            + [pltpu.VMEM((3 * PARTS * layers * rows, width), F32)],
             name="operate",
         )(*operands)
         if step == 0:
-            applied, edge, alone = results
+            applied, edge, alone, hot_row, hot_column = results
             earlier.append((solved, applied))
             zs.append(solved)
         elif last:

time: 128 us -> 118 us (0.922)
  local copies, waits for them, and re-layouts: 8.11 us -> 1.45 us
  Pallas kernels: 28.3 us -> 26.1 us
    unnamed x28 -> x16, local copies, waits for them, and re-layouts: 7.45 us -> 0.79 us
    pallas_call x4, Pallas kernels: 16.1 us -> 14.8 us  [local(): call(functools.partial(operate_kernel, step), outs, ([pltpu.VMEM((slots,...]
where the time goes in v3:
time: 118 us
  blocking collectives  86.4 us (73%)
  Pallas kernels  26.1 us (22%)
  starting transfers between devices  3.23 us (3%)
  local copies, waits for them, and re-layouts  1.45 us (1%)
    all_to_all x4, blocking collectives, local(): got = lax.all_to_all(sent, 'areal', split_axis=0, concat_axis=0, tiled=True)  49.1 us
    all_gather x3, blocking collectives, local(): edges = lax.all_gather(edge, 'layer', axis=0, tiled=False)  17.3 us
    pallas_call x4, Pallas kernels, local(): call(functools.partial(operate_kernel, step), outs, ([pltpu.VMEM((slots,...  14.8 us
    all_gather x1, blocking collectives, local(): all_matrices = lax.all_gather(matrices, 'layer', axis=0, tiled=False)  10.1 us
    all_to_all x1, blocking collectives, local(): lax.all_to_all(dots, ('areal', 'layer'), split_axis=0, concat_axis=0, til...  10 us
    pallas_call x4, Pallas kernels, local(): call(functools.partial(couple_kernel, step == 0, sections), [field, shape...  7.41 us
    ppermute x3, starting transfers between devices, turn(): lax.ppermute(array, 'layer', [(i, (i + by) % count) for i in range(count)])  3.23 us
    pallas_call x1, Pallas kernels, local(): call(functools.partial(setup_kernel, peers), [edge_shape, shape_of(16 * r...  3.05 us
  transfers between devices with their start and end apart: 3, of which 0 were waited for; matrix products, arithmetic and copies ran while one was open for 0% of the time, Pallas kernels for 0%

profile of v3, /device:TPU:0, one launch (start us, length us, event | category | flops | bytes accessed | tf_op | source)
XLA Modules:
  0.0 118.0 jit_solution(6936146709935828558)
XLA Ops:
  0.6 0.0 copy-start.2
  0.6 0.0 copy-start.3
  0.7 0.0 copy-start.7
  0.7 0.0 copy-start.6
  0.7 0.0 copy-start.5
  0.7 0.0 copy-start
  0.7 0.0 copy-start.4
  0.7 3.1 %setup.1 = (f32[56,256]{1,0:T(8,128)S(1)}, f32[128,256]{1,0:T(8,128)S(1)}, f32[3,4,8,256]{3,2,1,0:T(8,128)S(1)}, f32[3,3,4,8,256]{4,3,2,1,0:T(8,128)S(1)}, f32[3...) custom-call(f32[3,4,8,256]{3,2,1,0:T(8,128)} %refs_8_.15, ...), custom_call_target="tpu_custom_call" | custom-call | flops 4194304 | bytes 1048576 | tf_op jit(solution)/shard_map/setup/pallas_call | solution.py:709
  3.8 2.4 %collective-permute-start.2 = (f32[56,256]{1,0:T(8,128)S(1)}, f32[56,256]{1,0:T(8,128)S(1)}, u32[]{:S(2)}, u32[]{:S(2)}) collective-permute-start(f32[56,256]{1,0:T(8,128)S(1)} %get-tuple-element.44.refs_3_), channel_id=1, source_target_pairs={{0,3},{1,0},{2,1},{3,2},{4,7},{5,4},{6,5},{7,6},{8,11},{9,8},{10,9... | collective-permute-start | bytes 172040 | tf_op jit(solution)/shard_map/ppermute | solution.py:661
  6.2 0.6 collective-permute-start.1
  6.8 0.2 collective-permute-start
  7.0 10.1 %all-gather = f32[864,256]{1,0:T(8,128)S(1)} all-gather(f32[216,256]{1,0:T(8,128)S(1)} %get-tuple-element.45), channel_id=2, replica_groups=mesh['areal'=8,'layer'=4] {'layer'}, dimensions={0}, use_global_device_ids=true | all-gather | bytes 1105920 | tf_op jit(solution)/shard_map/all_gather | solution.py:734
  17.1 0.0 collective-permute-done.2.refs_2_
  17.1 0.0 collective-permute-done.1.refs_1_
  17.1 0.0 collective-permute-done.refs_0_
  17.1 0.0 copy-start.1
  17.1 0.7 copy-done.1
  17.8 1.9 %couple.4 = (f32[3,4,8,256]{3,2,1,0:T(8,128)S(1)}, f32[2,3,8,256]{3,2,1,0:T(8,128)S(1)}, f32[8,1,7168]{2,1,0:T(1,128)S(1)}) custom-call(f32[128,256]{1,0:T(8,128)S(1)} %collective-permute-done.refs_0_, f32[56,256]{1,0:T(8,128)S(1)} %collective-permute-done.1.refs_1_, f32[56,256]{1,0:T(8,128)S(1)} %collective-permute-done.2.refs_2_, ...), custom_call_target="tpu_custom_call" | custom-call | flops 4194304 | bytes 1048576 | tf_op jit(solution)/shard_map/couple/pallas_call | solution.py:752
  19.7 14.4 %all_to_all.25.refs_0_ = f32[8,1,7168]{2,1,0:T(1,128)S(1)} all-to-all(f32[8,1,7168]{2,1,0:T(1,128)S(1)} %get-tuple-element.52), channel_id=1, replica_groups=mesh['areal'=8,'layer'=4] {'areal'}, dimensions={0} | all-to-all | bytes 458752 | tf_op jit(solution)/shard_map/all_to_all | solution.py:765
  34.1 0.0 copy-done.2
  34.1 0.0 copy-done.3
  34.1 0.0 copy-done.7
  34.2 0.0 copy-done.6
  34.2 0.0 copy-done.5
  34.2 0.0 copy-done
  34.2 0.0 copy-done.4
  34.2 4.6 %operate.4 = (f32[3,4,8,256]{3,2,1,0:T(8,128)S(1)}, f32[56,256]{1,0:T(8,128)S(1)}, f32[3,4,8,256]{3,2,1,0:T(8,128)S(1)}, bf16[8,32,1024]{2,1,0:T(8,128)(2,1)S(1)}, bf16[8,1024,256]{2,1,0:T(8,128)(2,1)S(1)}) custom-call(f32[8,1,7168]{2,1,0:T(1,128)S(1)} %all_to_all.25.refs_0_, f32[3,4,8,256]{3,2,1,0:T(8,128)S(1)} %get-tuple-element.53.refs_1_.refs_13_.refs_10_.z0_ref, ...), custom_call_target="tpu_custom_call" | custom-call | flops 4194304 | bytes 1048576 | tf_op jit(solution)/shard_map/operate/pallas_call | solution.py:789
  38.7 5.7 %all-gather.1 = f32[224,256]{1,0:T(8,128)S(1)} all-gather(f32[56,256]{1,0:T(8,128)S(1)} %get-tuple-element.55), channel_id=3, replica_groups=mesh['areal'=8,'layer'=4] {'layer'}, dimensions={0}, use_global_device_ids=true | all-gather | bytes 286720 | tf_op jit(solution)/shard_map/all_gather | solution.py:751
  44.4 1.9 %couple.5 = (f32[3,4,8,256]{3,2,1,0:T(8,128)S(1)}, f32[2,3,8,256]{3,2,1,0:T(8,128)S(1)}, f32[8,1,6272]{2,1,0:T(1,128)S(1)}) custom-call(f32[128,256]{1,0:T(8,128)S(1)} %collective-permute-done.refs_0_, f32[56,256]{1,0:T(8,128)S(1)} %collective-permute-done.1.refs_1_, f32[56,256]{1,0:T(8,128)S(1)} %collective-permute-done.2.refs_2_, ...), custom_call_target="tpu_custom_call" | custom-call | flops 4194304 | bytes 1048576 | tf_op jit(solution)/shard_map/couple/pallas_call | solution.py:752
  46.3 11.7 %all_to_all.26.refs_0_ = f32[8,1,6272]{2,1,0:T(1,128)S(1)} all-to-all(f32[8,1,6272]{2,1,0:T(1,128)S(1)} %get-tuple-element.57), channel_id=1, replica_groups=mesh['areal'=8,'layer'=4] {'areal'}, dimensions={0} | all-to-all | bytes 401408 | tf_op jit(solution)/shard_map/all_to_all | solution.py:765
  58.0 3.2 %operate.5 = (f32[3,4,8,256]{3,2,1,0:T(8,128)S(1)}, f32[3,4,8,256]{3,2,1,0:T(8,128)S(1)}, f32[3,4,8,256]{3,2,1,0:T(8,128)S(1)}, f32[56,256]{1,0:T(8,128)S(1)}, f...) custom-call(f32[8,1,6272]{2,1,0:T(1,128)S(1)} %all_to_all.26.refs_0_, f32[3,4,8,256]{3,2,1,0:T(8,128)S(1)} %get-tuple-element.58.refs_1_, ...), custom_call_target="tpu_custom_call" | custom-call | flops 4194304 | bytes 1048576 | tf_op jit(solution)/shard_map/operate/pallas_call | solution.py:789
  61.2 5.7 %all-gather.2 = f32[224,256]{1,0:T(8,128)S(1)} all-gather(f32[56,256]{1,0:T(8,128)S(1)} %get-tuple-element.63), channel_id=4, replica_groups=mesh['areal'=8,'layer'=4] {'layer'}, dimensions={0}, use_global_device_ids=true | all-gather | bytes 286720 | tf_op jit(solution)/shard_map/all_gather | solution.py:751
  66.9 1.8 %couple.6 = (f32[3,4,8,256]{3,2,1,0:T(8,128)S(1)}, f32[2,3,8,256]{3,2,1,0:T(8,128)S(1)}, f32[8,1,6272]{2,1,0:T(1,128)S(1)}) custom-call(f32[128,256]{1,0:T(8,128)S(1)} %collective-permute-done.refs_0_, f32[56,256]{1,0:T(8,128)S(1)} %collective-permute-done.1.refs_1_, f32[56,256]{1,0:T(8,128)S(1)} %collective-permute-done.2.refs_2_, ...), custom_call_target="tpu_custom_call" | custom-call | flops 4194304 | bytes 1048576 | tf_op jit(solution)/shard_map/couple/pallas_call | solution.py:752
  68.7 11.5 %all_to_all.27.refs_0_ = f32[8,1,6272]{2,1,0:T(1,128)S(1)} all-to-all(f32[8,1,6272]{2,1,0:T(1,128)S(1)} %get-tuple-element.65), channel_id=1, replica_groups=mesh['areal'=8,'layer'=4] {'areal'}, dimensions={0} | all-to-all | bytes 401408 | tf_op jit(solution)/shard_map/all_to_all | solution.py:765
  80.2 3.2 %operate.6 = (f32[3,4,8,256]{3,2,1,0:T(8,128)S(1)}, f32[3,4,8,256]{3,2,1,0:T(8,128)S(1)}, f32[3,4,8,256]{3,2,1,0:T(8,128)S(1)}, f32[56,256]{1,0:T(8,128)S(1)}, f...) custom-call(f32[8,1,6272]{2,1,0:T(1,128)S(1)} %all_to_all.27.refs_0_, f32[3,4,8,256]{3,2,1,0:T(8,128)S(1)} %get-tuple-element.66.refs_1_, ...), custom_call_target="tpu_custom_call" | custom-call | flops 4194304 | bytes 1048576 | tf_op jit(solution)/shard_map/operate/pallas_call | solution.py:789
  83.5 5.9 %all-gather.3 = f32[224,256]{1,0:T(8,128)S(1)} all-gather(f32[56,256]{1,0:T(8,128)S(1)} %get-tuple-element.72), channel_id=5, replica_groups=mesh['areal'=8,'layer'=4] {'layer'}, dimensions={0}, use_global_device_ids=true | all-gather | bytes 286720 | tf_op jit(solution)/shard_map/all_gather | solution.py:751
  89.3 1.9 %couple.7 = (f32[3,4,8,256]{3,2,1,0:T(8,128)S(1)}, f32[2,3,8,256]{3,2,1,0:T(8,128)S(1)}, f32[8,1,6272]{2,1,0:T(1,128)S(1)}) custom-call(f32[128,256]{1,0:T(8,128)S(1)} %collective-permute-done.refs_0_, f32[56,256]{1,0:T(8,128)S(1)} %collective-permute-done.1.refs_1_, f32[56,256]{1,0:T(8,128)S(1)} %collective-permute-done.2.refs_2_, ...), custom_call_target="tpu_custom_call" | custom-call | flops 4194304 | bytes 1048576 | tf_op jit(solution)/shard_map/couple/pallas_call | solution.py:752
  91.2 11.5 %all_to_all.28.refs_0_ = f32[8,1,6272]{2,1,0:T(1,128)S(1)} all-to-all(f32[8,1,6272]{2,1,0:T(1,128)S(1)} %get-tuple-element.74), channel_id=1, replica_groups=mesh['areal'=8,'layer'=4] {'areal'}, dimensions={0} | all-to-all | bytes 401408 | tf_op jit(solution)/shard_map/all_to_all | solution.py:765
  102.7 3.8 %operate.7 = (f32[3,4,8,256]{3,2,1,0:T(8,128)}, f32[3,4,8,256]{3,2,1,0:T(8,128)S(1)}, f32[32,1,128]{2,1,0:T(1,128)S(1)}, f32[8,128]{1,0:T(8,128)S(1)}) custom-call(f32[8,1,6272]{2,1,0:T(1,128)S(1)} %all_to_all.28.refs_0_, f32[3,4,8,256]{3,2,1,0:T(8,128)S(1)} %get-tuple-element.75.refs_1_, f32[2,3,8,256]{3,2,1,0:T(8,128)S(1)} %get-tuple-element.76.refs_2_, ...), custom_call_target="tpu_custom_call" | custom-call | flops 4194304 | bytes 1048576 | tf_op jit(solution)/shard_map/operate/pallas_call | solution.py:789
  106.5 10.0 %all_to_all.29.dots_ref = f32[32,1,128]{2,1,0:T(1,128)S(1)} all-to-all(f32[32,1,128]{2,1,0:T(1,128)S(1)} %get-tuple-element.81), channel_id=1, replica_groups=mesh['areal'=8,'layer'=4] {'areal','layer'}, dimensions={0} | all-to-all | bytes 32768 | tf_op jit(solution)/shard_map/all_to_all | solution.py:807
  116.5 0.9 finish.1
  117.4 0.7 copy.13
  (1 shorter events, 0.0 us)
Async XLA Ops:
  0.6 33.5 %copy-start.2 = (s32[4,8,256]{2,1,0:T(8,128)S(1)}, s32[4,8,256]{2,1,0:T(8,128)}, u32[]{:S(2)}) copy-start(s32[4,8,256]{2,1,0:T(8,128)} %refs_5_.7) | copy-start | bytes 98308
  0.6 33.5 %copy-start.3 = (f32[3,4,8,256]{3,2,1,0:T(8,128)S(1)}, f32[3,4,8,256]{3,2,1,0:T(8,128)}, u32[]{:S(2)}) copy-start(f32[3,4,8,256]{3,2,1,0:T(8,128)} %refs_8_.15) | copy-start | bytes 294916
  0.7 33.5 %copy-start.7 = (bf16[3,3,4,8,256]{4,3,2,1,0:T(8,128)(2,1)S(1)}, bf16[3,3,4,8,256]{4,3,2,1,0:T(8,128)(2,1)}, u32[]{:S(2)}) copy-start(bf16[3,3,4,8,256]{4,3,2,1,0:T(8,128)(2,1)} %refs_10_.3) | copy-start | bytes 442372
  0.7 33.5 %copy-start.6 = (bf16[3,3,4,8,256]{4,3,2,1,0:T(8,128)(2,1)S(1)}, bf16[3,3,4,8,256]{4,3,2,1,0:T(8,128)(2,1)}, u32[]{:S(2)}) copy-start(bf16[3,3,4,8,256]{4,3,2,1,0:T(8,128)(2,1)} %refs_9_.5) | copy-start | bytes 442372
  0.7 33.5 %copy-start.5 = (bf16[3,3,4,8,256]{4,3,2,1,0:T(8,128)(2,1)S(1)}, bf16[3,3,4,8,256]{4,3,2,1,0:T(8,128)(2,1)}, u32[]{:S(2)}) copy-start(bf16[3,3,4,8,256]{4,3,2,1,0:T(8,128)(2,1)} %refs_8_.13) | copy-start | bytes 442372
  0.7 33.5 %copy-start = (bf16[6,3,3,4,8,256]{5,4,3,2,1,0:T(8,128)(2,1)S(1)}, bf16[6,3,3,4,8,256]{5,4,3,2,1,0:T(8,128)(2,1)}, u32[]{:S(2)}) copy-start(bf16[6,3,3,4,8,256]{5,4,3,2,1,0:T(8,128)(2,1)} %refs_4_.7) | copy-start | bytes 2654212
  0.7 33.5 %copy-start.4 = (bf16[3,3,4,8,256]{4,3,2,1,0:T(8,128)(2,1)S(1)}, bf16[3,3,4,8,256]{4,3,2,1,0:T(8,128)(2,1)}, u32[]{:S(2)}) copy-start(bf16[3,3,4,8,256]{4,3,2,1,0:T(8,128)(2,1)} %refs_3_.7) | copy-start | bytes 442372
  3.8 13.3 %collective-permute-start.2 = (f32[56,256]{1,0:T(8,128)S(1)}, f32[56,256]{1,0:T(8,128)S(1)}, u32[]{:S(2)}, u32[]{:S(2)}) collective-permute-start(f32[56,256]{1,0:T(8,128)S(1)} %get-tuple-element.44.refs_3_), channel_id=1, source_target_pairs={{0,3},{1,0},{2,1},{3,2},{4,7},{5,4},{6,5},{7,6},{8,11},{9,8},{10,9... | collective-permute-start | bytes 172040 | tf_op jit(solution)/shard_map/ppermute | solution.py:661
  6.2 10.9 %collective-permute-start.1 = (f32[56,256]{1,0:T(8,128)S(1)}, f32[56,256]{1,0:T(8,128)S(1)}, u32[]{:S(2)}, u32[]{:S(2)}) collective-permute-start(f32[56,256]{1,0:T(8,128)S(1)} %get-tuple-element.44.refs_3_), channel_id=1, source_target_pairs={{0,2},{1,3},{2,0},{3,1},{4,6},{5,7},{6,4},{7,5},{8,10},{9,11},{10,... | collective-permute-start | bytes 172040 | tf_op jit(solution)/shard_map/ppermute | solution.py:661
  6.8 10.2 %collective-permute-start = (f32[128,256]{1,0:T(8,128)S(1)}, f32[128,256]{1,0:T(8,128)S(1)}, u32[]{:S(2)}, u32[]{:S(2)}) collective-permute-start(f32[128,256]{1,0:T(8,128)S(1)} %get-tuple-element.43), channel_id=1, source_target_pairs={{0,1},{1,2},{2,3},{3,0},{4,5},{5,6},{6,7},{7,4},{8,9},{9,10},{10,1... | collective-permute-start | bytes 393224 | tf_op jit(solution)/shard_map/ppermute | solution.py:661
  17.1 0.8 copy-start.1

commit v4 on v3

--- a/solution.py
+++ b/solution.py
@@ -202,7 +202,7 @@
     right_hbm, pivot_hbm, lower_hbm, upper_hbm, active_hbm,
     from_hbm, owner_hbm, target_hbm, block_hbm,
     edge_ref, next_ref, alone_ref, from_above_ref, from_below_ref, matrix_ref,
-    slot_block_ref, slot_source_ref, slot_target_ref,
+    slot_block_ref, slot_source_ref, slot_target_ref, mask_ref,
     right_ref, pivot_ref, lower_ref, upper_ref, active_ref,
     from_ref, owner_ref, target_ref, block_ref,
     stacked, products, folded, semaphores,
@@ -231,6 +231,7 @@
         right_ref, pivot_ref, lower_ref, upper_ref, active_ref,
         edge_ref, next_ref, alone_ref, from_above_ref, from_below_ref, matrix_ref,
     )
+    mask_ref[...] = wide(active_ref[...])
     rows, width = folded.shape[1:]
     for r in range(rows):
         for number, ref in enumerate((from_ref, owner_ref, target_ref)):
@@ -471,9 +472,8 @@
                 hot_row_ref[peer, :, i * width : (i + 1) * width] = jnp.where(
                     row_number == upper[at : at + 1], 1.0, 0.0
                 ).astype(BF16)
-    total_ref[...] = jnp.zeros(total_ref.shape, F32)
-
-    def from_peer(peer, carry):
+    added = None
+    for peer in range(peers):
         hot = hot_row_ref[peer]
         pieces = []
         for c in range(3):
@@ -482,12 +482,11 @@
                 piece = rest.astype(BF16)
                 rest = rest - wide(piece)
                 pieces.append(hot * jnp.broadcast_to(piece, hot.shape))
-        total_ref[...] += jnp.dot(
+        product = jnp.dot(
             jnp.concatenate(pieces, axis=0), hot_column_ref[peer], preferred_element_type=F32
         )
-        return carry
-
-    lax.fori_loop(0, peers, from_peer, 0)
+        added = product if added is None else added + product
+    total_ref[...] = added
 
     active = [wide(active_ref[k]) for k in range(layers)]
     held = [[solved_ref[c, k] * active[k] for c in range(3)] for k in range(layers)]
@@ -537,7 +536,7 @@
         pairs = [(r, r), (r, applied), (applied, applied)]
     else:
         if last:
-            (v_ref, z_ref, edge_ref, history_ref) = outs
+            (z_ref, edge_ref, history_ref) = outs
         else:
             (v_ref, z_ref, w_ref, edge_ref, alone_ref, history_ref) = outs
         fresh = got_ref[0, 0:1, ending : ending + 128]
@@ -569,9 +568,9 @@
                     v = v - factors[i] * old_v[i]
                     z = z - factors[i] * old_z[i]
                     w = w - factors[i] * old_w[i]
-                v_ref[c, k] = v
                 z_ref[c, k] = z
                 if not last:
+                    v_ref[c, k] = v
                     w_ref[c, k] = w
                 new[k].append(w)
                 members[k].append(v)
@@ -619,7 +618,7 @@
     table = jnp.zeros((8, 128), F32)
     for j in range(ITERS):
         for i, weight in enumerate(columns[j] + [lengths[j]]):
-            table = jnp.where((row_at == i) & (column_at == j), weight, table)
+            table = jnp.where((row_at == j) & (column_at == i), weight, table)
     hessenberg_ref[...] = table[0 : hessenberg_ref.shape[0], 0 : hessenberg_ref.shape[1]]
     goal = [beta]
     triangle = []
@@ -705,7 +704,7 @@
     ]
     (
         edge, following, alone, from_above, from_below, matrices,
-        slot_block, slot_source, slot_target,
+        slot_block, slot_source, slot_target, active,
     ) = call(
         functools.partial(setup_kernel, peers),
         [
@@ -718,6 +717,7 @@
             shape_of(3, 3, slots, width),
             shape_of(slots, width, kind=jnp.int32),
             shape_of(slots, width),
+            shape_of(layers, rows, width),
         ],
         [pltpu.VMEM(operand.shape, operand.dtype) for operand in operands]
         + [
@@ -759,11 +759,11 @@
             scratch,
             name="couple",
         )(
-            *turned, edges, all_matrices, alone, from_above, from_below, active_cells,
+            *turned, edges, all_matrices, alone, from_above, from_below, active,
             slot_block, slot_source, slot_target,
         )
         got = lax.all_to_all(sent, "areal", split_axis=0, concat_axis=0, tiled=True)
-        operands = [got, solved, layer_sides, diag_blocks, couplings, active_cells]
+        operands = [got, solved, layer_sides, diag_blocks, couplings, active]
         if step > 0:
             operands += [hot_row, hot_column]
         if not last:
@@ -783,7 +783,7 @@
                 shape_of(peers, capacity, width, kind=BF16),
             ]
         elif last:
-            outs = [field, field, shape_of(peers * sections, 1, 128), history]
+            outs = [field, shape_of(peers * sections, 1, 128), history]
         else:
             outs = [field, field, field, edge_shape, field, history]
         results = call(
@@ -798,7 +798,7 @@
             earlier.append((solved, applied))
             zs.append(solved)
         elif last:
-            _, z, dots, sums = results
+            z, dots, sums = results
             zs.append(z)
         else:
             v, z, w, edge, alone, sums = results
@@ -806,9 +806,9 @@
             zs.append(z)
     dots = lax.all_to_all(dots, ("areal", "layer"), split_axis=0, concat_axis=0, tiled=True)
     update, hessenberg = call(
-        finish_kernel, [field, shape_of(ITERS + 1, ITERS)], name="finish"
+        finish_kernel, [field, shape_of(ITERS, ITERS + 1)], name="finish"
     )(dots, sums, *zs)
-    return update, hessenberg
+    return update, hessenberg.T
 
 
 def solution(mesh):

time: 118 us -> 110 us (0.932)
  Pallas kernels: 26.1 us -> 19.3 us
  local copies, waits for them, and re-layouts: 1.45 us -> 0.03 us
    pallas_call x4, Pallas kernels: 14.8 us -> 7.94 us  [local(): call(functools.partial(operate_kernel, step), outs, ([pltpu.VMEM((slots,...]
where the time goes in v4:
time: 110 us
  blocking collectives  86.4 us (79%)
  Pallas kernels  19.3 us (18%)
  starting transfers between devices  3.23 us (3%)
    all_to_all x4, blocking collectives, local(): got = lax.all_to_all(sent, 'areal', split_axis=0, concat_axis=0, tiled=True)  49.1 us
    all_gather x3, blocking collectives, local(): edges = lax.all_gather(edge, 'layer', axis=0, tiled=False)  17.3 us
    all_gather x1, blocking collectives, local(): all_matrices = lax.all_gather(matrices, 'layer', axis=0, tiled=False)  10.1 us
    all_to_all x1, blocking collectives, local(): lax.all_to_all(dots, ('areal', 'layer'), split_axis=0, concat_axis=0, til...  9.96 us
    pallas_call x4, Pallas kernels, local(): call(functools.partial(operate_kernel, step), outs, ([pltpu.VMEM((slots,...  7.94 us
    pallas_call x4, Pallas kernels, local(): call(functools.partial(couple_kernel, step == 0, sections), [field, shape...  7.41 us
    ppermute x3, starting transfers between devices, turn(): lax.ppermute(array, 'layer', [(i, (i + by) % count) for i in range(count)])  3.23 us
    pallas_call x1, Pallas kernels, local(): call(functools.partial(setup_kernel, peers), [edge_shape, shape_of(16 * r...  3.06 us
  transfers between devices with their start and end apart: 3, of which 0 were waited for; matrix products, arithmetic and copies ran while one was open for 0% of the time, Pallas kernels for 0%

profile of v4, /device:TPU:0, one launch (start us, length us, event | category | flops | bytes accessed | tf_op | source)
XLA Modules:
  0.0 109.7 jit_solution(16286409350068345560)
XLA Ops:
  0.6 0.0 copy-start.1
  0.6 0.0 copy-start.5
  0.7 0.0 copy-start.4
  0.7 0.0 copy-start.3
  0.7 0.0 copy-start
  0.7 0.0 copy-start.2
  0.7 3.1 %setup.1 = (f32[56,256]{1,0:T(8,128)S(1)}, f32[128,256]{1,0:T(8,128)S(1)}, f32[3,4,8,256]{3,2,1,0:T(8,128)S(1)}, f32[3,3,4,8,256]{4,3,2,1,0:T(8,128)S(1)}, f32[3...) custom-call(f32[3,4,8,256]{3,2,1,0:T(8,128)} %refs_8_.7, ...), custom_call_target="tpu_custom_call" | custom-call | flops 4194304 | bytes 1048576 | tf_op jit(solution)/shard_map/setup/pallas_call | solution.py:708
  3.8 2.4 %collective-permute-start.2 = (f32[56,256]{1,0:T(8,128)S(1)}, f32[56,256]{1,0:T(8,128)S(1)}, u32[]{:S(2)}, u32[]{:S(2)}) collective-permute-start(f32[56,256]{1,0:T(8,128)S(1)} %get-tuple-element.47.refs_3_), channel_id=1, source_target_pairs={{0,3},{1,0},{2,1},{3,2},{4,7},{5,4},{6,5},{7,6},{8,11},{9,8},{10,9... | collective-permute-start | bytes 172040 | tf_op jit(solution)/shard_map/ppermute | solution.py:660
  6.2 0.7 collective-permute-start.1
  6.8 0.2 collective-permute-start
  7.0 10.1 %all-gather = f32[864,256]{1,0:T(8,128)S(1)} all-gather(f32[216,256]{1,0:T(8,128)S(1)} %get-tuple-element.48), channel_id=2, replica_groups=mesh['areal'=8,'layer'=4] {'layer'}, dimensions={0}, use_global_device_ids=true | all-gather | bytes 1105920 | tf_op jit(solution)/shard_map/all_gather | solution.py:734
  17.1 0.0 collective-permute-done.2.refs_2_
  17.1 0.0 collective-permute-done.1.refs_1_
  17.1 0.0 collective-permute-done.refs_0_
  17.1 1.9 %couple.4 = (f32[3,4,8,256]{3,2,1,0:T(8,128)S(1)}, f32[2,3,8,256]{3,2,1,0:T(8,128)S(1)}, f32[8,1,7168]{2,1,0:T(1,128)S(1)}) custom-call(f32[128,256]{1,0:T(8,128)S(1)} %collective-permute-done.refs_0_, f32[56,256]{1,0:T(8,128)S(1)} %collective-permute-done.1.refs_1_, f32[56,256]{1,0:T(8,128)S(1)} %collective-permute-done.2.refs_2_, ...), custom_call_target="tpu_custom_call" | custom-call | flops 4194304 | bytes 1048576 | tf_op jit(solution)/shard_map/couple/pallas_call | solution.py:752
  18.9 14.4 %all_to_all.25.refs_0_ = f32[8,1,7168]{2,1,0:T(1,128)S(1)} all-to-all(f32[8,1,7168]{2,1,0:T(1,128)S(1)} %get-tuple-element.56), channel_id=1, replica_groups=mesh['areal'=8,'layer'=4] {'areal'}, dimensions={0} | all-to-all | bytes 458752 | tf_op jit(solution)/shard_map/all_to_all | solution.py:765
  33.4 0.0 copy-done.1
  33.4 0.0 copy-done.5
  33.4 0.0 copy-done.4
  33.4 0.0 copy-done.3
  33.4 0.0 copy-done
  33.4 0.0 copy-done.2
  33.4 2.6 %operate.4 = (f32[3,4,8,256]{3,2,1,0:T(8,128)S(1)}, f32[56,256]{1,0:T(8,128)S(1)}, f32[3,4,8,256]{3,2,1,0:T(8,128)S(1)}, bf16[8,32,1024]{2,1,0:T(8,128)(2,1)S(1)}, bf16[8,1024,256]{2,1,0:T(8,128)(2,1)S(1)}) custom-call(f32[8,1,7168]{2,1,0:T(1,128)S(1)} %all_to_all.25.refs_0_, f32[3,4,8,256]{3,2,1,0:T(8,128)S(1)} %get-tuple-element.57.refs_1_.refs_13_.refs_10_.z0_ref, ...), custom_call_target="tpu_custom_call" | custom-call | flops 4194304 | bytes 1048576 | tf_op jit(solution)/shard_map/operate/pallas_call | solution.py:789
  36.0 5.7 %all-gather.1 = f32[224,256]{1,0:T(8,128)S(1)} all-gather(f32[56,256]{1,0:T(8,128)S(1)} %get-tuple-element.59), channel_id=3, replica_groups=mesh['areal'=8,'layer'=4] {'layer'}, dimensions={0}, use_global_device_ids=true | all-gather | bytes 286720 | tf_op jit(solution)/shard_map/all_gather | solution.py:751
  41.6 1.8 %couple.5 = (f32[3,4,8,256]{3,2,1,0:T(8,128)S(1)}, f32[2,3,8,256]{3,2,1,0:T(8,128)S(1)}, f32[8,1,6272]{2,1,0:T(1,128)S(1)}) custom-call(f32[128,256]{1,0:T(8,128)S(1)} %collective-permute-done.refs_0_, f32[56,256]{1,0:T(8,128)S(1)} %collective-permute-done.1.refs_1_, f32[56,256]{1,0:T(8,128)S(1)} %collective-permute-done.2.refs_2_, ...), custom_call_target="tpu_custom_call" | custom-call | flops 4194304 | bytes 1048576 | tf_op jit(solution)/shard_map/couple/pallas_call | solution.py:752
  43.5 11.7 %all_to_all.26.refs_0_ = f32[8,1,6272]{2,1,0:T(1,128)S(1)} all-to-all(f32[8,1,6272]{2,1,0:T(1,128)S(1)} %get-tuple-element.61), channel_id=1, replica_groups=mesh['areal'=8,'layer'=4] {'areal'}, dimensions={0} | all-to-all | bytes 401408 | tf_op jit(solution)/shard_map/all_to_all | solution.py:765
  55.2 1.8 %operate.5 = (f32[3,4,8,256]{3,2,1,0:T(8,128)S(1)}, f32[3,4,8,256]{3,2,1,0:T(8,128)S(1)}, f32[3,4,8,256]{3,2,1,0:T(8,128)S(1)}, f32[56,256]{1,0:T(8,128)S(1)}, f...) custom-call(f32[8,1,6272]{2,1,0:T(1,128)S(1)} %all_to_all.26.refs_0_, f32[3,4,8,256]{3,2,1,0:T(8,128)S(1)} %get-tuple-element.62.refs_1_, ...), custom_call_target="tpu_custom_call" | custom-call | flops 4194304 | bytes 1048576 | tf_op jit(solution)/shard_map/operate/pallas_call | solution.py:789
  57.0 5.9 %all-gather.2 = f32[224,256]{1,0:T(8,128)S(1)} all-gather(f32[56,256]{1,0:T(8,128)S(1)} %get-tuple-element.67), channel_id=4, replica_groups=mesh['areal'=8,'layer'=4] {'layer'}, dimensions={0}, use_global_device_ids=true | all-gather | bytes 286720 | tf_op jit(solution)/shard_map/all_gather | solution.py:751
  62.9 1.8 %couple.6 = (f32[3,4,8,256]{3,2,1,0:T(8,128)S(1)}, f32[2,3,8,256]{3,2,1,0:T(8,128)S(1)}, f32[8,1,6272]{2,1,0:T(1,128)S(1)}) custom-call(f32[128,256]{1,0:T(8,128)S(1)} %collective-permute-done.refs_0_, f32[56,256]{1,0:T(8,128)S(1)} %collective-permute-done.1.refs_1_, f32[56,256]{1,0:T(8,128)S(1)} %collective-permute-done.2.refs_2_, ...), custom_call_target="tpu_custom_call" | custom-call | flops 4194304 | bytes 1048576 | tf_op jit(solution)/shard_map/couple/pallas_call | solution.py:752
  64.7 11.5 %all_to_all.27.refs_0_ = f32[8,1,6272]{2,1,0:T(1,128)S(1)} all-to-all(f32[8,1,6272]{2,1,0:T(1,128)S(1)} %get-tuple-element.69), channel_id=1, replica_groups=mesh['areal'=8,'layer'=4] {'areal'}, dimensions={0} | all-to-all | bytes 401408 | tf_op jit(solution)/shard_map/all_to_all | solution.py:765
  76.2 1.8 %operate.6 = (f32[3,4,8,256]{3,2,1,0:T(8,128)S(1)}, f32[3,4,8,256]{3,2,1,0:T(8,128)S(1)}, f32[3,4,8,256]{3,2,1,0:T(8,128)S(1)}, f32[56,256]{1,0:T(8,128)S(1)}, f...) custom-call(f32[8,1,6272]{2,1,0:T(1,128)S(1)} %all_to_all.27.refs_0_, f32[3,4,8,256]{3,2,1,0:T(8,128)S(1)} %get-tuple-element.70.refs_1_, ...), custom_call_target="tpu_custom_call" | custom-call | flops 4194304 | bytes 1048576 | tf_op jit(solution)/shard_map/operate/pallas_call | solution.py:789
  78.0 5.7 %all-gather.3 = f32[224,256]{1,0:T(8,128)S(1)} all-gather(f32[56,256]{1,0:T(8,128)S(1)} %get-tuple-element.76), channel_id=5, replica_groups=mesh['areal'=8,'layer'=4] {'layer'}, dimensions={0}, use_global_device_ids=true | all-gather | bytes 286720 | tf_op jit(solution)/shard_map/all_gather | solution.py:751
  83.7 1.8 %couple.7 = (f32[3,4,8,256]{3,2,1,0:T(8,128)S(1)}, f32[2,3,8,256]{3,2,1,0:T(8,128)S(1)}, f32[8,1,6272]{2,1,0:T(1,128)S(1)}) custom-call(f32[128,256]{1,0:T(8,128)S(1)} %collective-permute-done.refs_0_, f32[56,256]{1,0:T(8,128)S(1)} %collective-permute-done.1.refs_1_, f32[56,256]{1,0:T(8,128)S(1)} %collective-permute-done.2.refs_2_, ...), custom_call_target="tpu_custom_call" | custom-call | flops 4194304 | bytes 1048576 | tf_op jit(solution)/shard_map/couple/pallas_call | solution.py:752
  85.6 11.5 %all_to_all.28.refs_0_ = f32[8,1,6272]{2,1,0:T(1,128)S(1)} all-to-all(f32[8,1,6272]{2,1,0:T(1,128)S(1)} %get-tuple-element.78), channel_id=1, replica_groups=mesh['areal'=8,'layer'=4] {'areal'}, dimensions={0} | all-to-all | bytes 401408 | tf_op jit(solution)/shard_map/all_to_all | solution.py:765
  97.1 1.8 %operate.7 = (f32[3,4,8,256]{3,2,1,0:T(8,128)S(1)}, f32[32,1,128]{2,1,0:T(1,128)S(1)}, f32[8,128]{1,0:T(8,128)S(1)}) custom-call(f32[8,1,6272]{2,1,0:T(1,128)S(1)} %all_to_all.28.refs_0_, f32[3,4,8,256]{3,2,1,0:T(8,128)S(1)} %get-tuple-element.79.refs_1_, f32[2,3,8,256]{3,2,1,0:T(8,128)S(1)} %get-tuple-element.80.refs_2_, ...), custom_call_target="tpu_custom_call" | custom-call | flops 4194304 | bytes 1048576 | tf_op jit(solution)/shard_map/operate/pallas_call | solution.py:789
  98.9 10.0 %all_to_all.29.dots_ref = f32[32,1,128]{2,1,0:T(1,128)S(1)} all-to-all(f32[32,1,128]{2,1,0:T(1,128)S(1)} %get-tuple-element.85), channel_id=1, replica_groups=mesh['areal'=8,'layer'=4] {'areal','layer'}, dimensions={0} | all-to-all | bytes 32768 | tf_op jit(solution)/shard_map/all_to_all | solution.py:807
  108.8 0.9 finish.1
  (1 shorter events, 0.0 us)
Async XLA Ops:
  0.6 32.7 %copy-start.1 = (f32[3,4,8,256]{3,2,1,0:T(8,128)S(1)}, f32[3,4,8,256]{3,2,1,0:T(8,128)}, u32[]{:S(2)}) copy-start(f32[3,4,8,256]{3,2,1,0:T(8,128)} %refs_8_.7) | copy-start | bytes 294916
  0.6 32.7 %copy-start.5 = (bf16[3,3,4,8,256]{4,3,2,1,0:T(8,128)(2,1)S(1)}, bf16[3,3,4,8,256]{4,3,2,1,0:T(8,128)(2,1)}, u32[]{:S(2)}) copy-start(bf16[3,3,4,8,256]{4,3,2,1,0:T(8,128)(2,1)} %refs_10_.3) | copy-start | bytes 442372
  0.7 32.7 %copy-start.4 = (bf16[3,3,4,8,256]{4,3,2,1,0:T(8,128)(2,1)S(1)}, bf16[3,3,4,8,256]{4,3,2,1,0:T(8,128)(2,1)}, u32[]{:S(2)}) copy-start(bf16[3,3,4,8,256]{4,3,2,1,0:T(8,128)(2,1)} %refs_9_.5) | copy-start | bytes 442372
  0.7 32.7 %copy-start.3 = (bf16[3,3,4,8,256]{4,3,2,1,0:T(8,128)(2,1)S(1)}, bf16[3,3,4,8,256]{4,3,2,1,0:T(8,128)(2,1)}, u32[]{:S(2)}) copy-start(bf16[3,3,4,8,256]{4,3,2,1,0:T(8,128)(2,1)} %refs_8_.6) | copy-start | bytes 442372
  0.7 32.7 %copy-start = (bf16[6,3,3,4,8,256]{5,4,3,2,1,0:T(8,128)(2,1)S(1)}, bf16[6,3,3,4,8,256]{5,4,3,2,1,0:T(8,128)(2,1)}, u32[]{:S(2)}) copy-start(bf16[6,3,3,4,8,256]{5,4,3,2,1,0:T(8,128)(2,1)} %refs_4_.7) | copy-start | bytes 2654212
  0.7 32.7 %copy-start.2 = (bf16[3,3,4,8,256]{4,3,2,1,0:T(8,128)(2,1)S(1)}, bf16[3,3,4,8,256]{4,3,2,1,0:T(8,128)(2,1)}, u32[]{:S(2)}) copy-start(bf16[3,3,4,8,256]{4,3,2,1,0:T(8,128)(2,1)} %refs_3_.7) | copy-start | bytes 442372
  3.8 13.3 %collective-permute-start.2 = (f32[56,256]{1,0:T(8,128)S(1)}, f32[56,256]{1,0:T(8,128)S(1)}, u32[]{:S(2)}, u32[]{:S(2)}) collective-permute-start(f32[56,256]{1,0:T(8,128)S(1)} %get-tuple-element.47.refs_3_), channel_id=1, source_target_pairs={{0,3},{1,0},{2,1},{3,2},{4,7},{5,4},{6,5},{7,6},{8,11},{9,8},{10,9... | collective-permute-start | bytes 172040 | tf_op jit(solution)/shard_map/ppermute | solution.py:660
  6.2 10.9 %collective-permute-start.1 = (f32[56,256]{1,0:T(8,128)S(1)}, f32[56,256]{1,0:T(8,128)S(1)}, u32[]{:S(2)}, u32[]{:S(2)}) collective-permute-start(f32[56,256]{1,0:T(8,128)S(1)} %get-tuple-element.47.refs_3_), channel_id=1, source_target_pairs={{0,2},{1,3},{2,0},{3,1},{4,6},{5,7},{6,4},{7,5},{8,10},{9,11},{10,... | collective-permute-start | bytes 172040 | tf_op jit(solution)/shard_map/ppermute | solution.py:660
  6.8 10.2 %collective-permute-start = (f32[128,256]{1,0:T(8,128)S(1)}, f32[128,256]{1,0:T(8,128)S(1)}, u32[]{:S(2)}, u32[]{:S(2)}) collective-permute-start(f32[128,256]{1,0:T(8,128)S(1)} %get-tuple-element.46), channel_id=1, source_target_pairs={{0,1},{1,2},{2,3},{3,0},{4,5},{5,6},{6,7},{7,4},{8,9},{9,10},{10,1... | collective-permute-start | bytes 393224 | tf_op jit(solution)/shard_map/ppermute | solution.py:660

commit v5 on v4

--- a/solution.py
+++ b/solution.py
@@ -8,8 +8,9 @@
 from jax.sharding import PartitionSpec as P
 
 ITERS = 4
-PARTS = 3
+PARTS = 2
 TINY = 1e-06
+LANES = 128
 
 F32 = jnp.float32
 BF16 = jnp.bfloat16
@@ -128,11 +129,12 @@
 
 
 def routing_part(
-    peers, folded, block_ref, slot_block_ref, slot_source_ref, slot_target_ref, stacked, products
+    peers, cells, folded, block_ref,
+    slot_block_ref, slot_source_ref, slot_target_ref, start_ref, stacked, products, packed,
 ):
     rows, width = folded.shape[1:]
     slots = slot_source_ref.shape[0]
-    per_peer = slots // peers
+    per_peer = slot_target_ref.shape[0] // peers
     owner = folded[1]
     for o in range(peers):
         stacked[o * rows : (o + 1) * rows] = jnp.where(owner == o, 1.0, 0.0).astype(BF16)
@@ -152,13 +154,25 @@
         0.0,
     ).astype(BF16)
     rank = jnp.zeros((rows, width), F32)
+    start = jnp.zeros((1, width), jnp.int32)
+    starts, counts = [], []
+    slot_row = jnp.zeros((rows, width), jnp.int32)
+    lane = lax.broadcasted_iota(jnp.int32, start_ref.shape, 1)
+    listed = jnp.zeros(start_ref.shape, jnp.int32)
     for o in range(peers):
         part = slice(o * rows, (o + 1) * rows)
         before = jnp.dot(row_before, totals[part].astype(BF16), preferred_element_type=F32)
         rank = rank + jnp.where(owner == o, within[part] + before, 0.0)
+        slot_row = slot_row + jnp.where(owner == o, start, 0)
+        listed = jnp.where(lane == o, start[:, 0:LANES], listed)
+        count = jnp.sum(totals[part], axis=0, keepdims=True).astype(jnp.int32)
+        starts.append(start)
+        counts.append(count)
+        start = start + (count + (LANES - 1)) // LANES
+    start_ref[...] = listed
     rank = rank.astype(jnp.int32)
-    slot_row = owner * per_peer + rank // width
-    slot_column = rank % width
+    slot_row = slot_row + rank // LANES
+    slot_column = rank % LANES
     source = folded[0]
     target = folded[2]
     payloads = [
@@ -168,7 +182,7 @@
         wide(target % width),
     ]
     row_number = lax.broadcasted_iota(jnp.int32, (slots, width), 0)
-    column_number = lax.broadcasted_iota(jnp.int32, (width, width), 0)
+    column_number = lax.broadcasted_iota(jnp.int32, (LANES, width), 0)
     total = jnp.zeros(products.shape, F32)
     for r in range(rows):
         in_row = row_number == slot_row[r : r + 1]
@@ -190,7 +204,17 @@
         )
     products[...] = total
     slot_source_ref[...] = (products[0:slots] * width + products[slots : 2 * slots]).astype(jnp.int32)
-    slot_target_ref[...] = products[2 * slots : 3 * slots] * width + products[3 * slots : 4 * slots]
+    packed[...] = jnp.zeros(packed.shape, F32)
+    packed[0:slots] = products[2 * slots : 3 * slots] * width + products[3 * slots : 4 * slots]
+    at_lane = lax.broadcasted_iota(jnp.int32, (1, LANES), 1)
+    nowhere = float(cells)
+    for o in range(peers):
+        first = starts[o][0, 0]
+        for i in range(per_peer):
+            row = packed[pl.ds(first + i, 1), :]
+            slot_target_ref[o * per_peer + i : o * per_peer + i + 1] = jnp.where(
+                at_lane + i * LANES < counts[o][:, 0:LANES], row, nowhere
+            )
     for c in range(3):
         for d in range(3):
             at = 4 + c * 3 + d
@@ -202,10 +226,10 @@
     right_hbm, pivot_hbm, lower_hbm, upper_hbm, active_hbm,
     from_hbm, owner_hbm, target_hbm, block_hbm,
     edge_ref, next_ref, alone_ref, from_above_ref, from_below_ref, matrix_ref,
-    slot_block_ref, slot_source_ref, slot_target_ref, mask_ref,
+    slot_block_ref, slot_source_ref, slot_target_ref, start_ref, mask_ref,
     right_ref, pivot_ref, lower_ref, upper_ref, active_ref,
     from_ref, owner_ref, target_ref, block_ref,
-    stacked, products, folded, semaphores,
+    stacked, products, packed, folded, semaphores,
 ):
     copies = [
         pltpu.make_async_copy(source, landing, semaphores.at[number])
@@ -237,7 +261,8 @@
         for number, ref in enumerate((from_ref, owner_ref, target_ref)):
             folded[number, r : r + 1] = ref[0:1, r * width : (r + 1) * width]
     routing_part(
-        peers, folded, block_ref, slot_block_ref, slot_source_ref, slot_target_ref, stacked, products
+        peers, active_ref.size, folded, block_ref,
+        slot_block_ref, slot_source_ref, slot_target_ref, start_ref, stacked, products, packed,
     )
 
 
@@ -253,14 +278,15 @@
         edge_ref, refs = refs[0], refs[1:]
     (
         matrix_ref, alone_ref, above_ref, below_ref, active_ref,
-        slot_block_ref, slot_source_ref, slot_target_ref,
-        solved_ref, layer_ref, sent_ref, arriving, tops, borders, table,
+        slot_block_ref, slot_source_ref, slot_target_ref, start_ref,
+        solved_ref, layer_ref, sent_ref, arriving, tops, borders, table, packed,
     ) = refs
     layers, rows = alone_ref.shape[1], alone_ref.shape[2]
     width = alone_ref.shape[3]
     peers = sent_ref.shape[0]
     slots = slot_source_ref.shape[0]
-    per_peer = slots // peers
+    per_peer = slot_target_ref.shape[0] // peers
+    capacity = per_peer * LANES
     s = lax.axis_index("layer")
     a = lax.axis_index("areal")
     if first:
@@ -325,40 +351,40 @@
     for c in range(3):
         layer_ref[0, c] = upstairs[c] * upper_active
         layer_ref[1, c] = below[c] * lower_active
-    half = 128
-    groups = [(g, h) for g in range(slots // 8) for h in range(width // half)]
+    starts = start_ref[...]
+    packed[...] = jnp.zeros(packed.shape, F32)
     for g in range(slots // 8):
-        for h in range(width // half):
-            source = slot_source_ref[g * 8 : (g + 1) * 8, h * half : (h + 1) * half]
-            line = source // half
-            lane = source % half
-            found = [jnp.zeros((8, half), F32)] * 3
-            for r in range(layers * rows):
-                for q in range(width // half):
-                    here = line == r * (width // half) + q
-                    for c in range(3):
-                        row = jnp.broadcast_to(
-                            table[c, r : r + 1, q * half : (q + 1) * half], (8, half)
-                        )
-                        picked = jnp.take_along_axis(row, lane, axis=1)
-                        found[c] = jnp.where(here, picked, found[c])
+        group = slice(g * 8, (g + 1) * 8)
+        source = slot_source_ref[group]
+        line = source // LANES
+        lane = source % LANES
+        found = [jnp.zeros((8, LANES), F32)] * 3
+        for r in range(layers * rows):
+            for q in range(width // LANES):
+                here = line == r * (width // LANES) + q
+                for c in range(3):
+                    row = jnp.broadcast_to(
+                        table[c, r : r + 1, q * LANES : (q + 1) * LANES], (8, LANES)
+                    )
+                    picked = jnp.take_along_axis(row, lane, axis=1)
+                    found[c] = jnp.where(here, picked, found[c])
+        for c in range(3):
+            value = slot_block_ref[c, 0, group] * found[0]
+            for d in range(1, 3):
+                value = value + slot_block_ref[c, d, group] * found[d]
+            packed[c, group] = value
+    for peer in range(peers):
+        start = starts[0, peer]
+        for i in range(per_peer):
             for c in range(3):
-                value = slot_block_ref[c, 0, g * 8 : (g + 1) * 8, h * half : (h + 1) * half] * found[0]
-                for d in range(1, 3):
-                    value = value + (
-                        slot_block_ref[c, d, g * 8 : (g + 1) * 8, h * half : (h + 1) * half] * found[d]
-                    )
-                for i in range(8):
-                    slot = g * 8 + i
-                    peer, at = slot // per_peer, slot % per_peer
-                    start = (c * per_peer + at) * width + h * half
-                    sent_ref[peer, 0:1, start : start + half] = value[i : i + 1]
-    base = 3 * per_peer * width
+                at = c * capacity + i * LANES
+                sent_ref[peer, 0:1, at : at + LANES] = packed[c, pl.ds(start + i, 1), :]
+    base = 3 * capacity
     many = 3 * layers
     if not first:
-        sums = edge_ref[0, 6 * rows : 6 * rows + 1, 0:half]
+        sums = edge_ref[0, 6 * rows : 6 * rows + 1, 0:LANES]
         for section in range(1, sections):
-            sums = sums + edge_ref[section, 6 * rows : 6 * rows + 1, 0:half]
+            sums = sums + edge_ref[section, 6 * rows : 6 * rows + 1, 0:LANES]
     for peer in range(peers):
         side = jnp.where(peer > a, 1, 0)
         for i in range(many):
@@ -366,11 +392,11 @@
             sent_ref[peer, 0:1, start : start + width] = borders[side, i : i + 1]
         start = base + many * width
         if not first:
-            sent_ref[peer, 0:1, start : start + half] = sums
+            sent_ref[peer, 0:1, start : start + LANES] = sums
         else:
             for i in range(per_peer):
                 at = peer * per_peer + i
-                sent_ref[peer, 0:1, start + i * width : start + (i + 1) * width] = slot_target_ref[
+                sent_ref[peer, 0:1, start + i * LANES : start + (i + 1) * LANES] = slot_target_ref[
                     at : at + 1
                 ]
 
@@ -685,6 +711,8 @@
     slots = capacity * peers // width
     per_peer = slots // peers
     link_rows = links // width
+    compact = -(-(links // LANES + peers) // 8) * 8
+    packed_rows = compact + -(-capacity // LANES // 8) * 8
     field = shape_of(3, layers, rows, width)
     edge_rows = 7 * rows
     sent_width = (3 * per_peer + 3 * layers) * width + 128
@@ -704,7 +732,7 @@
     ]
     (
         edge, following, alone, from_above, from_below, matrices,
-        slot_block, slot_source, slot_target, active,
+        slot_block, slot_source, slot_target, starts, active,
     ) = call(
         functools.partial(setup_kernel, peers),
         [
@@ -714,15 +742,17 @@
             shape_of(3, 3, layers, rows, width),
             shape_of(3, 3, layers, rows, width),
             shape_of(27 * rows, width),
-            shape_of(3, 3, slots, width),
-            shape_of(slots, width, kind=jnp.int32),
-            shape_of(slots, width),
+            shape_of(3, 3, compact, LANES),
+            shape_of(compact, LANES, kind=jnp.int32),
+            shape_of(capacity * peers // LANES, LANES),
+            shape_of(1, LANES, kind=jnp.int32),
             shape_of(layers, rows, width),
         ],
         [pltpu.VMEM(operand.shape, operand.dtype) for operand in operands]
         + [
             pltpu.VMEM((peers * link_rows, width), BF16),
-            pltpu.VMEM((13 * slots, width), F32),
+            pltpu.VMEM((13 * compact, LANES), F32),
+            pltpu.VMEM((packed_rows, LANES), F32),
             pltpu.VMEM((3, link_rows, width), jnp.int32),
             pltpu.SemaphoreType.DMA((len(operands),)),
         ],
@@ -743,6 +773,7 @@
             pltpu.VMEM((sections, 3, rows, width), F32),
             pltpu.VMEM((2, 16, width), F32),
             pltpu.VMEM((3, layers * rows, width), F32),
+            pltpu.VMEM((3, packed_rows, LANES), F32),
         ]
         if step == 0:
             edges = edge
@@ -760,7 +791,7 @@
             name="couple",
         )(
             *turned, edges, all_matrices, alone, from_above, from_below, active,
-            slot_block, slot_source, slot_target,
+            slot_block, slot_source, slot_target, starts,
         )
         got = lax.all_to_all(sent, "areal", split_axis=0, concat_axis=0, tiled=True)
         operands = [got, solved, layer_sides, diag_blocks, couplings, active]

time: 110 us -> 107 us (0.973)
  Pallas kernels: 19.3 us -> 15.9 us
    pallas_call x4, Pallas kernels: 7.41 us -> 5.28 us  [local(): call(functools.partial(couple_kernel, step == 0, sections), [field, shape...]
    pallas_call x4, Pallas kernels: 7.94 us -> 6.41 us  [local(): call(functools.partial(operate_kernel, step), outs, ([pltpu.VMEM((slots,...]
where the time goes in v5:
time: 107 us; the launch traced here: 106 us
  blocking collectives  86.4 us (81%)
  Pallas kernels  15.9 us (15%)
  starting transfers between devices  3.23 us (3%)
    all_to_all x4, blocking collectives, local(): got = lax.all_to_all(sent, 'areal', split_axis=0, concat_axis=0, tiled=True)  49.1 us
    all_gather x3, blocking collectives, local(): edges = lax.all_gather(edge, 'layer', axis=0, tiled=False)  17.3 us
    all_gather x1, blocking collectives, local(): all_matrices = lax.all_gather(matrices, 'layer', axis=0, tiled=False)  10.1 us
    all_to_all x1, blocking collectives, local(): lax.all_to_all(dots, ('areal', 'layer'), split_axis=0, concat_axis=0, til...  9.96 us
    pallas_call x4, Pallas kernels, local(): call(functools.partial(operate_kernel, step), outs, ([pltpu.VMEM((slots,...  6.41 us
    pallas_call x4, Pallas kernels, local(): call(functools.partial(couple_kernel, step == 0, sections), [field, shape...  5.28 us
    pallas_call x1, Pallas kernels, local(): call(functools.partial(setup_kernel, peers), [edge_shape, shape_of(16 * r...  3.29 us
    ppermute x3, starting transfers between devices, turn(): lax.ppermute(array, 'layer', [(i, (i + by) % count) for i in range(count)])  3.23 us
  transfers between devices with their start and end apart: 3, of which 0 were waited for; matrix products, arithmetic and copies ran while one was open for 0% of the time, Pallas kernels for 0%

profile of v5, /device:TPU:0, one launch (start us, length us, event | category | flops | bytes accessed | tf_op | source)
XLA Modules:
  0.0 106.3 jit_solution(4023443281722937129)
XLA Ops:
  0.6 0.0 copy-start.1
  0.6 0.0 copy-start.5
  0.7 0.0 copy-start.4
  0.7 0.0 copy-start.3
  0.7 0.0 copy-start
  0.7 0.0 copy-start.2
  0.7 3.3 %setup.1 = (f32[56,256]{1,0:T(8,128)S(1)}, f32[128,256]{1,0:T(8,128)S(1)}, f32[3,4,8,256]{3,2,1,0:T(8,128)S(1)}, f32[3,3,4,8,256]{4,3,2,1,0:T(8,128)S(1)}, f32[3...) custom-call(f32[3,4,8,256]{3,2,1,0:T(8,128)} %refs_8_.7, ...), custom_call_target="tpu_custom_call" | custom-call | flops 4194304 | bytes 1048576 | tf_op jit(solution)/shard_map/setup/pallas_call | solution.py:736
  4.0 2.4 %collective-permute-start.2 = (f32[56,256]{1,0:T(8,128)S(1)}, f32[56,256]{1,0:T(8,128)S(1)}, u32[]{:S(2)}, u32[]{:S(2)}) collective-permute-start(f32[56,256]{1,0:T(8,128)S(1)} %get-tuple-element.48.refs_3_), channel_id=1, source_target_pairs={{0,3},{1,0},{2,1},{3,2},{4,7},{5,4},{6,5},{7,6},{8,11},{9,8},{10,9... | collective-permute-start | bytes 172040 | tf_op jit(solution)/shard_map/ppermute | solution.py:686
  6.4 0.6 collective-permute-start.1
  7.1 0.2 collective-permute-start
  7.2 10.1 %all-gather = f32[864,256]{1,0:T(8,128)S(1)} all-gather(f32[216,256]{1,0:T(8,128)S(1)} %get-tuple-element.49), channel_id=2, replica_groups=mesh['areal'=8,'layer'=4] {'layer'}, dimensions={0}, use_global_device_ids=true | all-gather | bytes 1105920 | tf_op jit(solution)/shard_map/all_gather | solution.py:764
  17.3 0.0 collective-permute-done.2.refs_2_
  17.3 0.0 collective-permute-done.1.refs_1_
  17.3 0.0 collective-permute-done.refs_0_
  17.3 1.3 %couple.4 = (f32[3,4,8,256]{3,2,1,0:T(8,128)S(1)}, f32[2,3,8,256]{3,2,1,0:T(8,128)S(1)}, f32[8,1,7168]{2,1,0:T(1,128)S(1)}) custom-call(f32[128,256]{1,0:T(8,128)S(1)} %collective-permute-done.refs_0_, f32[56,256]{1,0:T(8,128)S(1)} %collective-permute-done.1.refs_1_, f32[56,256]{1,0:T(8,128)S(1)} %collective-permute-done.2.refs_2_, ...), custom_call_target="tpu_custom_call" | custom-call | flops 4194304 | bytes 1048576 | tf_op jit(solution)/shard_map/couple/pallas_call | solution.py:783
  18.7 14.4 %all_to_all.25.refs_0_ = f32[8,1,7168]{2,1,0:T(1,128)S(1)} all-to-all(f32[8,1,7168]{2,1,0:T(1,128)S(1)} %get-tuple-element.58), channel_id=1, replica_groups=mesh['areal'=8,'layer'=4] {'areal'}, dimensions={0} | all-to-all | bytes 458752 | tf_op jit(solution)/shard_map/all_to_all | solution.py:796
  33.1 0.0 copy-done.1
  33.1 0.0 copy-done.5
  33.1 0.0 copy-done.4
  33.1 0.0 copy-done.3
  33.1 0.0 copy-done
  33.1 0.0 copy-done.2
  33.1 2.3 %operate.4 = (f32[3,4,8,256]{3,2,1,0:T(8,128)S(1)}, f32[56,256]{1,0:T(8,128)S(1)}, f32[3,4,8,256]{3,2,1,0:T(8,128)S(1)}, bf16[8,32,1024]{2,1,0:T(8,128)(2,1)S(1)}, bf16[8,1024,256]{2,1,0:T(8,128)(2,1)S(1)}) custom-call(f32[8,1,7168]{2,1,0:T(1,128)S(1)} %all_to_all.25.refs_0_, f32[3,4,8,256]{3,2,1,0:T(8,128)S(1)} %get-tuple-element.59.refs_1_.refs_13_.refs_10_.z0_ref, ...), custom_call_target="tpu_custom_call" | custom-call | flops 4194304 | bytes 1048576 | tf_op jit(solution)/shard_map/operate/pallas_call | solution.py:820
  35.4 5.7 %all-gather.1 = f32[224,256]{1,0:T(8,128)S(1)} all-gather(f32[56,256]{1,0:T(8,128)S(1)} %get-tuple-element.61), channel_id=3, replica_groups=mesh['areal'=8,'layer'=4] {'layer'}, dimensions={0}, use_global_device_ids=true | all-gather | bytes 286720 | tf_op jit(solution)/shard_map/all_gather | solution.py:782
  41.1 1.3 %couple.5 = (f32[3,4,8,256]{3,2,1,0:T(8,128)S(1)}, f32[2,3,8,256]{3,2,1,0:T(8,128)S(1)}, f32[8,1,6272]{2,1,0:T(1,128)S(1)}) custom-call(f32[128,256]{1,0:T(8,128)S(1)} %collective-permute-done.refs_0_, f32[56,256]{1,0:T(8,128)S(1)} %collective-permute-done.1.refs_1_, f32[56,256]{1,0:T(8,128)S(1)} %collective-permute-done.2.refs_2_, ...), custom_call_target="tpu_custom_call" | custom-call | flops 4194304 | bytes 1048576 | tf_op jit(solution)/shard_map/couple/pallas_call | solution.py:783
  42.4 11.7 %all_to_all.26.refs_0_ = f32[8,1,6272]{2,1,0:T(1,128)S(1)} all-to-all(f32[8,1,6272]{2,1,0:T(1,128)S(1)} %get-tuple-element.63), channel_id=1, replica_groups=mesh['areal'=8,'layer'=4] {'areal'}, dimensions={0} | all-to-all | bytes 401408 | tf_op jit(solution)/shard_map/all_to_all | solution.py:796
  54.1 1.4 %operate.5 = (f32[3,4,8,256]{3,2,1,0:T(8,128)S(1)}, f32[3,4,8,256]{3,2,1,0:T(8,128)S(1)}, f32[3,4,8,256]{3,2,1,0:T(8,128)S(1)}, f32[56,256]{1,0:T(8,128)S(1)}, f...) custom-call(f32[8,1,6272]{2,1,0:T(1,128)S(1)} %all_to_all.26.refs_0_, f32[3,4,8,256]{3,2,1,0:T(8,128)S(1)} %get-tuple-element.64.refs_1_, ...), custom_call_target="tpu_custom_call" | custom-call | flops 4194304 | bytes 1048576 | tf_op jit(solution)/shard_map/operate/pallas_call | solution.py:820
  55.5 5.7 %all-gather.2 = f32[224,256]{1,0:T(8,128)S(1)} all-gather(f32[56,256]{1,0:T(8,128)S(1)} %get-tuple-element.69), channel_id=4, replica_groups=mesh['areal'=8,'layer'=4] {'layer'}, dimensions={0}, use_global_device_ids=true | all-gather | bytes 286720 | tf_op jit(solution)/shard_map/all_gather | solution.py:782
  61.2 1.3 %couple.6 = (f32[3,4,8,256]{3,2,1,0:T(8,128)S(1)}, f32[2,3,8,256]{3,2,1,0:T(8,128)S(1)}, f32[8,1,6272]{2,1,0:T(1,128)S(1)}) custom-call(f32[128,256]{1,0:T(8,128)S(1)} %collective-permute-done.refs_0_, f32[56,256]{1,0:T(8,128)S(1)} %collective-permute-done.1.refs_1_, f32[56,256]{1,0:T(8,128)S(1)} %collective-permute-done.2.refs_2_, ...), custom_call_target="tpu_custom_call" | custom-call | flops 4194304 | bytes 1048576 | tf_op jit(solution)/shard_map/couple/pallas_call | solution.py:783
  62.5 11.5 %all_to_all.27.refs_0_ = f32[8,1,6272]{2,1,0:T(1,128)S(1)} all-to-all(f32[8,1,6272]{2,1,0:T(1,128)S(1)} %get-tuple-element.71), channel_id=1, replica_groups=mesh['areal'=8,'layer'=4] {'areal'}, dimensions={0} | all-to-all | bytes 401408 | tf_op jit(solution)/shard_map/all_to_all | solution.py:796
  74.0 1.4 %operate.6 = (f32[3,4,8,256]{3,2,1,0:T(8,128)S(1)}, f32[3,4,8,256]{3,2,1,0:T(8,128)S(1)}, f32[3,4,8,256]{3,2,1,0:T(8,128)S(1)}, f32[56,256]{1,0:T(8,128)S(1)}, f...) custom-call(f32[8,1,6272]{2,1,0:T(1,128)S(1)} %all_to_all.27.refs_0_, f32[3,4,8,256]{3,2,1,0:T(8,128)S(1)} %get-tuple-element.72.refs_1_, ...), custom_call_target="tpu_custom_call" | custom-call | flops 4194304 | bytes 1048576 | tf_op jit(solution)/shard_map/operate/pallas_call | solution.py:820
  75.4 5.9 %all-gather.3 = f32[224,256]{1,0:T(8,128)S(1)} all-gather(f32[56,256]{1,0:T(8,128)S(1)} %get-tuple-element.78), channel_id=5, replica_groups=mesh['areal'=8,'layer'=4] {'layer'}, dimensions={0}, use_global_device_ids=true | all-gather | bytes 286720 | tf_op jit(solution)/shard_map/all_gather | solution.py:782
  81.3 1.3 %couple.7 = (f32[3,4,8,256]{3,2,1,0:T(8,128)S(1)}, f32[2,3,8,256]{3,2,1,0:T(8,128)S(1)}, f32[8,1,6272]{2,1,0:T(1,128)S(1)}) custom-call(f32[128,256]{1,0:T(8,128)S(1)} %collective-permute-done.refs_0_, f32[56,256]{1,0:T(8,128)S(1)} %collective-permute-done.1.refs_1_, f32[56,256]{1,0:T(8,128)S(1)} %collective-permute-done.2.refs_2_, ...), custom_call_target="tpu_custom_call" | custom-call | flops 4194304 | bytes 1048576 | tf_op jit(solution)/shard_map/couple/pallas_call | solution.py:783
  82.6 11.5 %all_to_all.28.refs_0_ = f32[8,1,6272]{2,1,0:T(1,128)S(1)} all-to-all(f32[8,1,6272]{2,1,0:T(1,128)S(1)} %get-tuple-element.80), channel_id=1, replica_groups=mesh['areal'=8,'layer'=4] {'areal'}, dimensions={0} | all-to-all | bytes 401408 | tf_op jit(solution)/shard_map/all_to_all | solution.py:796
  94.1 1.4 %operate.7 = (f32[3,4,8,256]{3,2,1,0:T(8,128)S(1)}, f32[32,1,128]{2,1,0:T(1,128)S(1)}, f32[8,128]{1,0:T(8,128)S(1)}) custom-call(f32[8,1,6272]{2,1,0:T(1,128)S(1)} %all_to_all.28.refs_0_, f32[3,4,8,256]{3,2,1,0:T(8,128)S(1)} %get-tuple-element.81.refs_1_, f32[2,3,8,256]{3,2,1,0:T(8,128)S(1)} %get-tuple-element.82.refs_2_, ...), custom_call_target="tpu_custom_call" | custom-call | flops 4194304 | bytes 1048576 | tf_op jit(solution)/shard_map/operate/pallas_call | solution.py:820
  95.5 10.0 %all_to_all.29.dots_ref = f32[32,1,128]{2,1,0:T(1,128)S(1)} all-to-all(f32[32,1,128]{2,1,0:T(1,128)S(1)} %get-tuple-element.87), channel_id=1, replica_groups=mesh['areal'=8,'layer'=4] {'areal','layer'}, dimensions={0} | all-to-all | bytes 32768 | tf_op jit(solution)/shard_map/all_to_all | solution.py:838
  105.4 0.9 finish.1
  (1 shorter events, 0.0 us)
Async XLA Ops:
  0.6 32.5 %copy-start.1 = (f32[3,4,8,256]{3,2,1,0:T(8,128)S(1)}, f32[3,4,8,256]{3,2,1,0:T(8,128)}, u32[]{:S(2)}) copy-start(f32[3,4,8,256]{3,2,1,0:T(8,128)} %refs_8_.7) | copy-start | bytes 294916
  0.6 32.4 %copy-start.5 = (bf16[3,3,4,8,256]{4,3,2,1,0:T(8,128)(2,1)S(1)}, bf16[3,3,4,8,256]{4,3,2,1,0:T(8,128)(2,1)}, u32[]{:S(2)}) copy-start(bf16[3,3,4,8,256]{4,3,2,1,0:T(8,128)(2,1)} %refs_10_.3) | copy-start | bytes 442372
  0.7 32.4 %copy-start.4 = (bf16[3,3,4,8,256]{4,3,2,1,0:T(8,128)(2,1)S(1)}, bf16[3,3,4,8,256]{4,3,2,1,0:T(8,128)(2,1)}, u32[]{:S(2)}) copy-start(bf16[3,3,4,8,256]{4,3,2,1,0:T(8,128)(2,1)} %refs_9_.5) | copy-start | bytes 442372
  0.7 32.4 %copy-start.3 = (bf16[3,3,4,8,256]{4,3,2,1,0:T(8,128)(2,1)S(1)}, bf16[3,3,4,8,256]{4,3,2,1,0:T(8,128)(2,1)}, u32[]{:S(2)}) copy-start(bf16[3,3,4,8,256]{4,3,2,1,0:T(8,128)(2,1)} %refs_8_.6) | copy-start | bytes 442372
  0.7 32.4 %copy-start = (bf16[6,3,3,4,8,256]{5,4,3,2,1,0:T(8,128)(2,1)S(1)}, bf16[6,3,3,4,8,256]{5,4,3,2,1,0:T(8,128)(2,1)}, u32[]{:S(2)}) copy-start(bf16[6,3,3,4,8,256]{5,4,3,2,1,0:T(8,128)(2,1)} %refs_4_.7) | copy-start | bytes 2654212
  0.7 32.4 %copy-start.2 = (bf16[3,3,4,8,256]{4,3,2,1,0:T(8,128)(2,1)S(1)}, bf16[3,3,4,8,256]{4,3,2,1,0:T(8,128)(2,1)}, u32[]{:S(2)}) copy-start(bf16[3,3,4,8,256]{4,3,2,1,0:T(8,128)(2,1)} %refs_3_.7) | copy-start | bytes 442372
  4.0 13.3 %collective-permute-start.2 = (f32[56,256]{1,0:T(8,128)S(1)}, f32[56,256]{1,0:T(8,128)S(1)}, u32[]{:S(2)}, u32[]{:S(2)}) collective-permute-start(f32[56,256]{1,0:T(8,128)S(1)} %get-tuple-element.48.refs_3_), channel_id=1, source_target_pairs={{0,3},{1,0},{2,1},{3,2},{4,7},{5,4},{6,5},{7,6},{8,11},{9,8},{10,9... | collective-permute-start | bytes 172040 | tf_op jit(solution)/shard_map/ppermute | solution.py:686
  6.4 10.9 %collective-permute-start.1 = (f32[56,256]{1,0:T(8,128)S(1)}, f32[56,256]{1,0:T(8,128)S(1)}, u32[]{:S(2)}, u32[]{:S(2)}) collective-permute-start(f32[56,256]{1,0:T(8,128)S(1)} %get-tuple-element.48.refs_3_), channel_id=1, source_target_pairs={{0,2},{1,3},{2,0},{3,1},{4,6},{5,7},{6,4},{7,5},{8,10},{9,11},{10,... | collective-permute-start | bytes 172040 | tf_op jit(solution)/shard_map/ppermute | solution.py:686
  7.1 10.2 %collective-permute-start = (f32[128,256]{1,0:T(8,128)S(1)}, f32[128,256]{1,0:T(8,128)S(1)}, u32[]{:S(2)}, u32[]{:S(2)}) collective-permute-start(f32[128,256]{1,0:T(8,128)S(1)} %get-tuple-element.47), channel_id=1, source_target_pairs={{0,1},{1,2},{2,3},{3,0},{4,5},{5,6},{6,7},{7,4},{8,9},{9,10},{10,1... | collective-permute-start | bytes 393224 | tf_op jit(solution)/shard_map/ppermute | solution.py:686

commit v6 on v5

--- a/solution.py
+++ b/solution.py
@@ -270,12 +270,12 @@
     first, sections, *refs,
 ):
     turned, refs = refs[: sections - 1], refs[sections - 1 :]
-    if first:
-        own_ref, refs = refs[0], refs[1:]
-        edge_ref = refs[-1]
-        refs = refs[:-1]
-    else:
-        edge_ref, refs = refs[0], refs[1:]
+    own_ref, refs = refs[0], refs[1:]
+    moved = turned
+    if not first:
+        moved, refs = refs[: sections - 1], refs[sections - 1 :]
+    edge_ref = refs[-1]
+    refs = refs[:-1]
     (
         matrix_ref, alone_ref, above_ref, below_ref, active_ref,
         slot_block_ref, slot_source_ref, slot_target_ref, start_ref,
@@ -289,10 +289,9 @@
     capacity = per_peer * LANES
     s = lax.axis_index("layer")
     a = lax.axis_index("areal")
-    if first:
-        edge_ref[s] = own_ref[0 : 6 * rows]
-        for turn in range(1, sections):
-            edge_ref[lax.rem(s - turn + sections, sections)] = turned[turn - 1][0 : 6 * rows]
+    edge_ref[s] = own_ref[0 : 7 * rows]
+    for turn in range(1, sections):
+        edge_ref[lax.rem(s - turn + sections, sections)] = moved[turn - 1][0 : 7 * rows]
 
     def matrix(section, which):
         return [
@@ -775,11 +774,10 @@
             pltpu.VMEM((3, layers * rows, width), F32),
             pltpu.VMEM((3, packed_rows, LANES), F32),
         ]
-        if step == 0:
-            edges = edge
-            scratch.append(pltpu.VMEM((sections, 6 * rows, width), F32))
-        else:
-            edges = lax.all_gather(edge, "layer", axis=0, tiled=False)
+        edges = [edge]
+        scratch.append(pltpu.VMEM((sections, 7 * rows, width), F32))
+        if step > 0:
+            edges += [turn(edge, by) for by in range(1, sections)]
         solved, layer_sides, sent = call(
             functools.partial(couple_kernel, step == 0, sections),
             [
@@ -790,7 +788,7 @@
             scratch,
             name="couple",
         )(
-            *turned, edges, all_matrices, alone, from_above, from_below, active,
+            *turned, *edges, all_matrices, alone, from_above, from_below, active,
             slot_block, slot_source, slot_target, starts,
         )
         got = lax.all_to_all(sent, "areal", split_axis=0, concat_axis=0, tiled=True)

time: 107 us -> 102 us (0.953)
  blocking collectives: 86.4 us -> 65.7 us
  waiting for transfers between devices: 0.01 us -> 11.3 us
  starting transfers between devices: 3.23 us -> 7.56 us
    all_gather x3 -> x0, blocking collectives: 17.3 us -> none  [local(): edges = lax.all_gather(edge, 'layer', axis=0, tiled=False)]
    ppermute x3 -> x12, waiting for transfers between devices: 0.01 us -> 11.3 us  [turn(): lax.ppermute(array, 'layer', [(i, (i + by) % count) for i in range(count)])]
    ppermute x3 -> x12, starting transfers between devices: 3.23 us -> 7.56 us  [turn(): lax.ppermute(array, 'layer', [(i, (i + by) % count) for i in range(count)])]
    all_to_all x4, blocking collectives: 49.1 us -> 46.3 us  [local(): got = lax.all_to_all(sent, 'areal', split_axis=0, concat_axis=0, tiled=True)]
  transfers between devices with their start and end apart: 3 -> 12, of which waited for: 0 -> 9; matrix products, arithmetic and copies ran while one was open for 0% -> 0% of each run, Pallas kernels for 0% -> 0%
where the time goes in v6:
time: 102 us; the launch traced here: 101 us
  blocking collectives  65.7 us (64%)
  Pallas kernels  15.9 us (16%)
  waiting for transfers between devices  11.3 us (11%)
  starting transfers between devices  7.56 us (7%)
    all_to_all x4, blocking collectives, local(): got = lax.all_to_all(sent, 'areal', split_axis=0, concat_axis=0, tiled=True)  46.3 us
    ppermute x12, waiting for transfers between devices, turn(): lax.ppermute(array, 'layer', [(i, (i + by) % count) for i in range(count)])  11.3 us
    all_gather x1, blocking collectives, local(): all_matrices = lax.all_gather(matrices, 'layer', axis=0, tiled=False)  10.1 us
    all_to_all x1, blocking collectives, local(): lax.all_to_all(dots, ('areal', 'layer'), split_axis=0, concat_axis=0, til...  9.31 us
    ppermute x12, starting transfers between devices, turn(): lax.ppermute(array, 'layer', [(i, (i + by) % count) for i in range(count)])  7.56 us
    pallas_call x4, Pallas kernels, local(): call(functools.partial(operate_kernel, step), outs, ([pltpu.VMEM((slots,...  6.4 us
    pallas_call x4, Pallas kernels, local(): call(functools.partial(couple_kernel, step == 0, sections), [field, shape...  5.34 us
    pallas_call x1, Pallas kernels, local(): call(functools.partial(setup_kernel, peers), [edge_shape, shape_of(16 * r...  3.29 us
  transfers between devices with their start and end apart: 12, of which 9 were waited for; matrix products, arithmetic and copies ran while one was open for 0% of the time, Pallas kernels for 0%

profile of v6, /device:TPU:0, one launch (start us, length us, event | category | flops | bytes accessed | tf_op | source)
XLA Modules:
  0.0 101.3 jit_solution(16666029917049358060)
XLA Ops:
  0.6 0.0 copy-start.1
  0.6 0.0 copy-start.5
  0.7 0.0 copy-start.4
  0.7 0.0 copy-start.3
  0.7 0.0 copy-start
  0.7 0.0 copy-start.2
  0.7 3.3 %setup.1 = (f32[56,256]{1,0:T(8,128)S(1)}, f32[128,256]{1,0:T(8,128)S(1)}, f32[3,4,8,256]{3,2,1,0:T(8,128)S(1)}, f32[3,3,4,8,256]{4,3,2,1,0:T(8,128)S(1)}, f32[3...) custom-call(f32[3,4,8,256]{3,2,1,0:T(8,128)} %refs_8_.7, ...), custom_call_target="tpu_custom_call" | custom-call | flops 4194304 | bytes 1048576 | tf_op jit(solution)/shard_map/setup/pallas_call | solution.py:735
  4.0 2.4 %collective-permute-start.2 = (f32[56,256]{1,0:T(8,128)S(1)}, f32[56,256]{1,0:T(8,128)S(1)}, u32[]{:S(2)}, u32[]{:S(2)}) collective-permute-start(f32[56,256]{1,0:T(8,128)S(1)} %get-tuple-element.48.refs_3_), channel_id=1, source_target_pairs={{0,3},{1,0},{2,1},{3,2},{4,7},{5,4},{6,5},{7,6},{8,11},{9,8},{10,9... | collective-permute-start | bytes 172040 | tf_op jit(solution)/shard_map/ppermute | solution.py:685
  6.4 0.6 collective-permute-start.1
  7.1 0.2 collective-permute-start
  7.2 10.1 %all-gather = f32[864,256]{1,0:T(8,128)S(1)} all-gather(f32[216,256]{1,0:T(8,128)S(1)} %get-tuple-element.49), channel_id=2, replica_groups=mesh['areal'=8,'layer'=4] {'layer'}, dimensions={0}, use_global_device_ids=true | all-gather | bytes 1105920 | tf_op jit(solution)/shard_map/all_gather | solution.py:763
  17.3 0.0 collective-permute-done.2.refs_2_
  17.3 0.0 collective-permute-done.1.refs_1_
  17.3 0.0 collective-permute-done.refs_0_
  17.3 1.3 %couple.4 = (f32[3,4,8,256]{3,2,1,0:T(8,128)S(1)}, f32[2,3,8,256]{3,2,1,0:T(8,128)S(1)}, f32[8,1,7168]{2,1,0:T(1,128)S(1)}) custom-call(f32[128,256]{1,0:T(8,128)S(1)} %collective-permute-done.refs_0_, f32[56,256]{1,0:T(8,128)S(1)} %collective-permute-done.1.refs_1_, f32[56,256]{1,0:T(8,128)S(1)} %collective-permute-done.2.refs_2_, ...), custom_call_target="tpu_custom_call" | custom-call | flops 4194304 | bytes 1048576 | tf_op jit(solution)/shard_map/couple/pallas_call | solution.py:781
  18.7 14.4 %all_to_all.25.refs_0_ = f32[8,1,7168]{2,1,0:T(1,128)S(1)} all-to-all(f32[8,1,7168]{2,1,0:T(1,128)S(1)} %get-tuple-element.58), channel_id=1, replica_groups=mesh['areal'=8,'layer'=4] {'areal'}, dimensions={0} | all-to-all | bytes 458752 | tf_op jit(solution)/shard_map/all_to_all | solution.py:794
  33.1 0.0 copy-done.1
  33.1 0.0 copy-done.5
  33.1 2.3 %operate.4 = (f32[3,4,8,256]{3,2,1,0:T(8,128)S(1)}, f32[56,256]{1,0:T(8,128)S(1)}, f32[3,4,8,256]{3,2,1,0:T(8,128)S(1)}, bf16[8,32,1024]{2,1,0:T(8,128)(2,1)S(1)}, bf16[8,1024,256]{2,1,0:T(8,128)(2,1)S(1)}) custom-call(f32[8,1,7168]{2,1,0:T(1,128)S(1)} %all_to_all.25.refs_0_, f32[3,4,8,256]{3,2,1,0:T(8,128)S(1)} %get-tuple-element.59.refs_1_.refs_13_.refs_10_.z0_ref, ...), custom_call_target="tpu_custom_call" | custom-call | flops 4194304 | bytes 1048576 | tf_op jit(solution)/shard_map/operate/pallas_call | solution.py:818
  35.4 0.0 collective-permute-start.5
  35.4 1.4 %collective-permute-start.4 = (f32[56,256]{1,0:T(8,128)S(1)}, f32[56,256]{1,0:T(8,128)S(1)}, u32[]{:S(2)}, u32[]{:S(2)}) collective-permute-start(f32[56,256]{1,0:T(8,128)S(1)} %get-tuple-element.61.refs_3_), channel_id=1, source_target_pairs={{0,2},{1,3},{2,0},{3,1},{4,6},{5,7},{6,4},{7,5},{8,10},{9,11},{10,... | collective-permute-start | bytes 172040 | tf_op jit(solution)/shard_map/ppermute | solution.py:685
  36.8 0.2 collective-permute-start.3
  36.9 0.3 collective-permute-done.5.refs_6_
  37.2 3.1 %collective-permute-done.4.refs_5_ = f32[56,256]{1,0:T(8,128)S(1)} collective-permute-done((f32[56,256]{1,0:T(8,128)S(1)}, f32[56,256]{1,0:T(8,128)S(1)}, u32[]{:S(2)}, u32[]{:S(2)}) %collective-permute-start.4) | collective-permute-done | bytes 57376 | tf_op jit(solution)/shard_map/ppermute | solution.py:685
  40.4 0.3 collective-permute-done.3.refs_4_
  40.7 1.3 %couple.5 = (f32[3,4,8,256]{3,2,1,0:T(8,128)S(1)}, f32[2,3,8,256]{3,2,1,0:T(8,128)S(1)}, f32[8,1,6272]{2,1,0:T(1,128)S(1)}) custom-call(f32[128,256]{1,0:T(8,128)S(1)} %collective-permute-done.refs_0_, f32[56,256]{1,0:T(8,128)S(1)} %collective-permute-done.1.refs_1_, f32[56,256]{1,0:T(8,128)S(1)} %collective-permute-done.2.refs_2_, ...), custom_call_target="tpu_custom_call" | custom-call | flops 4194304 | bytes 1048576 | tf_op jit(solution)/shard_map/couple/pallas_call | solution.py:781
  42.0 11.0 %all_to_all.26.refs_0_ = f32[8,1,6272]{2,1,0:T(1,128)S(1)} all-to-all(f32[8,1,6272]{2,1,0:T(1,128)S(1)} %get-tuple-element.63), channel_id=1, replica_groups=mesh['areal'=8,'layer'=4] {'areal'}, dimensions={0} | all-to-all | bytes 401408 | tf_op jit(solution)/shard_map/all_to_all | solution.py:794
  53.0 1.4 %operate.5 = (f32[3,4,8,256]{3,2,1,0:T(8,128)S(1)}, f32[3,4,8,256]{3,2,1,0:T(8,128)S(1)}, f32[3,4,8,256]{3,2,1,0:T(8,128)S(1)}, f32[56,256]{1,0:T(8,128)S(1)}, f...) custom-call(f32[8,1,6272]{2,1,0:T(1,128)S(1)} %all_to_all.26.refs_0_, f32[3,4,8,256]{3,2,1,0:T(8,128)S(1)} %get-tuple-element.64.refs_1_, ...), custom_call_target="tpu_custom_call" | custom-call | flops 4194304 | bytes 1048576 | tf_op jit(solution)/shard_map/operate/pallas_call | solution.py:818
  54.4 0.0 collective-permute-start.8
  54.4 1.2 %collective-permute-start.7 = (f32[56,256]{1,0:T(8,128)S(1)}, f32[56,256]{1,0:T(8,128)S(1)}, u32[]{:S(2)}, u32[]{:S(2)}) collective-permute-start(f32[56,256]{1,0:T(8,128)S(1)} %get-tuple-element.69.refs_3_), channel_id=1, source_target_pairs={{0,2},{1,3},{2,0},{3,1},{4,6},{5,7},{6,4},{7,5},{8,10},{9,11},{10,... | collective-permute-start | bytes 172040 | tf_op jit(solution)/shard_map/ppermute | solution.py:685
  55.6 0.2 collective-permute-start.6
  55.8 0.4 collective-permute-done.8.refs_6_
  56.2 3.0 %collective-permute-done.7.refs_5_ = f32[56,256]{1,0:T(8,128)S(1)} collective-permute-done((f32[56,256]{1,0:T(8,128)S(1)}, f32[56,256]{1,0:T(8,128)S(1)}, u32[]{:S(2)}, u32[]{:S(2)}) %collective-permute-start.7) | collective-permute-done | bytes 57376 | tf_op jit(solution)/shard_map/ppermute | solution.py:685
  59.3 0.3 collective-permute-done.6.refs_4_
  59.6 1.3 %couple.6 = (f32[3,4,8,256]{3,2,1,0:T(8,128)S(1)}, f32[2,3,8,256]{3,2,1,0:T(8,128)S(1)}, f32[8,1,6272]{2,1,0:T(1,128)S(1)}) custom-call(f32[128,256]{1,0:T(8,128)S(1)} %collective-permute-done.refs_0_, f32[56,256]{1,0:T(8,128)S(1)} %collective-permute-done.1.refs_1_, f32[56,256]{1,0:T(8,128)S(1)} %collective-permute-done.2.refs_2_, ...), custom_call_target="tpu_custom_call" | custom-call | flops 4194304 | bytes 1048576 | tf_op jit(solution)/shard_map/couple/pallas_call | solution.py:781
  60.9 10.3 %all_to_all.27.refs_0_ = f32[8,1,6272]{2,1,0:T(1,128)S(1)} all-to-all(f32[8,1,6272]{2,1,0:T(1,128)S(1)} %get-tuple-element.71), channel_id=1, replica_groups=mesh['areal'=8,'layer'=4] {'areal'}, dimensions={0} | all-to-all | bytes 401408 | tf_op jit(solution)/shard_map/all_to_all | solution.py:794
  71.2 1.4 %operate.6 = (f32[3,4,8,256]{3,2,1,0:T(8,128)S(1)}, f32[3,4,8,256]{3,2,1,0:T(8,128)S(1)}, f32[3,4,8,256]{3,2,1,0:T(8,128)S(1)}, f32[56,256]{1,0:T(8,128)S(1)}, f...) custom-call(f32[8,1,6272]{2,1,0:T(1,128)S(1)} %all_to_all.27.refs_0_, f32[3,4,8,256]{3,2,1,0:T(8,128)S(1)} %get-tuple-element.72.refs_1_, ...), custom_call_target="tpu_custom_call" | custom-call | flops 4194304 | bytes 1048576 | tf_op jit(solution)/shard_map/operate/pallas_call | solution.py:818
  72.6 0.2 collective-permute-start.11
  72.8 1.0 %collective-permute-start.10 = (f32[56,256]{1,0:T(8,128)S(1)}, f32[56,256]{1,0:T(8,128)S(1)}, u32[]{:S(2)}, u32[]{:S(2)}) collective-permute-start(f32[56,256]{1,0:T(8,128)S(1)} %get-tuple-element.78.refs_3_), channel_id=1, source_target_pairs={{0,2},{1,3},{2,0},{3,1},{4,6},{5,7},{6,4},{7,5},{8,10},{9,11},{10,... | collective-permute-start | bytes 172040 | tf_op jit(solution)/shard_map/ppermute | solution.py:685
  73.9 0.2 collective-permute-start.9
  74.0 0.7 collective-permute-done.11.refs_6_
  74.7 2.8 %collective-permute-done.10.refs_5_ = f32[56,256]{1,0:T(8,128)S(1)} collective-permute-done((f32[56,256]{1,0:T(8,128)S(1)}, f32[56,256]{1,0:T(8,128)S(1)}, u32[]{:S(2)}, u32[]{:S(2)}) %collective-permute-start.10) | collective-permute-done | bytes 57376 | tf_op jit(solution)/shard_map/ppermute | solution.py:685
  77.5 0.3 collective-permute-done.9.refs_4_
  77.8 1.3 %couple.7 = (f32[3,4,8,256]{3,2,1,0:T(8,128)S(1)}, f32[2,3,8,256]{3,2,1,0:T(8,128)S(1)}, f32[8,1,6272]{2,1,0:T(1,128)S(1)}) custom-call(f32[128,256]{1,0:T(8,128)S(1)} %collective-permute-done.refs_0_, f32[56,256]{1,0:T(8,128)S(1)} %collective-permute-done.1.refs_1_, f32[56,256]{1,0:T(8,128)S(1)} %collective-permute-done.2.refs_2_, ...), custom_call_target="tpu_custom_call" | custom-call | flops 4194304 | bytes 1048576 | tf_op jit(solution)/shard_map/couple/pallas_call | solution.py:781
  79.1 10.5 %all_to_all.28.refs_0_ = f32[8,1,6272]{2,1,0:T(1,128)S(1)} all-to-all(f32[8,1,6272]{2,1,0:T(1,128)S(1)} %get-tuple-element.80), channel_id=1, replica_groups=mesh['areal'=8,'layer'=4] {'areal'}, dimensions={0} | all-to-all | bytes 401408 | tf_op jit(solution)/shard_map/all_to_all | solution.py:794
  89.7 1.4 %operate.7 = (f32[3,4,8,256]{3,2,1,0:T(8,128)S(1)}, f32[32,1,128]{2,1,0:T(1,128)S(1)}, f32[8,128]{1,0:T(8,128)S(1)}) custom-call(f32[8,1,6272]{2,1,0:T(1,128)S(1)} %all_to_all.28.refs_0_, f32[3,4,8,256]{3,2,1,0:T(8,128)S(1)} %get-tuple-element.81.refs_1_, f32[2,3,8,256]{3,2,1,0:T(8,128)S(1)} %get-tuple-element.82.refs_2_, ...), custom_call_target="tpu_custom_call" | custom-call | flops 4194304 | bytes 1048576 | tf_op jit(solution)/shard_map/operate/pallas_call | solution.py:818
  91.1 9.3 %all_to_all.29.dots_ref = f32[32,1,128]{2,1,0:T(1,128)S(1)} all-to-all(f32[32,1,128]{2,1,0:T(1,128)S(1)} %get-tuple-element.87), channel_id=1, replica_groups=mesh['areal'=8,'layer'=4] {'areal','layer'}, dimensions={0} | all-to-all | bytes 32768 | tf_op jit(solution)/shard_map/all_to_all | solution.py:836
  100.4 0.9 finish.1
  (5 shorter events, 0.0 us)
Async XLA Ops:
  0.6 32.5 %copy-start.1 = (f32[3,4,8,256]{3,2,1,0:T(8,128)S(1)}, f32[3,4,8,256]{3,2,1,0:T(8,128)}, u32[]{:S(2)}) copy-start(f32[3,4,8,256]{3,2,1,0:T(8,128)} %refs_8_.7) | copy-start | bytes 294916
  0.6 32.4 %copy-start.5 = (bf16[3,3,4,8,256]{4,3,2,1,0:T(8,128)(2,1)S(1)}, bf16[3,3,4,8,256]{4,3,2,1,0:T(8,128)(2,1)}, u32[]{:S(2)}) copy-start(bf16[3,3,4,8,256]{4,3,2,1,0:T(8,128)(2,1)} %refs_10_.3) | copy-start | bytes 442372
  0.7 32.4 %copy-start.4 = (bf16[3,3,4,8,256]{4,3,2,1,0:T(8,128)(2,1)S(1)}, bf16[3,3,4,8,256]{4,3,2,1,0:T(8,128)(2,1)}, u32[]{:S(2)}) copy-start(bf16[3,3,4,8,256]{4,3,2,1,0:T(8,128)(2,1)} %refs_9_.5) | copy-start | bytes 442372
  0.7 32.4 %copy-start.3 = (bf16[3,3,4,8,256]{4,3,2,1,0:T(8,128)(2,1)S(1)}, bf16[3,3,4,8,256]{4,3,2,1,0:T(8,128)(2,1)}, u32[]{:S(2)}) copy-start(bf16[3,3,4,8,256]{4,3,2,1,0:T(8,128)(2,1)} %refs_8_.6) | copy-start | bytes 442372
  0.7 32.4 %copy-start = (bf16[6,3,3,4,8,256]{5,4,3,2,1,0:T(8,128)(2,1)S(1)}, bf16[6,3,3,4,8,256]{5,4,3,2,1,0:T(8,128)(2,1)}, u32[]{:S(2)}) copy-start(bf16[6,3,3,4,8,256]{5,4,3,2,1,0:T(8,128)(2,1)} %refs_4_.7) | copy-start | bytes 2654212
  0.7 32.4 %copy-start.2 = (bf16[3,3,4,8,256]{4,3,2,1,0:T(8,128)(2,1)S(1)}, bf16[3,3,4,8,256]{4,3,2,1,0:T(8,128)(2,1)}, u32[]{:S(2)}) copy-start(bf16[3,3,4,8,256]{4,3,2,1,0:T(8,128)(2,1)} %refs_3_.7) | copy-start | bytes 442372
  4.0 13.3 %collective-permute-start.2 = (f32[56,256]{1,0:T(8,128)S(1)}, f32[56,256]{1,0:T(8,128)S(1)}, u32[]{:S(2)}, u32[]{:S(2)}) collective-permute-start(f32[56,256]{1,0:T(8,128)S(1)} %get-tuple-element.48.refs_3_), channel_id=1, source_target_pairs={{0,3},{1,0},{2,1},{3,2},{4,7},{5,4},{6,5},{7,6},{8,11},{9,8},{10,9... | collective-permute-start | bytes 172040 | tf_op jit(solution)/shard_map/ppermute | solution.py:685
  6.4 10.9 %collective-permute-start.1 = (f32[56,256]{1,0:T(8,128)S(1)}, f32[56,256]{1,0:T(8,128)S(1)}, u32[]{:S(2)}, u32[]{:S(2)}) collective-permute-start(f32[56,256]{1,0:T(8,128)S(1)} %get-tuple-element.48.refs_3_), channel_id=1, source_target_pairs={{0,2},{1,3},{2,0},{3,1},{4,6},{5,7},{6,4},{7,5},{8,10},{9,11},{10,... | collective-permute-start | bytes 172040 | tf_op jit(solution)/shard_map/ppermute | solution.py:685
  7.1 10.2 %collective-permute-start = (f32[128,256]{1,0:T(8,128)S(1)}, f32[128,256]{1,0:T(8,128)S(1)}, u32[]{:S(2)}, u32[]{:S(2)}) collective-permute-start(f32[128,256]{1,0:T(8,128)S(1)} %get-tuple-element.47), channel_id=1, source_target_pairs={{0,1},{1,2},{2,3},{3,0},{4,5},{5,6},{6,7},{7,4},{8,9},{9,10},{10,1... | collective-permute-start | bytes 393224 | tf_op jit(solution)/shard_map/ppermute | solution.py:685
  35.4 1.8 %collective-permute-start.5 = (f32[56,256]{1,0:T(8,128)S(1)}, f32[56,256]{1,0:T(8,128)S(1)}, u32[]{:S(2)}, u32[]{:S(2)}) collective-permute-start(f32[56,256]{1,0:T(8,128)S(1)} %get-tuple-element.61.refs_3_), channel_id=1, source_target_pairs={{0,3},{1,0},{2,1},{3,2},{4,7},{5,4},{6,5},{7,6},{8,11},{9,8},{10,9... | collective-permute-start | bytes 172040 | tf_op jit(solution)/shard_map/ppermute | solution.py:685
  35.4 5.0 %collective-permute-start.4 = (f32[56,256]{1,0:T(8,128)S(1)}, f32[56,256]{1,0:T(8,128)S(1)}, u32[]{:S(2)}, u32[]{:S(2)}) collective-permute-start(f32[56,256]{1,0:T(8,128)S(1)} %get-tuple-element.61.refs_3_), channel_id=1, source_target_pairs={{0,2},{1,3},{2,0},{3,1},{4,6},{5,7},{6,4},{7,5},{8,10},{9,11},{10,... | collective-permute-start | bytes 172040 | tf_op jit(solution)/shard_map/ppermute | solution.py:685
  36.8 3.9 %collective-permute-start.3 = (f32[56,256]{1,0:T(8,128)S(1)}, f32[56,256]{1,0:T(8,128)S(1)}, u32[]{:S(2)}, u32[]{:S(2)}) collective-permute-start(f32[56,256]{1,0:T(8,128)S(1)} %get-tuple-element.61.refs_3_), channel_id=1, source_target_pairs={{0,1},{1,2},{2,3},{3,0},{4,5},{5,6},{6,7},{7,4},{8,9},{9,10},{10,1... | collective-permute-start | bytes 172040 | tf_op jit(solution)/shard_map/ppermute | solution.py:685
  54.4 1.9 %collective-permute-start.8 = (f32[56,256]{1,0:T(8,128)S(1)}, f32[56,256]{1,0:T(8,128)S(1)}, u32[]{:S(2)}, u32[]{:S(2)}) collective-permute-start(f32[56,256]{1,0:T(8,128)S(1)} %get-tuple-element.69.refs_3_), channel_id=1, source_target_pairs={{0,3},{1,0},{2,1},{3,2},{4,7},{5,4},{6,5},{7,6},{8,11},{9,8},{10,9... | collective-permute-start | bytes 172040 | tf_op jit(solution)/shard_map/ppermute | solution.py:685
  54.4 4.9 %collective-permute-start.7 = (f32[56,256]{1,0:T(8,128)S(1)}, f32[56,256]{1,0:T(8,128)S(1)}, u32[]{:S(2)}, u32[]{:S(2)}) collective-permute-start(f32[56,256]{1,0:T(8,128)S(1)} %get-tuple-element.69.refs_3_), channel_id=1, source_target_pairs={{0,2},{1,3},{2,0},{3,1},{4,6},{5,7},{6,4},{7,5},{8,10},{9,11},{10,... | collective-permute-start | bytes 172040 | tf_op jit(solution)/shard_map/ppermute | solution.py:685
  55.6 3.9 %collective-permute-start.6 = (f32[56,256]{1,0:T(8,128)S(1)}, f32[56,256]{1,0:T(8,128)S(1)}, u32[]{:S(2)}, u32[]{:S(2)}) collective-permute-start(f32[56,256]{1,0:T(8,128)S(1)} %get-tuple-element.69.refs_3_), channel_id=1, source_target_pairs={{0,1},{1,2},{2,3},{3,0},{4,5},{5,6},{6,7},{7,4},{8,9},{9,10},{10,1... | collective-permute-start | bytes 172040 | tf_op jit(solution)/shard_map/ppermute | solution.py:685
  72.6 2.1 %collective-permute-start.11 = (f32[56,256]{1,0:T(8,128)S(1)}, f32[56,256]{1,0:T(8,128)S(1)}, u32[]{:S(2)}, u32[]{:S(2)}) collective-permute-start(f32[56,256]{1,0:T(8,128)S(1)} %get-tuple-element.78.refs_3_), channel_id=1, source_target_pairs={{0,3},{1,0},{2,1},{3,2},{4,7},{5,4},{6,5},{7,6},{8,11},{9,8},{10,9... | collective-permute-start | bytes 172040 | tf_op jit(solution)/shard_map/ppermute | solution.py:685
  72.8 4.7 %collective-permute-start.10 = (f32[56,256]{1,0:T(8,128)S(1)}, f32[56,256]{1,0:T(8,128)S(1)}, u32[]{:S(2)}, u32[]{:S(2)}) collective-permute-start(f32[56,256]{1,0:T(8,128)S(1)} %get-tuple-element.78.refs_3_), channel_id=1, source_target_pairs={{0,2},{1,3},{2,0},{3,1},{4,6},{5,7},{6,4},{7,5},{8,10},{9,11},{10,... | collective-permute-start | bytes 172040 | tf_op jit(solution)/shard_map/ppermute | solution.py:685
  73.9 3.9 %collective-permute-start.9 = (f32[56,256]{1,0:T(8,128)S(1)}, f32[56,256]{1,0:T(8,128)S(1)}, u32[]{:S(2)}, u32[]{:S(2)}) collective-permute-start(f32[56,256]{1,0:T(8,128)S(1)} %get-tuple-element.78.refs_3_), channel_id=1, source_target_pairs={{0,1},{1,2},{2,3},{3,0},{4,5},{5,6},{6,7},{7,4},{8,9},{9,10},{10,1... | collective-permute-start | bytes 172040 | tf_op jit(solution)/shard_map/ppermute | solution.py:685
